TPU v7x, 32 devices: a whole 2x2x4 slice. The times are simulated.
32 devices in a mesh: rows: 8 (over z, y), var: 4 (over x, core).
Axes of the slice: x: 2, y: 2, z: 4, core: 2. Of those that a mesh axis runs over, the one named last changes fastest.
Arguments:
- signal_matrix: bfloat16 [128, 768, 32], P('rows'), may hold values from -6 to 6
- frame_numbers: int32 [128, 768], P('rows'), may hold values from 0 to 5, as said below
- variate_order: int32 [32], replicated, may hold values from 0 to 31, each once
- embed_weight: bfloat16 [8, 12, 64], P('var'), may hold values from -1.75 to 1.75
- head_weight: bfloat16 [8, 64, 4], P('var'), may hold values from -0.75 to 0.75
- down_a: bfloat16 [6144, 512], replicated, may hold values from -0.078125 to 0.078125
- iso_a: bfloat16 [8192, 512], replicated, may hold values from -0.0625 to 0.0625
- up_a: bfloat16 [512, 6144], replicated, may hold values from -0.25 to 0.25
- down_b: bfloat16 [8192, 512], replicated, may hold values from -0.0625 to 0.0625
- iso_b: bfloat16 [6144, 512], replicated, may hold values from -0.078125 to 0.078125
- up_b: bfloat16 [512, 8192], replicated, may hold values from -0.25 to 0.25
- merge_weight: bfloat16 [1024, 512], replicated, may hold values from -0.1875 to 0.1875
- ff_in: bfloat16 [512, 2048], replicated, may hold values from -0.25 to 0.25
- ff_out: bfloat16 [2048, 512], replicated, may hold values from -0.125 to 0.125
- norm_gains: float32 [3, 512], replicated, may hold values from 0.25 to 1.75
- estimate_cotangent: bfloat16 [128, 768, 32], P('rows', None, 'var'), may hold values from -6 to 6
Outputs:
- prediction: float32 [128, 768, 32], P('rows', None, 'var')
- series_grad: float32 [128, 768, 32], P('rows', None, 'var')
- embed_grad: float32 [8, 12, 64], P('var')
- head_grad: float32 [8, 64, 4], P('var')
- down_a_grad: float32 [6144, 512], P('rows', 'var')
- iso_a_grad: float32 [8192, 512], P('rows', 'var')
- up_a_grad: float32 [512, 6144], P('rows', 'var')
- down_b_grad: float32 [8192, 512], P('rows', 'var')
- iso_b_grad: float32 [6144, 512], P('rows', 'var')
- up_b_grad: float32 [512, 8192], P('rows', 'var')
- merge_grad: float32 [1024, 512], P('rows', 'var')
- ff_in_grad: float32 [512, 2048], P('rows', 'var')
- ff_out_grad: float32 [2048, 512], P('rows', 'var')
- gains_grad: float32 [3, 512], replicated
Inputs may be any that keep to these rules, and one draw needn't show every extreme that they name: `frame_numbers`: each row of 768 positions is cut into windows of 96, 144 or 192 positions starting at multiples of 48; the number starts at 0 in each row and rises by one at each window's start; each row's first window has 192 positions. Some row holds six windows. `variate_order`: each variate appears once.
All inputs are finite; a program needn't handle non-finite values.
Results may differ from a plain program's by a relative error of at most 0.019.
Values may be sent and summed in bfloat16 or wider, within the bound.
No kernel may reach another device: no remote copies, remote signals or barrier semaphores. Data moves between devices by JAX's collectives and lax.ppermute only.
A program may use at most 576 MiB of HBM per device.

v0:
```python
import jax
import jax.numpy as jnp
from jax import lax
from jax.sharding import PartitionSpec as P

SA = 12
SB = 16


def product(left, right):
    return jnp.dot(left, right, preferred_element_type=jnp.float32)


def shift_rows(values, offset):
    length = values.shape[1]
    if offset == 0:
        return values
    filler = jnp.zeros_like(values[:, : abs(offset)])
    if offset > 0:
        return jnp.concatenate([filler, values[:, : length - offset]], axis=1)
    return jnp.concatenate([values[:, -offset:], filler], axis=1)


def shift_marks(window_marks, offset):
    length = window_marks.shape[1]
    if offset == 0:
        return window_marks
    filler = jnp.full_like(window_marks[:, : abs(offset)], -1)
    if offset > 0:
        return jnp.concatenate([filler, window_marks[:, : length - offset]], axis=1)
    return jnp.concatenate([window_marks[:, -offset:], filler], axis=1)


def same_window(window_marks, offset):
    return (shift_marks(window_marks, offset) == window_marks).astype(jnp.float32)


def window_mean(values, window_marks, half_span):
    running = jnp.zeros_like(values)
    counted = jnp.zeros(window_marks.shape, jnp.float32)
    for offset in range(-half_span, half_span + 1):
        inside = same_window(window_marks, offset)
        running = running + shift_rows(values, offset) * inside[..., None]
        counted = counted + inside
    return running / counted[..., None]


def trend_of(values, window_marks):
    return 0.5 * (window_mean(values, window_marks, 6) + window_mean(values, window_marks, 8))


def layer_norm(values, norm_gain):
    centre = values - jnp.mean(values, axis=-1, keepdims=True)
    spread = jnp.mean(centre * centre, axis=-1, keepdims=True)
    return centre * lax.rsqrt(spread + 1e-05) * norm_gain


def gelu_exact(values):
    return jax.nn.gelu(values, approximate=False)


def embed_columns(grouped, window_marks):
    pieces = []
    for offset in (1, 0, -1):
        inside = same_window(window_marks, offset)[:, :, None, None].astype(grouped.dtype)
        pieces.append(shift_rows(grouped, offset) * inside)
    return jnp.concatenate(pieces, axis=-1)


def iso_columns(values, coarse_marks, tap_count):
    pieces = []
    for tap_index in range(tap_count):
        offset = tap_count - 1 - tap_index
        inside = same_window(coarse_marks, offset)[..., None].astype(values.dtype)
        pieces.append(shift_rows(values, offset) * inside)
    return jnp.concatenate(pieces, axis=-1)


def scale_forward(
    seasonal, seasonal_low, window_marks, down_weight, iso_weight, up_weight, norm_gain, stride
):
    row_count, length, feature_count = seasonal.shape
    slot_count = length // stride
    blocks = seasonal_low.reshape(row_count, slot_count, stride * feature_count)
    activated = jnp.tanh(product(blocks, down_weight))
    coarse_marks = window_marks[:, ::stride]
    tap_count = iso_weight.shape[0] // feature_count
    columns = iso_columns(activated.astype(jnp.bfloat16), coarse_marks, tap_count)
    second = jnp.tanh(product(columns, iso_weight))
    joined_in = second + activated
    joined_low = layer_norm(joined_in, norm_gain).astype(jnp.bfloat16)
    lifted = jnp.tanh(product(joined_low, up_weight)).reshape(row_count, length, feature_count)
    lifted_in = lifted + seasonal
    branch_low = layer_norm(lifted_in, norm_gain).astype(jnp.bfloat16)
    return (
        branch_low,
        (
            blocks,
            activated,
            coarse_marks,
            columns,
            second,
            joined_in,
            joined_low,
            lifted,
            lifted_in,
        ),
    )


def scale_backward(branch_grad, saved, down_weight, iso_weight, up_weight, norm_gain, stride):
    blocks, activated, coarse_marks, columns, second, joined_in, joined_low, lifted, lifted_in = (
        saved
    )
    row_count, length, feature_count = lifted.shape
    slot_count = length // stride
    tap_count = iso_weight.shape[0] // feature_count
    lifted_grad, gain_late = jax.vjp(layer_norm, lifted_in, norm_gain)[1](branch_grad)
    up_pre = (
        (lifted_grad * (1.0 - lifted * lifted))
        .reshape(row_count, slot_count, stride * feature_count)
        .astype(jnp.bfloat16)
    )
    up_grad = jnp.einsum("rnd,rnk->dk", joined_low, up_pre, preferred_element_type=jnp.float32)
    joined_grad = jnp.einsum("rnk,dk->rnd", up_pre, up_weight, preferred_element_type=jnp.float32)
    sum_grad, gain_early = jax.vjp(layer_norm, joined_in, norm_gain)[1](joined_grad)
    iso_pre = (sum_grad * (1.0 - second * second)).astype(jnp.bfloat16)
    iso_grad = jnp.einsum("rnk,rnd->kd", columns, iso_pre, preferred_element_type=jnp.float32)
    column_grad = jnp.einsum("rnd,kd->rnk", iso_pre, iso_weight, preferred_element_type=jnp.float32)
    spread_back = jax.vjp(lambda values: iso_columns(values, coarse_marks, tap_count), activated)[
        1
    ](column_grad)[0]
    act_grad = spread_back + sum_grad
    down_pre = (act_grad * (1.0 - activated * activated)).astype(jnp.bfloat16)
    down_grad = jnp.einsum("rnk,rnd->kd", blocks, down_pre, preferred_element_type=jnp.float32)
    block_grad = jnp.einsum(
        "rnd,kd->rnk", down_pre, down_weight, preferred_element_type=jnp.float32
    )
    seasonal_grad = block_grad.reshape(row_count, length, feature_count) + lifted_grad
    return (seasonal_grad, down_grad, iso_grad, up_grad, gain_early + gain_late)


def mixer_forward(hidden_low, window_marks, mixer_weights, norm_gains):
    down_a, iso_a, up_a, down_b, iso_b, up_b, merge_weight, ff_in, ff_out = mixer_weights
    hidden = hidden_low.astype(jnp.float32)
    trend_part = trend_of(hidden, window_marks)
    seasonal = hidden - trend_part
    seasonal_low = seasonal.astype(jnp.bfloat16)
    branch_a, saved_a = scale_forward(
        seasonal, seasonal_low, window_marks, down_a, iso_a, up_a, norm_gains[0], SA
    )
    branch_b, saved_b = scale_forward(
        seasonal, seasonal_low, window_marks, down_b, iso_b, up_b, norm_gains[0], SB
    )
    stacked = jnp.concatenate([branch_a, branch_b], axis=-1)
    merged = product(stacked, merge_weight)
    mixed = layer_norm(merged, norm_gains[1])
    mixed_low = mixed.astype(jnp.bfloat16)
    inner_pre = product(mixed_low, ff_in)
    inner_low = gelu_exact(inner_pre).astype(jnp.bfloat16)
    outer_act = product(inner_low, ff_out)
    final_in = mixed + outer_act
    result = layer_norm(final_in, norm_gains[2]) + trend_part
    return (
        result,
        (hidden, saved_a, saved_b, stacked, merged, mixed_low, inner_pre, inner_low, final_in),
    )


def mixer_backward(result_grad, saved, window_marks, mixer_weights, norm_gains):
    down_a, iso_a, up_a, down_b, iso_b, up_b, merge_weight, ff_in, ff_out = mixer_weights
    hidden, saved_a, saved_b, stacked, merged, mixed_low, inner_pre, inner_low, final_in = saved
    feature_count = hidden.shape[-1]
    final_grad, gain_last = jax.vjp(layer_norm, final_in, norm_gains[2])[1](result_grad)
    outer_low = final_grad.astype(jnp.bfloat16)
    ff_out_grad = jnp.einsum(
        "rtf,rtd->fd", inner_low, outer_low, preferred_element_type=jnp.float32
    )
    inner_grad = jnp.einsum("rtd,fd->rtf", outer_low, ff_out, preferred_element_type=jnp.float32)
    inner_pre_grad = jax.vjp(gelu_exact, inner_pre)[1](inner_grad)[0].astype(jnp.bfloat16)
    ff_in_grad = jnp.einsum(
        "rtd,rtf->df", mixed_low, inner_pre_grad, preferred_element_type=jnp.float32
    )
    mixed_grad = (
        jnp.einsum("rtf,df->rtd", inner_pre_grad, ff_in, preferred_element_type=jnp.float32)
        + final_grad
    )
    merged_grad, gain_mid = jax.vjp(layer_norm, merged, norm_gains[1])[1](mixed_grad)
    merged_low = merged_grad.astype(jnp.bfloat16)
    merge_grad = jnp.einsum("rtk,rtd->kd", stacked, merged_low, preferred_element_type=jnp.float32)
    stacked_grad = jnp.einsum(
        "rtd,kd->rtk", merged_low, merge_weight, preferred_element_type=jnp.float32
    )
    seasonal_a, down_a_grad, iso_a_grad, up_a_grad, gain_a = scale_backward(
        stacked_grad[..., :feature_count], saved_a, down_a, iso_a, up_a, norm_gains[0], SA
    )
    seasonal_b, down_b_grad, iso_b_grad, up_b_grad, gain_b = scale_backward(
        stacked_grad[..., feature_count:], saved_b, down_b, iso_b, up_b, norm_gains[0], SB
    )
    seasonal_grad = seasonal_a + seasonal_b
    trend_back = jax.vjp(lambda values: trend_of(values, window_marks), hidden)[1](
        result_grad - seasonal_grad
    )[0]
    hidden_grad = seasonal_grad + trend_back
    gains_grad = jnp.stack([gain_a + gain_b, gain_mid, gain_last])
    weight_grads = (
        down_a_grad,
        iso_a_grad,
        up_a_grad,
        down_b_grad,
        iso_b_grad,
        up_b_grad,
        merge_grad,
        ff_in_grad,
        ff_out_grad,
    )
    return (hidden_grad, weight_grads, gains_grad)


def body(
    signal_matrix,
    frame_numbers,
    variate_order,
    embed_weight,
    head_weight,
    down_a,
    iso_a,
    up_a,
    down_b,
    iso_b,
    up_b,
    merge_weight,
    ff_in,
    ff_out,
    norm_gains,
    estimate_cotangent,
):
    var_size = lax.axis_size("var")
    var_index = lax.axis_index("var")
    local_rows, length, variates = signal_matrix.shape
    group_count, tap_width, group_width = embed_weight.shape
    per_group = head_weight.shape[2]
    time_rows = local_rows // var_size
    chosen = lax.dynamic_slice_in_dim(
        variate_order, var_index * (group_count * per_group), group_count * per_group
    )
    grouped = jnp.take(signal_matrix, chosen, axis=2).reshape(
        local_rows, length, group_count, per_group
    )
    embed_cols = embed_columns(grouped, frame_numbers)
    embedded = jnp.einsum(
        "rtgk,gkd->rtgd", embed_cols, embed_weight, preferred_element_type=jnp.float32
    )
    embedded_low = embedded.reshape(local_rows, length, group_count * group_width).astype(
        jnp.bfloat16
    )
    hidden_low = lax.all_to_all(embedded_low, "var", split_axis=0, concat_axis=2, tiled=True)
    time_marks = lax.dynamic_slice_in_dim(frame_numbers, var_index * time_rows, time_rows, 0)
    mixer_weights = (down_a, iso_a, up_a, down_b, iso_b, up_b, merge_weight, ff_in, ff_out)
    result, saved = mixer_forward(hidden_low, time_marks, mixer_weights, norm_gains)
    result_low = result.astype(jnp.bfloat16)
    back_groups = lax.all_to_all(
        result_low, "var", split_axis=2, concat_axis=0, tiled=True
    ).reshape(local_rows, length, group_count, group_width)
    grad_groups = estimate_cotangent.reshape(local_rows, length, group_count, per_group)
    predicted = jnp.einsum(
        "rtgd,gdk->rtgk", back_groups, head_weight, preferred_element_type=jnp.float32
    ).reshape(local_rows, length, group_count * per_group)
    head_grad = jnp.einsum(
        "rtgd,rtgk->gdk", back_groups, grad_groups, preferred_element_type=jnp.float32
    )
    result_grad_low = (
        jnp.einsum("rtgk,gdk->rtgd", grad_groups, head_weight, preferred_element_type=jnp.float32)
        .reshape(local_rows, length, group_count * group_width)
        .astype(jnp.bfloat16)
    )
    result_grad = lax.all_to_all(
        result_grad_low, "var", split_axis=0, concat_axis=2, tiled=True
    ).astype(jnp.float32)
    hidden_again, result_grad = lax.optimization_barrier((hidden_low, result_grad))
    saved = mixer_forward(hidden_again, time_marks, mixer_weights, norm_gains)[1]
    hidden_grad, weight_grads, gains_grad = mixer_backward(
        result_grad, saved, time_marks, mixer_weights, norm_gains
    )
    (
        down_a_grad,
        iso_a_grad,
        up_a_grad,
        down_b_grad,
        iso_b_grad,
        up_b_grad,
        merge_grad,
        ff_in_grad,
        ff_out_grad,
    ) = weight_grads
    hidden_grad_low = lax.all_to_all(
        hidden_grad.astype(jnp.bfloat16), "var", split_axis=2, concat_axis=0, tiled=True
    ).reshape(local_rows, length, group_count, group_width)
    embed_grad = jnp.einsum(
        "rtgk,rtgd->gkd", embed_cols, hidden_grad_low, preferred_element_type=jnp.float32
    )
    column_grad = jnp.einsum(
        "rtgd,gkd->rtgk", hidden_grad_low, embed_weight, preferred_element_type=jnp.float32
    )
    series_grad = jax.vjp(
        lambda values: embed_columns(values, frame_numbers), grouped.astype(jnp.float32)
    )[1](column_grad)[0]
    series_grad = series_grad.reshape(local_rows, length, group_count * per_group)
    embed_sum, head_sum = lax.psum((embed_grad, head_grad), "rows")
    gains_sum = lax.psum(gains_grad, ("rows", "var"))
    first_section = (
        lax.psum_scatter(
            down_a_grad.astype(jnp.bfloat16), "rows", scatter_dimension=0, tiled=True
        ).astype(jnp.float32),
        lax.psum_scatter(
            iso_a_grad.astype(jnp.bfloat16), "rows", scatter_dimension=0, tiled=True
        ).astype(jnp.float32),
        lax.psum_scatter(
            up_a_grad.astype(jnp.bfloat16), "rows", scatter_dimension=0, tiled=True
        ).astype(jnp.float32),
        lax.psum_scatter(
            down_b_grad.astype(jnp.bfloat16), "rows", scatter_dimension=0, tiled=True
        ).astype(jnp.float32),
        lax.psum_scatter(
            iso_b_grad.astype(jnp.bfloat16), "rows", scatter_dimension=0, tiled=True
        ).astype(jnp.float32),
        lax.psum_scatter(
            up_b_grad.astype(jnp.bfloat16), "rows", scatter_dimension=0, tiled=True
        ).astype(jnp.float32),
        lax.psum_scatter(
            merge_grad.astype(jnp.bfloat16), "rows", scatter_dimension=0, tiled=True
        ).astype(jnp.float32),
        lax.psum_scatter(
            ff_in_grad.astype(jnp.bfloat16), "rows", scatter_dimension=0, tiled=True
        ).astype(jnp.float32),
        lax.psum_scatter(
            ff_out_grad.astype(jnp.bfloat16), "rows", scatter_dimension=0, tiled=True
        ).astype(jnp.float32),
    )
    (
        section_a,
        section_b,
        section_c,
        section_d,
        section_e,
        section_f,
        section_g,
        section_h,
        section_i,
    ) = first_section
    summed = (
        lax.psum_scatter(
            section_a.astype(jnp.bfloat16), "var", scatter_dimension=1, tiled=True
        ).astype(jnp.float32),
        lax.psum_scatter(
            section_b.astype(jnp.bfloat16), "var", scatter_dimension=1, tiled=True
        ).astype(jnp.float32),
        lax.psum_scatter(
            section_c.astype(jnp.bfloat16), "var", scatter_dimension=1, tiled=True
        ).astype(jnp.float32),
        lax.psum_scatter(
            section_d.astype(jnp.bfloat16), "var", scatter_dimension=1, tiled=True
        ).astype(jnp.float32),
        lax.psum_scatter(
            section_e.astype(jnp.bfloat16), "var", scatter_dimension=1, tiled=True
        ).astype(jnp.float32),
        lax.psum_scatter(
            section_f.astype(jnp.bfloat16), "var", scatter_dimension=1, tiled=True
        ).astype(jnp.float32),
        lax.psum_scatter(
            section_g.astype(jnp.bfloat16), "var", scatter_dimension=1, tiled=True
        ).astype(jnp.float32),
        lax.psum_scatter(
            section_h.astype(jnp.bfloat16), "var", scatter_dimension=1, tiled=True
        ).astype(jnp.float32),
        lax.psum_scatter(
            section_i.astype(jnp.bfloat16), "var", scatter_dimension=1, tiled=True
        ).astype(jnp.float32),
    )
    return (
        predicted,
        series_grad,
        embed_sum,
        head_sum,
        summed[0],
        summed[1],
        summed[2],
        summed[3],
        summed[4],
        summed[5],
        summed[6],
        summed[7],
        summed[8],
        gains_sum,
    )


def solution(mesh):
    placed = (
        P("rows", None, None),
        P("rows", None),
        P(),
        P("var", None, None),
        P("var", None, None),
        P(),
        P(),
        P(),
        P(),
        P(),
        P(),
        P(),
        P(),
        P(),
        P(),
        P("rows", None, "var"),
    )
    return jax.shard_map(
        body,
        mesh=mesh,
        in_specs=placed,
        out_specs=(
            P("rows", None, "var"),
            P("rows", None, "var"),
            P("var", None, None),
            P("var", None, None),
            P("rows", "var"),
            P("rows", "var"),
            P("rows", "var"),
            P("rows", "var"),
            P("rows", "var"),
            P("rows", "var"),
            P("rows", "var"),
            P("rows", "var"),
            P("rows", "var"),
            P(),
        ),
        check_vma=False,
    )
```

profile of v0, /device:TPU:0, one launch (start us, length us, event | category | flops | bytes accessed | tf_op | source)
XLA Modules:
  0.0 1914.1 jit_solution(10102850091631067651)
XLA Ops:
  23.2 34.6 %all-to-all-done = bf16[16,768,128]{1,2,0:T(8,128)(2,1)} async-done(((bf16[16,768,128]{1,2,0:T(8,128)(2,1)}), bf16[16,768,128]{1,2,0:T(8,128)(2,1)}, u32[]{:S(2)}, u32[]{:S(2)}) %all-to-all-start) | async-done | bytes 3145760 | tf_op jit(solution)/shard_map/all_to_all | solution.py:257
  77.7 21.7 %all-to-all-done.2 = bf16[16,768,128]{1,2,0:T(8,128)(2,1)} async-done(((bf16[16,768,128]{1,2,0:T(8,128)(2,1)}), bf16[16,768,128]{1,2,0:T(8,128)(2,1)}, u32[]{:S(2)}, u32[]{:S(2)}) %all-to-all-start.2) | async-done | bytes 3145760 | tf_op jit(solution)/shard_map/all_to_all | solution.py:277
  223.5 36.1 %fusion.268 = (bf16[4,768,512]{2,1,0:T(8,128)(2,1)}, f32[4,768,512]{2,1,0:T(8,128)}) fusion(f32[4,768]{1,0:T(4,128)S(1)} %get-tuple-element.188, f32[4,768]{1,0:T(4,128)S(1)} %get-tuple-element.192, f32[4,760,512]{2,1,0:T(8,128)} %get-tuple-element.272, f32[4,768]{1,0:T(4,128)S(1)} %get-tuple-element.191, f32[4,761,512]{2,1,0:T(8,128)} %get-tuple-element.274, ...), kind=kLoop, calls=%fused_computation.556 | loop fusion | flops 80216064 | bytes 112877568 | tf_op jit(solution)/shard_map/convert_element_type | solution.py:148
  273.2 36.2 %fusion.78 = (bf16[4,768,512]{2,1,0:T(8,128)(2,1)}, f32[4,768,512]{2,1,0:T(8,128)}) fusion(bf16[4,768,512]{2,1,0:T(8,128)(2,1)} %all_to_all.45, f32[4,768]{1,0:T(4,128)S(1)} %get-tuple-element.188, f32[4,768]{1,0:T(4,128)S(1)} %get-tuple-element.192, f32[4,760,512]{2,1,0:T(8,128)} %get-tuple-element.288, f32[4,768]{1,0:T(4,128)S(1)} %get-tuple-element.191, ...), kind=kLoop, calls=%fused_computation.188 | loop fusion | flops 80216064 | bytes 112877568 | tf_op jit(solution)/shard_map/convert_element_type | solution.py:148
  502.3 22.1 %fusion.56 = (u8[768,2048]{1,0:T(8,128)(4,1)}, u8[768,2048]{1,0:T(8,128)(4,1)}, f32[4,768,2048]{2,1,0:T(8,128)}) fusion(bf16[512,2048]{1,0:T(8,128)(2,1)S(1)} %copy-done, f32[4,768,512]{2,1,0:T(8,128)} %copy.135, f32[4,768]{1,0:T(4,128)S(1)} %fusion.189, f32[4,768]{1,0:T(4,128)S(1)} %broadcast_multiply_fusion.1, f32[512]{0:T(512)S(1)} %bitcast.417), kind=kOutput, calls=%fused_computation.154 | convolution fusion | flops 6527385600 | bytes 36726784 | tf_op jit(solution)/shard_map/dot_general | solution.py:11
  524.4 59.9 %multiply_convert_fusion = (bf16[4,768,2048]{2,1,0:T(8,128)(2,1)}, f32[4,768,2048]{2,1,0:T(8,128)}) fusion(f32[4,768,2048]{2,1,0:T(8,128)} %get-tuple-element.446, u8[768,2048]{1,0:T(8,128)(4,1)} %get-tuple-element.75, u8[768,2048]{1,0:T(8,128)(4,1)} %get-tuple-element.74), kind=kLoop, calls=%fused_computation.17 | loop fusion | flops 440401920 | bytes 66060288 | tf_op jit(solution)/shard_map/convert_element_type | solution.py:160
  603.5 27.3 %add_convert_fusion = bf16[4,768,2048]{2,1,0:T(8,128)(2,1)} fusion(f32[4,768,2048]{2,1,0:T(8,128)} %get-tuple-element.105, f32[4,768,2048]{2,1,0:T(8,128)} %get-tuple-element.446, bf16[2048,512]{1,0:T(8,128)(2,1)} %param.29, f32[4,768,512]{2,1,0:T(8,128)} %get-tuple-element.103, f32[4,768]{1,0:T(4,128)S(1)} %negate_multiply_fusion.5), kind=kOutput, calls=%fused_computation.16 | convolution fusion | flops 6533677056 | bytes 71315456 | tf_op jit(solution)/shard_map/rtd,fd->rtf/dot_general | solution.py:179
  664.4 14.8 bitcast_convert_fusion.6
  708.5 17.4 fusion.259
  884.8 22.2 %fusion.55 = (u8[768,2048]{1,0:T(8,128)(4,1)}, u8[768,2048]{1,0:T(8,128)(4,1)}, f32[4,768,2048]{2,1,0:T(8,128)}) fusion(bf16[512,2048]{1,0:T(8,128)(2,1)S(1)} %copy-done, f32[4,768,512]{2,1,0:T(8,128)} %copy.122, f32[512]{0:T(512)S(1)} %bitcast.422, f32[4,768]{1,0:T(4,128)S(1)} %add_rsqrt_fusion.1, f32[4,768]{1,0:T(4,128)S(1)} %broadcast_multiply_fusion.5), kind=kOutput, calls=%fused_computation.153 | convolution fusion | flops 6527385600 | bytes 36726784 | tf_op jit(solution)/shard_map/dot_general | solution.py:11
  907.2 63.5 %fusion.376 = (f32[4,768]{1,0:T(4,128)S(1)}, f32[4,768,512]{2,1,0:T(8,128)}) fusion(bf16[2048,512]{1,0:T(8,128)(2,1)} %param.29, f32[4,768,2048]{2,1,0:T(8,128)} %get-tuple-element.456, u8[768,2048]{1,0:T(8,128)(4,1)} %get-tuple-element.77, u8[768,2048]{1,0:T(8,128)(4,1)} %get-tuple-element.76, f32[512]{0:T(512)S(1)} %bitcast.423, ...), kind=kOutput, calls=%fused_computation.618 | convolution fusion | flops 6890714112 | bytes 43030528 | tf_op jit(solution)/shard_map/dot_general | solution.py:11
  972.5 16.2 broadcast_divide_fusion
  1022.3 17.9 slice_multiply_fusion.6
  1040.2 66.2 %reduce-scatter.31.cloned.1.call-done = bf16[768,512]{1,0:T(8,128)(2,1)} async-done(((bf16[6144,512]{1,0:T(8,128)(2,1)}), bf16[768,512]{1,0:T(8,128)(2,1)}) %reduce-scatter.31.cloned.1.call-update) | async-done | bytes 786448 | tf_op jit(solution)/shard_map/reduce_scatter | solution.py:312
  1108.8 17.9 slice_multiply_fusion.7
  1126.8 17.9 slice_multiply_fusion.8
  1144.7 82.5 %reduce-scatter.35.cloned.1.call-done = bf16[64,6144]{1,0:T(8,128)(2,1)} async-done(((bf16[512,6144]{1,0:T(8,128)(2,1)}), bf16[64,6144]{1,0:T(8,128)(2,1)}) %reduce-scatter.35.cloned.1.call-update) | async-done | bytes 786448 | tf_op jit(solution)/shard_map/reduce_scatter | solution.py:318
  1227.3 17.9 slice_multiply_fusion.9
  1245.2 17.9 slice_multiply_fusion.10
  1263.2 114.4 %reduce-scatter.33.cloned.1.call-done = bf16[1024,512]{1,0:T(8,128)(2,1)} async-done(((bf16[8192,512]{1,0:T(8,128)(2,1)}), bf16[1024,512]{1,0:T(8,128)(2,1)}) %reduce-scatter.33.cloned.1.call-update) | async-done | bytes 1048592 | tf_op jit(solution)/shard_map/reduce_scatter | solution.py:315
  1395.8 17.9 slice_multiply_fusion.11
  1413.7 114.2 %reduce-scatter.39.cloned.1.call-done = bf16[1024,512]{1,0:T(8,128)(2,1)} async-done(((bf16[8192,512]{1,0:T(8,128)(2,1)}), bf16[1024,512]{1,0:T(8,128)(2,1)}) %reduce-scatter.39.cloned.1.call-update) | async-done | bytes 1048592 | tf_op jit(solution)/shard_map/reduce_scatter | solution.py:321
  1530.1 63.0 %add_convert_fusion.1 = bf16[4,768,512]{2,1,0:T(8,128)(2,1)} fusion(f32[4,768,512]{2,1,0:T(8,128)} %get-tuple-element.95, f32[4,762,512]{2,1,0:T(8,128)} %get-tuple-element.235, f32[4,763,512]{2,1,0:T(8,128)} %get-tuple-element.237, f32[4,764,512]{2,1,0:T(8,128)} %get-tuple-element.239, f32[4,765,512]{2,1,0:T(8,128)} %get-tuple-element.241, ...), kind=kLoop, calls=%fused_computation.125 | loop fusion | flops 48758784 | bytes 197246976 | tf_op jit(solution)/shard_map/convert_element_type | solution.py:297
  1604.2 73.0 %psum.23 = f32[3,512]{1,0:T(4,128)} all-reduce(f32[3,512]{1,0:T(4,128)S(1)} %pad_maximum_fusion.8), channel_id=1, replica_groups=mesh['rows'=8,'var'=4] {'rows','var'}, use_global_device_ids=true, to_apply=%region_62.63 | all-reduce | flops 1536 | bytes 12288 | tf_op jit(solution)/shard_map/psum | solution.py:310
  1684.3 16.7 reduce-scatter.63.cloned.1.call-done
  1707.8 37.8 %all-reduce.186 = (f32[2,12,64]{2,1,0:T(8,128)S(1)}, f32[2,64,4]{1,2,0:T(4,128)}) all-reduce(f32[2,12,64]{2,1,0:T(8,128)S(1)} %fusion.123, f32[2,64,4]{1,2,0:T(4,128)S(1)} %convolution_bitcast_fusion), channel_id=1, replica_groups=mesh['rows'=8,'var'=4] {'rows'}, use_global_device_ids=true, to_apply=%region_36.37 | all-reduce | flops 2048 | bytes 16384 | tf_op jit(solution)/shard_map/psum | solution.py:309
  1755.5 16.7 reduce-scatter.61.cloned.1.call-done
  1774.1 23.8 %reduce-scatter.55.cloned.1.call-done = bf16[128,768]{1,0:T(8,128)(2,1)} async-done(((bf16[512,768]{1,0:T(8,128)(2,1)}), bf16[128,768]{1,0:T(8,128)(2,1)}) %reduce-scatter.55.cloned.1.call-update) | async-done | bytes 196624
  1799.7 23.8 %reduce-scatter.37.cloned.1.call-done = bf16[64,1536]{1,0:T(8,128)(2,1)} async-done(((bf16[64,6144]{1,0:T(8,128)(2,1)}), bf16[64,1536]{1,0:T(8,128)(2,1)}) %reduce-scatter.37.cloned.1.call-update) | async-done | bytes 196624 | tf_op jit(solution)/shard_map/reduce_scatter | solution.py:358
  1825.2 25.5 %reduce-scatter.57.cloned.1.call-done = bf16[128,1024]{1,0:T(8,128)(2,1)} async-done(((bf16[512,1024]{1,0:T(8,128)(2,1)}), bf16[128,1024]{1,0:T(8,128)(2,1)}) %reduce-scatter.57.cloned.1.call-update) | async-done | bytes 262160
  1852.6 25.2 %reduce-scatter.59.cloned.1.call-done = bf16[128,1024]{1,0:T(8,128)(2,1)} async-done(((bf16[512,1024]{1,0:T(8,128)(2,1)}), bf16[128,1024]{1,0:T(8,128)(2,1)}) %reduce-scatter.59.cloned.1.call-update) | async-done | bytes 262160
  1879.8 25.2 %reduce-scatter.45.cloned.1.call-done = bf16[64,2048]{1,0:T(8,128)(2,1)} async-done(((bf16[64,8192]{1,0:T(8,128)(2,1)}), bf16[64,2048]{1,0:T(8,128)(2,1)}) %reduce-scatter.45.cloned.1.call-update) | async-done | bytes 262160 | tf_op jit(solution)/shard_map/reduce_scatter | solution.py:367
  (820 shorter events, 708.7 us)
Async XLA Ops:
  7.2 495.1 %copy-start = (bf16[512,2048]{1,0:T(8,128)(2,1)S(1)}, bf16[512,2048]{1,0:T(8,128)(2,1)}, u32[]{:S(2)}) copy-start(bf16[512,2048]{1,0:T(8,128)(2,1)} %param.28) | copy-start | bytes 6291460
  15.4 42.4 %all-to-all-start = ((bf16[16,768,128]{1,2,0:T(8,128)(2,1)}), bf16[16,768,128]{1,2,0:T(8,128)(2,1)}, u32[]{:S(2)}, u32[]{:S(2)}) async-start(bf16[16,768,128]{1,2,0:T(8,128)(2,1)} %bitcast.338), calls=%async_computation | async-start | bytes 6291456 | tf_op jit(solution)/shard_map/all_to_all | solution.py:257
  57.7 41.6 %all-to-all-start.2 = ((bf16[16,768,128]{1,2,0:T(8,128)(2,1)}), bf16[16,768,128]{1,2,0:T(8,128)(2,1)}, u32[]{:S(2)}, u32[]{:S(2)}) async-start(bf16[16,768,128]{1,2,0:T(8,128)(2,1)} %bitcast.335), calls=%async_computation.2 | async-start | bytes 6291456 | tf_op jit(solution)/shard_map/all_to_all | solution.py:277
  62.4 908.3 %reduce-scatter.47.cloned.1.call-start = ((), (), s32[]{:S(2)}) async-start(), calls=%async_computation.30 | async-start | bytes 1179648 | tf_op jit(solution)/shard_map/reduce_scatter | solution.py:330
  63.0 210.0 %copy-start.59 = (f32[4,768]{1,0:T(4,128)}, f32[4,768]{1,0:T(4,128)S(1)}, u32[]{:S(2)}) copy-start(f32[4,768]{1,0:T(4,128)S(1)} %get-tuple-element.175) | copy-start | bytes 36868
  63.1 210.0 %copy-start.61 = (f32[4,768]{1,0:T(4,128)}, f32[4,768]{1,0:T(4,128)S(1)}, u32[]{:S(2)}) copy-start(f32[4,768]{1,0:T(4,128)S(1)} %get-tuple-element.176) | copy-start | bytes 36868
  63.1 210.0 %copy-start.63 = (f32[4,768]{1,0:T(4,128)}, f32[4,768]{1,0:T(4,128)S(1)}, u32[]{:S(2)}) copy-start(f32[4,768]{1,0:T(4,128)S(1)} %get-tuple-element.177) | copy-start | bytes 36868
  63.1 210.0 %copy-start.65 = (f32[4,768]{1,0:T(4,128)}, f32[4,768]{1,0:T(4,128)S(1)}, u32[]{:S(2)}) copy-start(f32[4,768]{1,0:T(4,128)S(1)} %get-tuple-element.178) | copy-start | bytes 36868
  63.1 210.0 %copy-start.67 = (f32[4,768]{1,0:T(4,128)}, f32[4,768]{1,0:T(4,128)S(1)}, u32[]{:S(2)}) copy-start(f32[4,768]{1,0:T(4,128)S(1)} %get-tuple-element.179) | copy-start | bytes 36868
  63.1 210.0 %copy-start.69 = (f32[4,768]{1,0:T(4,128)}, f32[4,768]{1,0:T(4,128)S(1)}, u32[]{:S(2)}) copy-start(f32[4,768]{1,0:T(4,128)S(1)} %get-tuple-element.180) | copy-start | bytes 36868
  63.1 210.0 %copy-start.71 = (f32[4,768]{1,0:T(4,128)}, f32[4,768]{1,0:T(4,128)S(1)}, u32[]{:S(2)}) copy-start(f32[4,768]{1,0:T(4,128)S(1)} %get-tuple-element.186) | copy-start | bytes 36868
  63.1 210.0 %copy-start.73 = (f32[4,768]{1,0:T(4,128)}, f32[4,768]{1,0:T(4,128)S(1)}, u32[]{:S(2)}) copy-start(f32[4,768]{1,0:T(4,128)S(1)} %get-tuple-element.185) | copy-start | bytes 36868
  63.1 210.0 %copy-start.75 = (f32[4,768]{1,0:T(4,128)}, f32[4,768]{1,0:T(4,128)S(1)}, u32[]{:S(2)}) copy-start(f32[4,768]{1,0:T(4,128)S(1)} %get-tuple-element.184) | copy-start | bytes 36868
  657.5 331.2 %reduce-scatter.53.cloned.1.call-start = ((), (), s32[]{:S(2)}) async-start(), calls=%async_computation.33 | async-start | bytes 2359296 | tf_op jit(solution)/shard_map/reduce_scatter | solution.py:336
  679.2 319.1 %reduce-scatter.49.cloned.1.call-start = ((), (), s32[]{:S(2)}) async-start(), calls=%async_computation.31 | async-start | bytes 2359296 | tf_op jit(solution)/shard_map/reduce_scatter | solution.py:333
  708.4 293.6 %reduce-scatter.41.cloned.1.call-start = ((), (), s32[]{:S(2)}) async-start(), calls=%async_computation.27 | async-start | bytes 7077888 | tf_op jit(solution)/shard_map/reduce_scatter | solution.py:324
  753.0 353.5 %reduce-scatter.31.cloned.1.call-start = ((), (), s32[]{:S(2)}) async-start(), calls=%async_computation.22 | async-start | bytes 7077888 | tf_op jit(solution)/shard_map/reduce_scatter | solution.py:312
  791.7 435.5 %reduce-scatter.35.cloned.1.call-start = ((), (), s32[]{:S(2)}) async-start(), calls=%async_computation.24 | async-start | bytes 7077888 | tf_op jit(solution)/shard_map/reduce_scatter | solution.py:318
  798.4 579.2 %reduce-scatter.33.cloned.1.call-start = ((), (), s32[]{:S(2)}) async-start(), calls=%async_computation.23 | async-start | bytes 9437184 | tf_op jit(solution)/shard_map/reduce_scatter | solution.py:315
  807.3 720.5 %reduce-scatter.39.cloned.1.call-start = ((), (), s32[]{:S(2)}) async-start(), calls=%async_computation.26 | async-start | bytes 9437184 | tf_op jit(solution)/shard_map/reduce_scatter | solution.py:321
  822.0 859.4 %reduce-scatter.43.cloned.1.call-start = ((), (), s32[]{:S(2)}) async-start(), calls=%async_computation.28 | async-start | bytes 9437184 | tf_op jit(solution)/shard_map/reduce_scatter | solution.py:327
  907.1 793.9 %reduce-scatter.63.cloned.1.call-start = ((), (), s32[]{:S(2)}) async-start(), calls=%async_computation.38 | async-start | bytes 163840
  972.4 780.0 %reduce-scatter.65.cloned.1.call-start = ((), (), s32[]{:S(2)}) async-start(), calls=%async_computation.39 | async-start | bytes 327680
  990.5 763.5 %reduce-scatter.51.cloned.1.call-start = ((), (), s32[]{:S(2)}) async-start(), calls=%async_computation.32 | async-start | bytes 327680 | tf_op jit(solution)/shard_map/reduce_scatter | solution.py:373
  998.4 773.9 %reduce-scatter.61.cloned.1.call-start = ((), (), s32[]{:S(2)}) async-start(), calls=%async_computation.37 | async-start | bytes 983040
  1017.6 581.7 %all-to-all-start.1 = ((bf16[4,768,512]{1,0,2:T(4,128)(2,1)}), bf16[4,768,512]{1,0,2:T(4,128)(2,1)}, u32[]{:S(2)}, u32[]{:S(2)}) async-start(bf16[4,768,512]{1,0,2:T(4,128)(2,1)} %copy.125), calls=%async_computation.1 | async-start | bytes 6291456 | tf_op jit(solution)/shard_map/all_to_all | solution.py:262
  1022.2 775.7 %reduce-scatter.55.cloned.1.call-start = ((), (), s32[]{:S(2)}) async-start(), calls=%async_computation.34 | async-start | bytes 983040
  1108.8 714.7 %reduce-scatter.37.cloned.1.call-start = ((), (), s32[]{:S(2)}) async-start(), calls=%async_computation.25 | async-start | bytes 983040 | tf_op jit(solution)/shard_map/reduce_scatter | solution.py:358
  1227.2 623.5 %reduce-scatter.57.cloned.1.call-start = ((), (), s32[]{:S(2)}) async-start(), calls=%async_computation.35 | async-start | bytes 1310720
  1379.9 498.0 %reduce-scatter.59.cloned.1.call-start = ((), (), s32[]{:S(2)}) async-start(), calls=%async_computation.36 | async-start | bytes 1310720
  1599.3 103.2 %all-to-all-start.3 = ((bf16[4,768,512]{1,0,2:T(4,128)(2,1)}), bf16[4,768,512]{1,0,2:T(4,128)(2,1)}, u32[]{:S(2)}, u32[]{:S(2)}) async-start(bf16[4,768,512]{1,0,2:T(4,128)(2,1)} %copy.139), calls=%async_computation.3 | async-start | bytes 6291456 | tf_op jit(solution)/shard_map/all_to_all | solution.py:296
  1604.0 301.1 %reduce-scatter.45.cloned.1.call-start = ((), (), s32[]{:S(2)}) async-start(), calls=%async_computation.29 | async-start | bytes 1310720 | tf_op jit(solution)/shard_map/reduce_scatter | solution.py:367
  (211 other events, 4360.3 us)
Sparse Core Ops, SparseCore 0:
  657.6 65.2 reduce-scatter.46
  726.4 67.5 reduce-scatter.52
  797.6 67.5 reduce-scatter.48
  868.6 117.0 reduce-scatter.40
  989.1 117.2 reduce-scatter.30
  1109.8 117.3 reduce-scatter.34
  1230.8 146.7 reduce-scatter.32
  1381.2 146.5 reduce-scatter.38
  1531.5 147.8 reduce-scatter.42
  1682.2 18.7 reduce-scatter.62
  1704.0 20.0 reduce-scatter.64
  1726.4 20.0 reduce-scatter.50
  1749.0 23.1 reduce-scatter.60
  1774.6 23.1 reduce-scatter.54
  1800.2 23.1 reduce-scatter.36
  1825.9 24.7 reduce-scatter.56
  1853.0 24.7 reduce-scatter.58
  1880.3 24.7 reduce-scatter.44
where the time goes:
time: 1920 us; the launch traced here: 1910 us
  waiting for transfers between devices  591 us (31%)
  other arithmetic  487 us (25%)
  matrix products  361 us (19%)
  local copies, waits for them, and re-layouts  326 us (17%)
  blocking collectives  111 us (6%)
  starting transfers between devices  20.2 us (1%)
    dot_general x18, matrix products, product(): return jnp.dot(left, right, preferred_element_type=jnp.float32)  199 us
    mul x8, other arithmetic, window_mean(): running = running + shift_rows(values, offset) * inside[..., None]  122 us
    reduce_scatter x1, waiting for transfers between devices, body(): lax.psum_scatter(iso_a_grad.astype(jnp.bfloat16), 'rows', scatter_dimensi...  114 us
    reduce_scatter x1, waiting for transfers between devices, body(): lax.psum_scatter(down_b_grad.astype(jnp.bfloat16), 'rows', scatter_dimens...  114 us
    unnamed x24, waiting for transfers between devices  108 us
    slice x16, local copies, waits for them, and re-layouts, shift_rows(): return jnp.concatenate([values[:, -offset:], filler], axis=1)  103 us
    reduce_scatter x1, waiting for transfers between devices, body(): lax.psum_scatter(up_a_grad.astype(jnp.bfloat16), 'rows', scatter_dimensio...  82.5 us
    psum x1, blocking collectives, body(): gains_sum = lax.psum(gains_grad, ('rows', 'var'))  73 us
  transfers between devices with their start and end apart: 22, of which 13 were waited for; matrix products, arithmetic and copies ran while one was open for 31% of the time, Pallas kernels for 0%

commit v1 on v0

--- a/solution.py
+++ b/solution.py
@@ -217,6 +217,30 @@
     return (hidden_grad, weight_grads, gains_grad)
 
 
+def block_diagonal(pieces):
+    count, height, width = pieces.shape
+    eye = jnp.eye(count, dtype=pieces.dtype)
+    spread = pieces[:, :, None, :] * eye[:, None, :, None]
+    return spread.reshape(count * height, count * width)
+
+
+def diagonal_blocks(matrix, count):
+    height, width = matrix.shape[0] // count, matrix.shape[1] // count
+    blocks = matrix.reshape(count, height, count, width)
+    return jnp.stack([blocks[at, :, at, :] for at in range(count)])
+
+
+def scatter_sum(grad, row_shards, column_shards):
+    height, width = grad.shape
+    pieces = grad.astype(jnp.bfloat16).reshape(
+        row_shards, height // row_shards, column_shards, width // column_shards
+    )
+    pieces = pieces.transpose(0, 2, 1, 3).reshape(-1, width // column_shards)
+    return lax.psum_scatter(pieces, ("rows", "var"), scatter_dimension=0, tiled=True).astype(
+        jnp.float32
+    )
+
+
 def body(
     signal_matrix,
     frame_numbers,
@@ -235,164 +259,81 @@
     norm_gains,
     estimate_cotangent,
 ):
-    var_size = lax.axis_size("var")
+    row_shards, column_shards = lax.axis_size("rows"), lax.axis_size("var")
     var_index = lax.axis_index("var")
     local_rows, length, variates = signal_matrix.shape
-    group_count, tap_width, group_width = embed_weight.shape
+    local_groups, tap_width, group_width = embed_weight.shape
     per_group = head_weight.shape[2]
-    time_rows = local_rows // var_size
-    chosen = lax.dynamic_slice_in_dim(
-        variate_order, var_index * (group_count * per_group), group_count * per_group
-    )
-    grouped = jnp.take(signal_matrix, chosen, axis=2).reshape(
-        local_rows, length, group_count, per_group
-    )
-    embed_cols = embed_columns(grouped, frame_numbers)
-    embedded = jnp.einsum(
-        "rtgk,gkd->rtgd", embed_cols, embed_weight, preferred_element_type=jnp.float32
-    )
-    embedded_low = embedded.reshape(local_rows, length, group_count * group_width).astype(
+    groups = local_groups * column_shards
+    own_variates = variates // column_shards
+    time_rows = local_rows // column_shards
+    embed_all, head_all = lax.all_gather(
+        (embed_weight, head_weight), "var", axis=0, tiled=True
+    )
+    embed_matrix = jnp.concatenate(
+        [
+            block_diagonal(embed_all[:, tap * per_group : (tap + 1) * per_group])
+            for tap in range(3)
+        ],
+        axis=0,
+    )
+    head_matrix = block_diagonal(head_all)
+    signal = lax.dynamic_slice_in_dim(signal_matrix, var_index * time_rows, time_rows, 0)
+    marks = lax.dynamic_slice_in_dim(frame_numbers, var_index * time_rows, time_rows, 0)
+    pick = jax.nn.one_hot(variate_order, variates, dtype=jnp.bfloat16)
+    grouped = jnp.einsum("rtv,cv->rtc", signal, pick, preferred_element_type=jnp.float32).astype(
         jnp.bfloat16
     )
-    hidden_low = lax.all_to_all(embedded_low, "var", split_axis=0, concat_axis=2, tiled=True)
-    time_marks = lax.dynamic_slice_in_dim(frame_numbers, var_index * time_rows, time_rows, 0)
+    cotangent = lax.all_to_all(
+        estimate_cotangent, "var", split_axis=0, concat_axis=2, tiled=True
+    )
+    embed_cols = embed_columns(grouped[..., None], marks)
+    embed_cols = jnp.concatenate([embed_cols[..., tap] for tap in range(3)], axis=-1)
+    hidden_low = product(embed_cols, embed_matrix).astype(jnp.bfloat16)
     mixer_weights = (down_a, iso_a, up_a, down_b, iso_b, up_b, merge_weight, ff_in, ff_out)
-    result, saved = mixer_forward(hidden_low, time_marks, mixer_weights, norm_gains)
+    result, saved = mixer_forward(hidden_low, marks, mixer_weights, norm_gains)
     result_low = result.astype(jnp.bfloat16)
-    back_groups = lax.all_to_all(
-        result_low, "var", split_axis=2, concat_axis=0, tiled=True
-    ).reshape(local_rows, length, group_count, group_width)
-    grad_groups = estimate_cotangent.reshape(local_rows, length, group_count, per_group)
-    predicted = jnp.einsum(
-        "rtgd,gdk->rtgk", back_groups, head_weight, preferred_element_type=jnp.float32
-    ).reshape(local_rows, length, group_count * per_group)
-    head_grad = jnp.einsum(
-        "rtgd,rtgk->gdk", back_groups, grad_groups, preferred_element_type=jnp.float32
-    )
-    result_grad_low = (
-        jnp.einsum("rtgk,gdk->rtgd", grad_groups, head_weight, preferred_element_type=jnp.float32)
-        .reshape(local_rows, length, group_count * group_width)
+    predicted = product(result_low, head_matrix)
+    head_grad = diagonal_blocks(
+        jnp.einsum("rtd,rtk->dk", result_low, cotangent, preferred_element_type=jnp.float32), groups
+    )
+    result_grad = (
+        jnp.einsum("rtk,dk->rtd", cotangent, head_matrix, preferred_element_type=jnp.float32)
         .astype(jnp.bfloat16)
-    )
-    result_grad = lax.all_to_all(
-        result_grad_low, "var", split_axis=0, concat_axis=2, tiled=True
-    ).astype(jnp.float32)
-    hidden_again, result_grad = lax.optimization_barrier((hidden_low, result_grad))
-    saved = mixer_forward(hidden_again, time_marks, mixer_weights, norm_gains)[1]
+        .astype(jnp.float32)
+    )
     hidden_grad, weight_grads, gains_grad = mixer_backward(
-        result_grad, saved, time_marks, mixer_weights, norm_gains
-    )
-    (
-        down_a_grad,
-        iso_a_grad,
-        up_a_grad,
-        down_b_grad,
-        iso_b_grad,
-        up_b_grad,
-        merge_grad,
-        ff_in_grad,
-        ff_out_grad,
-    ) = weight_grads
-    hidden_grad_low = lax.all_to_all(
-        hidden_grad.astype(jnp.bfloat16), "var", split_axis=2, concat_axis=0, tiled=True
-    ).reshape(local_rows, length, group_count, group_width)
-    embed_grad = jnp.einsum(
-        "rtgk,rtgd->gkd", embed_cols, hidden_grad_low, preferred_element_type=jnp.float32
+        result_grad, saved, marks, mixer_weights, norm_gains
+    )
+    hidden_grad_low = hidden_grad.astype(jnp.bfloat16)
+    embed_full = jnp.einsum(
+        "rtk,rtd->kd", embed_cols, hidden_grad_low, preferred_element_type=jnp.float32
+    )
+    embed_grad = jnp.concatenate(
+        [
+            diagonal_blocks(embed_full[tap * variates : (tap + 1) * variates], groups)
+            for tap in range(3)
+        ],
+        axis=1,
     )
     column_grad = jnp.einsum(
-        "rtgd,gkd->rtgk", hidden_grad_low, embed_weight, preferred_element_type=jnp.float32
-    )
-    series_grad = jax.vjp(
-        lambda values: embed_columns(values, frame_numbers), grouped.astype(jnp.float32)
-    )[1](column_grad)[0]
-    series_grad = series_grad.reshape(local_rows, length, group_count * per_group)
-    embed_sum, head_sum = lax.psum((embed_grad, head_grad), "rows")
-    gains_sum = lax.psum(gains_grad, ("rows", "var"))
-    first_section = (
-        lax.psum_scatter(
-            down_a_grad.astype(jnp.bfloat16), "rows", scatter_dimension=0, tiled=True
-        ).astype(jnp.float32),
-        lax.psum_scatter(
-            iso_a_grad.astype(jnp.bfloat16), "rows", scatter_dimension=0, tiled=True
-        ).astype(jnp.float32),
-        lax.psum_scatter(
-            up_a_grad.astype(jnp.bfloat16), "rows", scatter_dimension=0, tiled=True
-        ).astype(jnp.float32),
-        lax.psum_scatter(
-            down_b_grad.astype(jnp.bfloat16), "rows", scatter_dimension=0, tiled=True
-        ).astype(jnp.float32),
-        lax.psum_scatter(
-            iso_b_grad.astype(jnp.bfloat16), "rows", scatter_dimension=0, tiled=True
-        ).astype(jnp.float32),
-        lax.psum_scatter(
-            up_b_grad.astype(jnp.bfloat16), "rows", scatter_dimension=0, tiled=True
-        ).astype(jnp.float32),
-        lax.psum_scatter(
-            merge_grad.astype(jnp.bfloat16), "rows", scatter_dimension=0, tiled=True
-        ).astype(jnp.float32),
-        lax.psum_scatter(
-            ff_in_grad.astype(jnp.bfloat16), "rows", scatter_dimension=0, tiled=True
-        ).astype(jnp.float32),
-        lax.psum_scatter(
-            ff_out_grad.astype(jnp.bfloat16), "rows", scatter_dimension=0, tiled=True
-        ).astype(jnp.float32),
-    )
-    (
-        section_a,
-        section_b,
-        section_c,
-        section_d,
-        section_e,
-        section_f,
-        section_g,
-        section_h,
-        section_i,
-    ) = first_section
-    summed = (
-        lax.psum_scatter(
-            section_a.astype(jnp.bfloat16), "var", scatter_dimension=1, tiled=True
-        ).astype(jnp.float32),
-        lax.psum_scatter(
-            section_b.astype(jnp.bfloat16), "var", scatter_dimension=1, tiled=True
-        ).astype(jnp.float32),
-        lax.psum_scatter(
-            section_c.astype(jnp.bfloat16), "var", scatter_dimension=1, tiled=True
-        ).astype(jnp.float32),
-        lax.psum_scatter(
-            section_d.astype(jnp.bfloat16), "var", scatter_dimension=1, tiled=True
-        ).astype(jnp.float32),
-        lax.psum_scatter(
-            section_e.astype(jnp.bfloat16), "var", scatter_dimension=1, tiled=True
-        ).astype(jnp.float32),
-        lax.psum_scatter(
-            section_f.astype(jnp.bfloat16), "var", scatter_dimension=1, tiled=True
-        ).astype(jnp.float32),
-        lax.psum_scatter(
-            section_g.astype(jnp.bfloat16), "var", scatter_dimension=1, tiled=True
-        ).astype(jnp.float32),
-        lax.psum_scatter(
-            section_h.astype(jnp.bfloat16), "var", scatter_dimension=1, tiled=True
-        ).astype(jnp.float32),
-        lax.psum_scatter(
-            section_i.astype(jnp.bfloat16), "var", scatter_dimension=1, tiled=True
-        ).astype(jnp.float32),
-    )
-    return (
-        predicted,
-        series_grad,
-        embed_sum,
-        head_sum,
-        summed[0],
-        summed[1],
-        summed[2],
-        summed[3],
-        summed[4],
-        summed[5],
-        summed[6],
-        summed[7],
-        summed[8],
-        gains_sum,
-    )
+        "rtd,kd->rtk", hidden_grad_low, embed_matrix, preferred_element_type=jnp.float32
+    )
+    series_grad = 0.0
+    for tap, offset in enumerate((1, 0, -1)):
+        inside = same_window(marks, offset)[:, :, None]
+        piece = column_grad[..., tap * variates : (tap + 1) * variates] * inside
+        series_grad = series_grad + shift_rows(piece, -offset)
+    outward = lax.all_to_all(
+        jnp.stack([predicted, series_grad]), "var", split_axis=3, concat_axis=1, tiled=True
+    )
+    embed_sum, head_sum, gains_sum = lax.psum(
+        (embed_grad, head_grad, gains_grad), ("rows", "var")
+    )
+    embed_sum = lax.dynamic_slice_in_dim(embed_sum, var_index * local_groups, local_groups, 0)
+    head_sum = lax.dynamic_slice_in_dim(head_sum, var_index * local_groups, local_groups, 0)
+    summed = tuple(scatter_sum(grad, row_shards, column_shards) for grad in weight_grads)
+    return (outward[0], outward[1], embed_sum, head_sum, *summed, gains_sum)
 
 
 def solution(mesh):

time: 1920 us -> 1630 us (0.85)
  matrix products: 361 us -> 252 us
  other arithmetic: 487 us -> 388 us
  blocking collectives: 111 us -> 55.1 us
  local copies, waits for them, and re-layouts: 326 us -> 287 us
    reduce_scatter x12 -> x9, waiting for transfers between devices: 426 us -> 604 us  [scatter_sum(): lax.psum_scatter(pieces, ('rows', 'var'), scatter_dimension=0, tiled=True)]
    dot_general x18 -> x11, matrix products: 199 us -> 78 us  [product(): return jnp.dot(left, right, preferred_element_type=jnp.float32)]
    unnamed x24 -> x9, waiting for transfers between devices: 108 us -> 0.15 us
    reshape x1 -> x12, local copies, waits for them, and re-layouts: 0.05 us -> 79.1 us  [the longest x9 78.8 us: scatter_sum(): grad.astype(jnp.bfloat16)]
    psum x2 -> x1, blocking collectives: 111 us -> 43.1 us  [body(): lax.psum((embed_grad, head_grad, gains_grad), ('rows', 'var'))]
    all_to_all x4 -> x2, waiting for transfers between devices: 56.2 us -> 0.01 us  [the longest x1 0.01 us: body(): lax.all_to_all(estimate_cotangent, 'var', split_axis=0, concat_axis=2, ti...]
    transpose x1 -> x9, local copies, waits for them, and re-layouts: 0.08 us -> 55.4 us  [scatter_sum(): pieces = pieces.transpose(0, 2, 1, 3).reshape(-1, width // column_shards)]
    slice x16 -> x8, local copies, waits for them, and re-layouts: 103 us -> 49.7 us  [shift_rows(): return jnp.concatenate([values[:, -offset:], filler], axis=1)]
  transfers between devices with their start and end apart: 22 -> 11, of which waited for: 13 -> 5; matrix products, arithmetic and copies ran while one was open for 31% -> 52% of each run, Pallas kernels for 0% -> 0%
where the time goes in v1:
time: 1630 us; the launch traced here: 1610 us
  waiting for transfers between devices  605 us (37%)
  other arithmetic  388 us (24%)
  local copies, waits for them, and re-layouts  287 us (18%)
  matrix products  252 us (15%)
  blocking collectives  55.1 us (3%)
  between operations  16.7 us (1%)
    reduce_scatter x9, waiting for transfers between devices, scatter_sum(): lax.psum_scatter(pieces, ('rows', 'var'), scatter_dimension=0, tiled=True)  604 us
    mul x8, other arithmetic, window_mean(): running = running + shift_rows(values, offset) * inside[..., None]  124 us
    reshape x9, local copies, waits for them, and re-layouts, scatter_sum(): grad.astype(jnp.bfloat16)  78.8 us
    dot_general x11, matrix products, product(): return jnp.dot(left, right, preferred_element_type=jnp.float32)  78 us
    convert_element_type x1, other arithmetic, mixer_forward(): inner_low = gelu_exact(inner_pre).astype(jnp.bfloat16)  59.6 us
    convert_element_type x1, other arithmetic, body(): hidden_grad_low = hidden_grad.astype(jnp.bfloat16)  58.9 us
    transpose x9, local copies, waits for them, and re-layouts, scatter_sum(): pieces = pieces.transpose(0, 2, 1, 3).reshape(-1, width // column_shards)  55.4 us
    slice x8, local copies, waits for them, and re-layouts, shift_rows(): return jnp.concatenate([values[:, -offset:], filler], axis=1)  49.7 us
  transfers between devices with their start and end apart: 11, of which 5 were waited for; matrix products, arithmetic and copies ran while one was open for 52% of the time, Pallas kernels for 0%

profile of v1, /device:TPU:0, one launch (start us, length us, event | category | flops | bytes accessed | tf_op | source)
XLA Modules:
  0.0 1613.3 jit_solution(3855779374925000853)
XLA Ops:
  74.8 36.5 %fusion.43 = (bf16[4,768,512]{2,1,0:T(8,128)(2,1)}, f32[4,768,512]{2,1,0:T(8,128)}) fusion(bf16[4,768,512]{2,1,0:T(8,128)(2,1)} %copy-done.2, f32[4,768]{1,0:T(4,128)S(1)} %get-tuple-element.123, f32[4,768]{1,0:T(4,128)S(1)} %get-tuple-element.127, f32[4,760,512]{2,1,0:T(8,128)} %get-tuple-element.200, f32[4,768]{1,0:T(4,128)S(1)} %get-tuple-element.126, ...), kind=kLoop, calls=%fused_computation.130 | loop fusion | flops 80216064 | bytes 112877568 | tf_op jit(solution)/shard_map/convert_element_type | solution.py:148
  225.5 22.0 %fusion.34 = (u8[768,2048]{1,0:T(8,128)(4,1)}, u8[768,2048]{1,0:T(8,128)(4,1)}, f32[4,768,2048]{2,1,0:T(8,128)}) fusion(bf16[512,2048]{1,0:T(8,128)(2,1)S(1)} %copy-done, f32[4,768,512]{2,1,0:T(8,128)} %copy.151, f32[512]{0:T(512)S(1)} %bitcast.506, f32[4,768]{1,0:T(4,128)S(1)} %fusion.139, f32[4,768]{1,0:T(4,128)S(1)} %broadcast_multiply_fusion.5), kind=kOutput, calls=%fused_computation.110 | convolution fusion | flops 6527385600 | bytes 36726784 | tf_op jit(solution)/shard_map/dot_general | solution.py:11
  247.5 59.6 %multiply_convert_fusion = (bf16[4,768,2048]{2,1,0:T(8,128)(2,1)S(1)}, f32[4,768,2048]{2,1,0:T(8,128)}) fusion(f32[4,768,2048]{2,1,0:T(8,128)} %get-tuple-element.341, u8[768,2048]{1,0:T(8,128)(4,1)} %get-tuple-element.15, u8[768,2048]{1,0:T(8,128)(4,1)} %get-tuple-element.14), kind=kLoop, calls=%fused_computation.8 | loop fusion | flops 440401920 | bytes 66060288 | tf_op jit(solution)/shard_map/convert_element_type | solution.py:160
  307.1 13.3 fusion.276
  334.8 26.6 %add_convert_fusion = bf16[4,768,2048]{2,1,0:T(8,128)(2,1)} fusion(f32[4,768,2048]{2,1,0:T(8,128)} %get-tuple-element.44, f32[4,768,2048]{2,1,0:T(8,128)} %get-tuple-element.341, bf16[2048,512]{1,0:T(8,128)(2,1)} %param.29, f32[4,768]{1,0:T(4,128)S(1)} %negate_multiply_fusion.4, bf16[512,4,768]{0,2,1:T(8,128)(2,1)} %copy-done.8, ...), kind=kOutput, calls=%fused_computation.7 | convolution fusion | flops 6544687104 | bytes 74500096 | tf_op jit(solution)/shard_map/rtd,fd->rtf/dot_general | solution.py:179
  361.4 14.3 multiply_reduce_fusion
  388.9 14.7 bitcast_convert_fusion.7
  409.3 16.2 %bitcast_convert_fusion.6 = bf16[2048,512]{1,0:T(8,128)(2,1)} fusion(bf16[4,768,2048]{2,1,0:T(8,128)(2,1)} %copy-done.14, f32[4,768]{1,0:T(4,128)S(1)} %negate_multiply_fusion.4, bf16[512,4,768]{0,2,1:T(8,128)(2,1)} %copy-done.8, f32[4,768,512]{2,1,0:T(8,128)} %get-tuple-element.343, f32[4,768]{1,0:T(4,128)S(1)} %get-tuple-element.275, ...), kind=kOutput, calls=%fused_computation.119 | convolution fusion | flops 6457655296 | bytes 24168448 | tf_op jit(solution)/shard_map/rtf,rtd->fd/dot_general | solution.py:176
  429.9 11.2 fusion.61
  441.4 10.6 multiply_reduce_fusion.1
  452.0 13.1 fusion.178
  483.2 13.4 reshape.471
  529.7 9.8 reshape.475
  591.6 12.5 reshape.469
  620.8 14.6 reshape.477
  635.4 11.7 copy.201
  669.1 12.5 reshape.473
  721.7 13.1 fusion.38
  740.0 9.8 slice_multiply_fusion.25
  758.4 17.6 %slice_multiply_fusion.7 = (f32[4,766,512]{2,1,0:T(8,128)}, f32[4,766,512]{2,1,0:T(8,128)}, f32[4,766,512]{2,1,0:T(8,128)}, f32[4,766,512]{2,1,0:T(8,128)}) fusion(f32[4,768,512]{2,1,0:T(8,128)} %fusion.37, f32[4,766]{1,0:T(4,128)S(1)} %slice.722, f32[4,766]{1,0:T(4,128)S(1)} %bitcast.495, f32[4,768,512]{2,1,0:T(8,128)} %get-tuple-element.35), kind=kLoop, calls=%fused_computation.51 | loop fusion | flops 6275072 | bytes 50225088 | tf_op jit(solution)/shard_map/transpose(jvp())/mul | solution.py:43
  776.1 17.5 %slice_multiply_fusion.8 = (f32[4,765,512]{2,1,0:T(8,128)}, f32[4,765,512]{2,1,0:T(8,128)}, f32[4,765,512]{2,1,0:T(8,128)}, f32[4,765,512]{2,1,0:T(8,128)}) fusion(f32[4,768,512]{2,1,0:T(8,128)} %fusion.37, f32[4,765]{1,0:T(4,128)S(1)} %slice.721, f32[4,765]{1,0:T(4,128)S(1)} %bitcast.494, f32[4,768,512]{2,1,0:T(8,128)} %get-tuple-element.35), kind=kLoop, calls=%fused_computation.52 | loop fusion | flops 6266880 | bytes 50159520 | tf_op jit(solution)/shard_map/transpose(jvp())/mul | solution.py:43
  793.6 17.6 %slice_multiply_fusion.9 = (f32[4,764,512]{2,1,0:T(8,128)}, f32[4,764,512]{2,1,0:T(8,128)}, f32[4,764,512]{2,1,0:T(8,128)}, f32[4,764,512]{2,1,0:T(8,128)}) fusion(f32[4,768,512]{2,1,0:T(8,128)} %fusion.37, f32[4,764]{1,0:T(4,128)S(1)} %slice.720, f32[4,764]{1,0:T(4,128)S(1)} %bitcast.493, f32[4,768,512]{2,1,0:T(8,128)} %get-tuple-element.35), kind=kLoop, calls=%fused_computation.53 | loop fusion | flops 6258688 | bytes 50093952 | tf_op jit(solution)/shard_map/transpose(jvp())/mul | solution.py:43
  811.2 17.7 %slice_multiply_fusion.10 = (f32[4,763,512]{2,1,0:T(8,128)}, f32[4,763,512]{2,1,0:T(8,128)}, f32[4,763,512]{2,1,0:T(8,128)}, f32[4,763,512]{2,1,0:T(8,128)}) fusion(f32[4,768,512]{2,1,0:T(8,128)} %fusion.37, f32[4,763]{1,0:T(4,128)S(1)} %slice.719, f32[4,763]{1,0:T(4,128)S(1)} %bitcast.492, f32[4,768,512]{2,1,0:T(8,128)} %get-tuple-element.35), kind=kLoop, calls=%fused_computation.54 | loop fusion | flops 6250496 | bytes 50028384 | tf_op jit(solution)/shard_map/transpose(jvp())/mul | solution.py:43
  828.9 17.6 %slice_multiply_fusion.6 = (f32[4,767,512]{2,1,0:T(8,128)}, f32[4,767,512]{2,1,0:T(8,128)}, f32[4,767,512]{2,1,0:T(8,128)}, f32[4,767,512]{2,1,0:T(8,128)}) fusion(f32[4,768,512]{2,1,0:T(8,128)} %fusion.37, f32[4,767]{1,0:T(4,128)S(1)} %slice.723, f32[4,767]{1,0:T(4,128)S(1)} %bitcast.496, f32[4,768,512]{2,1,0:T(8,128)} %get-tuple-element.35), kind=kLoop, calls=%fused_computation.50 | loop fusion | flops 6283264 | bytes 50290656 | tf_op jit(solution)/shard_map/transpose(jvp())/mul | solution.py:43
  846.4 17.5 %slice_multiply_fusion.11 = (f32[4,762,512]{2,1,0:T(8,128)}, f32[4,762,512]{2,1,0:T(8,128)}, f32[4,762,512]{2,1,0:T(8,128)}, f32[4,762,512]{2,1,0:T(8,128)}) fusion(f32[4,768,512]{2,1,0:T(8,128)} %fusion.37, f32[4,762]{1,0:T(4,128)S(1)} %slice.718, f32[4,762]{1,0:T(4,128)S(1)} %bitcast.491, f32[4,768,512]{2,1,0:T(8,128)} %get-tuple-element.35), kind=kLoop, calls=%fused_computation.55 | loop fusion | flops 6242304 | bytes 49962816 | tf_op jit(solution)/shard_map/transpose(jvp())/mul | solution.py:43
  864.0 58.9 %add_convert_fusion.1 = bf16[4,768,512]{2,1,0:T(8,128)(2,1)S(1)} fusion(f32[4,768,512]{2,1,0:T(8,128)} %copy-done.5, f32[4,762,512]{2,1,0:T(8,128)} %get-tuple-element.165, f32[4,763,512]{2,1,0:T(8,128)} %get-tuple-element.167, f32[4,764,512]{2,1,0:T(8,128)} %get-tuple-element.169, f32[4,765,512]{2,1,0:T(8,128)} %get-tuple-element.171, ...), kind=kLoop, calls=%fused_computation.93 | loop fusion | flops 56623104 | bytes 187834368 | tf_op jit(solution)/shard_map/convert_element_type | solution.py:308
  941.3 43.1 %all-reduce.142 = (f32[8,12,64]{2,0,1:T(8,128)S(1)}, f32[8,64,4]{1,2,0:T(4,128)S(1)}, f32[3,512]{1,0:T(4,128)}) all-reduce(f32[8,12,64]{2,0,1:T(8,128)S(1)} %pad_maximum_fusion.9, f32[8,64,4]{1,2,0:T(4,128)S(1)} %constant_dynamic-update-slice_fusion.2, ...), channel_id=1, replica_groups=mesh['rows'=8,'var'=4] {'rows','var'}, use_global_device_ids=true, to_apply=%region_24.25 | all-reduce | flops 9728 | bytes 77824 | tf_op jit(solution)/shard_map/psum | solution.py:330
  993.5 43.8 %reduce-scatter.18.cloned.1.call-done = bf16[768,128]{1,0:T(8,128)(2,1)} async-done(((bf16[24576,128]{1,0:T(8,128)(2,1)}), bf16[768,128]{1,0:T(8,128)(2,1)}) %reduce-scatter.18.cloned.1.call-update) | async-done | bytes 196624 | tf_op jit(solution)/shard_map/reduce_scatter | solution.py:239
  1039.0 117.8 %reduce-scatter.10.cloned.1.call-done = bf16[768,128]{1,0:T(8,128)(2,1)} async-done(((bf16[24576,128]{1,0:T(8,128)(2,1)}), bf16[768,128]{1,0:T(8,128)(2,1)}) %reduce-scatter.10.cloned.1.call-update) | async-done | bytes 196624 | tf_op jit(solution)/shard_map/reduce_scatter | solution.py:239
  1158.4 149.7 %reduce-scatter.12.cloned.1.call-done = bf16[1024,128]{1,0:T(8,128)(2,1)} async-done(((bf16[32768,128]{1,0:T(8,128)(2,1)}), bf16[1024,128]{1,0:T(8,128)(2,1)}) %reduce-scatter.12.cloned.1.call-update) | async-done | bytes 262160 | tf_op jit(solution)/shard_map/reduce_scatter | solution.py:239
  1310.0 146.6 %reduce-scatter.20.cloned.1.call-done = bf16[64,2048]{1,0:T(8,128)(2,1)} async-done(((bf16[2048,2048]{1,0:T(8,128)(2,1)}), bf16[64,2048]{1,0:T(8,128)(2,1)}) %reduce-scatter.20.cloned.1.call-update) | async-done | bytes 262160 | tf_op jit(solution)/shard_map/reduce_scatter | solution.py:239
  1458.3 146.5 %reduce-scatter.16.cloned.1.call-done = bf16[1024,128]{1,0:T(8,128)(2,1)} async-done(((bf16[32768,128]{1,0:T(8,128)(2,1)}), bf16[1024,128]{1,0:T(8,128)(2,1)}) %reduce-scatter.16.cloned.1.call-update) | async-done | bytes 262160 | tf_op jit(solution)/shard_map/reduce_scatter | solution.py:239
  (637 shorter events, 449.2 us)
Async XLA Ops:
  7.2 218.3 %copy-start = (bf16[512,2048]{1,0:T(8,128)(2,1)S(1)}, bf16[512,2048]{1,0:T(8,128)(2,1)}, u32[]{:S(2)}) copy-start(bf16[512,2048]{1,0:T(8,128)(2,1)} %param.28) | copy-start | bytes 6291460
  7.2 313.3 %all-to-all-start = ((bf16[16,768,8]{1,2,0:T(8,128)(2,1)}), bf16[16,768,8]{1,2,0:T(8,128)(2,1)}, u32[]{:S(2)}, u32[]{:S(2)}) async-start(bf16[16,768,8]{1,2,0:T(8,128)(2,1)} %param.31), calls=%async_computation | async-start | bytes 393216 | tf_op jit(solution)/shard_map/all_to_all | solution.py:287
  11.6 975.8 %reduce-scatter.22.cloned.1.call-start = ((), (), s32[]{:S(2)}) async-start(), calls=%async_computation.17 | async-start | bytes 1081344 | tf_op jit(solution)/shard_map/reduce_scatter | solution.py:239
  13.2 61.6 %copy-start.71 = (f32[4,768]{1,0:T(4,128)}, f32[4,768]{1,0:T(4,128)S(1)}, u32[]{:S(2)}) copy-start(f32[4,768]{1,0:T(4,128)S(1)} %get-tuple-element.107) | copy-start | bytes 36868
  20.4 54.4 %copy-start.108 = (f32[4,768]{1,0:T(4,128)}, f32[4,768]{1,0:T(4,128)S(1)}, u32[]{:S(2)}) copy-start(f32[4,768]{1,0:T(4,128)S(1)} %get-tuple-element.110) | copy-start | bytes 36868
  24.2 43.4 %copy-start.2 = (bf16[4,768,512]{2,1,0:T(8,128)(2,1)}, bf16[4,768,512]{2,1,0:T(8,128)(2,1)S(1)}, u32[]{:S(2)}) copy-start(bf16[4,768,512]{2,1,0:T(8,128)(2,1)S(1)} %convolution_convert_fusion.1) | copy-start | bytes 9437188
  74.5 36.8 %copy-start.61 = (f32[4,768]{1,0:T(4,128)}, f32[4,768]{1,0:T(4,128)S(1)}, u32[]{:S(2)}) copy-start(f32[4,768]{1,0:T(4,128)S(1)} %get-tuple-element.113) | copy-start | bytes 36868
  74.5 36.8 %copy-start.63 = (f32[4,768]{1,0:T(4,128)}, f32[4,768]{1,0:T(4,128)S(1)}, u32[]{:S(2)}) copy-start(f32[4,768]{1,0:T(4,128)S(1)} %get-tuple-element.114) | copy-start | bytes 36868
  74.6 36.8 %copy-start.65 = (f32[4,768]{1,0:T(4,128)}, f32[4,768]{1,0:T(4,128)S(1)}, u32[]{:S(2)}) copy-start(f32[4,768]{1,0:T(4,128)S(1)} %get-tuple-element.115) | copy-start | bytes 36868
  74.6 36.8 %copy-start.67 = (f32[4,768]{1,0:T(4,128)}, f32[4,768]{1,0:T(4,128)S(1)}, u32[]{:S(2)}) copy-start(f32[4,768]{1,0:T(4,128)S(1)} %get-tuple-element.116) | copy-start | bytes 36868
  74.6 36.8 %copy-start.69 = (f32[4,768]{1,0:T(4,128)}, f32[4,768]{1,0:T(4,128)S(1)}, u32[]{:S(2)}) copy-start(f32[4,768]{1,0:T(4,128)S(1)} %get-tuple-element.117) | copy-start | bytes 36868
  74.6 36.8 %copy-start.73 = (f32[4,768]{1,0:T(4,128)}, f32[4,768]{1,0:T(4,128)S(1)}, u32[]{:S(2)}) copy-start(f32[4,768]{1,0:T(4,128)S(1)} %get-tuple-element.112) | copy-start | bytes 36868
  74.6 36.8 %copy-start.75 = (f32[4,768]{1,0:T(4,128)}, f32[4,768]{1,0:T(4,128)S(1)}, u32[]{:S(2)}) copy-start(f32[4,768]{1,0:T(4,128)S(1)} %get-tuple-element.122) | copy-start | bytes 36868
  74.6 36.8 %copy-start.77 = (f32[4,768]{1,0:T(4,128)}, f32[4,768]{1,0:T(4,128)S(1)}, u32[]{:S(2)}) copy-start(f32[4,768]{1,0:T(4,128)S(1)} %get-tuple-element.121) | copy-start | bytes 36868
  74.6 36.8 %copy-start.79 = (f32[4,768]{1,0:T(4,128)}, f32[4,768]{1,0:T(4,128)S(1)}, u32[]{:S(2)}) copy-start(f32[4,768]{1,0:T(4,128)S(1)} %get-tuple-element.120) | copy-start | bytes 36868
  74.6 36.8 %copy-start.81 = (f32[4,768]{1,0:T(4,128)}, f32[4,768]{1,0:T(4,128)S(1)}, u32[]{:S(2)}) copy-start(f32[4,768]{1,0:T(4,128)S(1)} %get-tuple-element.119) | copy-start | bytes 36868
  74.6 36.8 %copy-start.83 = (f32[4,768]{1,0:T(4,128)}, f32[4,768]{1,0:T(4,128)S(1)}, u32[]{:S(2)}) copy-start(f32[4,768]{1,0:T(4,128)S(1)} %get-tuple-element.118) | copy-start | bytes 36868
  142.3 64.6 %copy-start.44 = (f32[1,512]{1,0:T(1,128)}, f32[1,512]{1,0:T(1,128)S(1)}, u32[]{:S(2)}) copy-start(f32[1,512]{1,0:T(1,128)S(1)} %get-tuple-element.278) | copy-start | bytes 6148
  247.5 59.6 %copy-start.6 = (f32[4,768,512]{2,1,0:T(8,128)S(1)}, f32[4,768,512]{2,1,0:T(8,128)}, u32[]{:S(2)}) copy-start(f32[4,768,512]{2,1,0:T(8,128)} %copy.151) | copy-start | bytes 18874372
  388.8 599.9 %reduce-scatter.24.cloned.1.call-start = ((), (), s32[]{:S(2)}) async-start(), calls=%async_computation.18 | async-start | bytes 2162688 | tf_op jit(solution)/shard_map/reduce_scatter | solution.py:239
  408.8 581.5 %reduce-scatter.26.cloned.1.call-start = ((), (), s32[]{:S(2)}) async-start(), calls=%async_computation.19 | async-start | bytes 2162688 | tf_op jit(solution)/shard_map/reduce_scatter | solution.py:239
  441.1 550.7 %reduce-scatter.14.cloned.1.call-start = ((), (), s32[]{:S(2)}) async-start(), calls=%async_computation.13 | async-start | bytes 6488064 | tf_op jit(solution)/shard_map/reduce_scatter | solution.py:239
  503.6 533.7 %reduce-scatter.18.cloned.1.call-start = ((), (), s32[]{:S(2)}) async-start(), calls=%async_computation.15 | async-start | bytes 6488064 | tf_op jit(solution)/shard_map/reduce_scatter | solution.py:239
  546.7 610.0 %reduce-scatter.10.cloned.1.call-start = ((), (), s32[]{:S(2)}) async-start(), calls=%async_computation.11 | async-start | bytes 6488064 | tf_op jit(solution)/shard_map/reduce_scatter | solution.py:239
  583.5 724.7 %reduce-scatter.12.cloned.1.call-start = ((), (), s32[]{:S(2)}) async-start(), calls=%async_computation.12 | async-start | bytes 8650752 | tf_op jit(solution)/shard_map/reduce_scatter | solution.py:239
  613.1 843.5 %reduce-scatter.20.cloned.1.call-start = ((), (), s32[]{:S(2)}) async-start(), calls=%async_computation.16 | async-start | bytes 8650752 | tf_op jit(solution)/shard_map/reduce_scatter | solution.py:239
  647.2 957.6 %reduce-scatter.16.cloned.1.call-start = ((), (), s32[]{:S(2)}) async-start(), calls=%async_computation.14 | async-start | bytes 8650752 | tf_op jit(solution)/shard_map/reduce_scatter | solution.py:239
  864.0 60.7 %copy-start.24 = (bf16[4,768,32]{1,2,0:T(8,128)(2,1)S(1)}, bf16[4,768,32]{1,2,0:T(8,128)(2,1)}, u32[]{:S(2)}) copy-start(bf16[4,768,32]{1,2,0:T(8,128)(2,1)} %copy-done.23) | copy-start | bytes 589828
  864.0 60.7 %copy-start.41 = (bf16[4,768,32]{1,2,0:T(8,128)(2,1)S(1)}, bf16[4,768,32]{1,2,0:T(8,128)(2,1)}, u32[]{:S(2)}) copy-start(bf16[4,768,32]{1,2,0:T(8,128)(2,1)} %copy-done.40) | copy-start | bytes 589828
  864.0 60.7 %copy-start.43 = (bf16[4,768,32]{1,2,0:T(8,128)(2,1)S(1)}, bf16[4,768,32]{1,2,0:T(8,128)(2,1)}, u32[]{:S(2)}) copy-start(bf16[4,768,32]{1,2,0:T(8,128)(2,1)} %copy-done.42) | copy-start | bytes 589828
  933.7 52.0 %all-to-all-start.1 = ((f32[2,4,768,32]{2,1,0,3:T(4,128)}), f32[2,4,768,32]{2,1,0,3:T(4,128)S(1)}, u32[]{:S(2)}, u32[]{:S(2)}) async-start(f32[2,4,768,32]{2,1,0,3:T(4,128)} %copy.159), calls=%async_computation.1 | async-start | bytes 1572864 | tf_op jit(solution)/shard_map/all_to_all | solution.py:327
  937.2 669.4 %copy-start.1 = (bf16[512,2048]{1,0:T(8,128)(2,1)S(1)}, bf16[512,2048]{1,0:T(8,128)(2,1)}, u32[]{:S(2)}) copy-start(bf16[512,2048]{1,0:T(8,128)(2,1)} %param.28) | copy-start | bytes 6291460
  (143 other events, 1058.1 us)
Sparse Core Ops, SparseCore 0:
  389.0 138.3 reduce-scatter.21
  529.6 134.4 reduce-scatter.23
  666.4 134.4 reduce-scatter.25
  806.4 110.8 reduce-scatter.13
  922.7 114.5 reduce-scatter.17
  1042.8 113.9 reduce-scatter.9
  1159.0 149.1 reduce-scatter.11
  1310.5 146.0 reduce-scatter.19
  1458.8 145.9 reduce-scatter.15

commit v2 on v1

v2 whole, which is shorter than its diff:
```python
import functools

import jax
import jax.numpy as jnp
from jax import lax
from jax.experimental import pallas as pl
from jax.experimental.pallas import tpu as pltpu
from jax.sharding import PartitionSpec as P

SA = 12
SB = 16
F32 = jnp.float32
BF16 = jnp.bfloat16
VMEM_LIMIT = 60 * 1024 * 1024


def nn(left, right):
    return lax.dot_general(left, right, (((1,), (0,)), ((), ())), preferred_element_type=F32)


def nt(left, right):
    return lax.dot_general(left, right, (((1,), (1,)), ((), ())), preferred_element_type=F32)


def tn(left, right):
    return lax.dot_general(left, right, (((0,), (0,)), ((), ())), preferred_element_type=F32)


def flip(values):
    return values.astype(F32).T.astype(BF16)


LANES = 128


def picked(ref, rows):
    return jnp.concatenate([ref[c, rows, :] for c in range(ref.shape[0])], axis=1)


def placed(ref, rows, values):
    for c in range(ref.shape[0]):
        ref[c, rows, :] = values[:, c * LANES : (c + 1) * LANES]


def norm_parts(values):
    centre = values - jnp.mean(values, axis=-1, keepdims=True)
    spread = jnp.mean(centre * centre, axis=-1, keepdims=True)
    scale = lax.rsqrt(spread + 1e-05)
    return centre * scale, scale


def norm_back(grad, unit, scale, gain):
    inner = grad * gain
    first = jnp.mean(inner, axis=-1, keepdims=True)
    second = jnp.mean(inner * unit, axis=-1, keepdims=True)
    return (inner - first - unit * second) * scale, jnp.sum(grad * unit, axis=0, keepdims=True)


def gelu_pair(values):
    size = jnp.abs(values)
    bell = jnp.exp(values * values * -0.5)
    t = 1.0 / (1.0 + size * (0.3275911 * 0.7071067811865476))
    series = t * (
        0.127414796
        + t * (-0.142248368 + t * (0.7107068705 + t * (-0.7265760135 + t * 0.5307027145)))
    )
    tail = series * bell
    below = jnp.where(values >= 0.0, 1.0 - tail, tail)
    return values * below, below + values * bell * 0.3989422804014327


def bands(marks_column, marks_row, row_start, column_start):
    height, width = marks_column.shape[0], marks_row.shape[1]
    here = lax.broadcasted_iota(jnp.int32, (height, width), 0) + row_start
    there = lax.broadcasted_iota(jnp.int32, (height, width), 1) + column_start
    gap = jnp.abs(here - there)
    same = marks_column == marks_row
    near = jnp.where(jnp.logical_and(same, gap <= 6), 1.0, 0.0).astype(BF16)
    wide = jnp.where(jnp.logical_and(same, gap <= 8), 1.0, 0.0).astype(BF16)
    return near, wide


def tiles_of(length):
    tile, span = 256, 512
    return [(at, min(max(at - 128, 0), length - span), tile, span) for at in range(0, length, tile)]


def front_kernel(signal_ref, flags_ref, marks_ref, weight_ref, trend_ref, seasonal_ref, hidden_ref):
    length = signal_ref.shape[0]
    variates = signal_ref.shape[1]
    signal = signal_ref[...].astype(F32)
    before = (pltpu.roll(signal, 1, 0) * flags_ref[:, 0:1]).astype(BF16)
    after = (pltpu.roll(signal, length - 1, 0) * flags_ref[:, 1:2]).astype(BF16)
    hidden = nn(before, weight_ref[0:variates, :])
    hidden = hidden + nn(signal_ref[...], weight_ref[variates : 2 * variates, :])
    hidden = hidden + nn(after, weight_ref[2 * variates : 3 * variates, :])
    hidden_ref[...] = hidden.astype(BF16)
    for at, low, tile, span in tiles_of(length):
        near, wide = bands(
            flags_ref[at : at + tile, 4:5], marks_ref[0, :, low : low + span], at, low
        )
        source = hidden_ref[low : low + span, :]
        trend = nn(near, source) * flags_ref[at : at + tile, 2:3]
        trend = trend + nn(wide, source) * flags_ref[at : at + tile, 3:4]
        trend_ref[at : at + tile, :] = trend
        placed(seasonal_ref, slice(at, at + tile), hidden_ref[at : at + tile, :].astype(F32) - trend)


def front(signal, flags, marks_row, weight, length):
    positions, variates = signal.shape
    width = weight.shape[1]
    whole = lambda shape: pl.BlockSpec(shape, lambda i: (0,) * len(shape))
    return pl.pallas_call(
        front_kernel,
        grid=(positions // length,),
        in_specs=[
            pl.BlockSpec((length, variates), lambda i: (i, 0)),
            pl.BlockSpec((length, flags.shape[1]), lambda i: (i, 0)),
            pl.BlockSpec((1, 1, length), lambda i: (i, 0, 0)),
            whole(weight.shape),
        ],
        out_specs=[
            pl.BlockSpec((length, width), lambda i: (i, 0)),
            pl.BlockSpec((width // LANES, length, LANES), lambda i: (0, i, 0)),
        ],
        out_shape=[
            jax.ShapeDtypeStruct((positions, width), F32),
            jax.ShapeDtypeStruct((width // LANES, positions, LANES), F32),
        ],
        scratch_shapes=[pltpu.VMEM((length, width), BF16)],
        compiler_params=pltpu.CompilerParams(vmem_limit_bytes=VMEM_LIMIT),
        name="front",
    )(signal, flags, marks_row, weight)


def scale_forward_kernel(
    stride, taps, step_taps,
    seasonal_ref, down_ref, iso_ref, up_ref, since_ref, gain_ref,
    lifted_ref, act_ref, second_ref, joined_ref,
    total,
):
    step = pl.program_id(0)
    blocks, width = act_ref.shape
    down_steps, iso_steps = stride // step_taps, taps // step_taps

    @pl.when(step == 0)
    def _():
        total[...] = jnp.zeros_like(total)

    @pl.when(step < down_steps)
    def _():
        sums = total[...]
        for k in range(step_taps):
            rows = picked(seasonal_ref, pl.ds(step * step_taps + k, blocks, stride=stride))
            sums = sums + nn(rows.astype(BF16), down_ref[k * width : (k + 1) * width, :])
        total[...] = sums

    @pl.when(step == down_steps - 1)
    def _():
        active = jnp.tanh(total[...])
        act_ref[...] = active
        total[...] = jnp.zeros_like(total)

    @pl.when(jnp.logical_and(step >= down_steps, step < down_steps + iso_steps))
    def _():
        sums = total[...]
        for k in range(step_taps):
            back = taps - 1 - ((step - down_steps) * step_taps + k)
            rows = pltpu.roll(act_ref[...], back, 0)
            rows = jnp.where(since_ref[...] >= back, rows, 0.0).astype(BF16)
            sums = sums + nn(rows, iso_ref[k * width : (k + 1) * width, :])
        total[...] = sums

    @pl.when(step == down_steps + iso_steps - 1)
    def _():
        second = jnp.tanh(total[...])
        second_ref[...] = second
        unit, _ = norm_parts(second + act_ref[...])
        joined_ref[...] = (unit * gain_ref[0:1, :]).astype(BF16)

    @pl.when(step >= down_steps + iso_steps)
    def _():
        for k in range(step_taps):
            lifted = nn(joined_ref[...], up_ref[:, k * width : (k + 1) * width])
            lifted_ref[k] = jnp.tanh(lifted).astype(BF16)


def scale_forward(seasonal, down, iso, up, since, gains, stride):
    width, positions = down.shape[1], seasonal.shape[1]
    blocks = positions // stride
    taps = iso.shape[0] // width
    step_taps = 2
    ds, isteps = stride // step_taps, taps // step_taps
    whole = lambda shape: pl.BlockSpec(
        shape, lambda t: (0,) * len(shape), pipeline_mode=pl.Buffered(1)
    )
    clip = lambda value, top: jnp.minimum(jnp.maximum(value, 0), top)
    return pl.pallas_call(
        functools.partial(scale_forward_kernel, stride, taps, step_taps),
        grid=(2 * ds + isteps,),
        in_specs=[
            whole(seasonal.shape),
            pl.BlockSpec((step_taps * width, width), lambda t: (clip(t, ds - 1), 0)),
            pl.BlockSpec((step_taps * width, width), lambda t: (clip(t - ds, isteps - 1), 0)),
            pl.BlockSpec((width, step_taps * width), lambda t: (0, clip(t - ds - isteps, ds - 1))),
            whole(since.shape),
            whole(gains.shape),
        ],
        out_specs=[
            pl.BlockSpec(
                (step_taps, blocks, width), lambda t: (clip(t - ds - isteps, ds - 1), 0, 0)
            ),
            pl.BlockSpec((blocks, width), lambda t: (0, 0)),
            pl.BlockSpec((blocks, width), lambda t: (0, 0)),
            pl.BlockSpec((blocks, width), lambda t: (0, 0)),
        ],
        out_shape=[
            jax.ShapeDtypeStruct((stride, blocks, width), BF16),
            jax.ShapeDtypeStruct((blocks, width), F32),
            jax.ShapeDtypeStruct((blocks, width), F32),
            jax.ShapeDtypeStruct((blocks, width), BF16),
        ],
        scratch_shapes=[pltpu.VMEM((blocks, width), F32)],
        compiler_params=pltpu.CompilerParams(vmem_limit_bytes=VMEM_LIMIT),
        name="scale_forward",
    )(seasonal, down, iso, up, since, gains)


def tail_kernel(
    lifted_a_ref, lifted_b_ref, seasonal_ref, trend_ref, cot_ref,
    merge_ref, ff_in_ref, ff_out_ref, head_ref, gains_ref,
    pred_ref, up_a_ref, up_b_ref, sres_ref,
    merge_out, ff_in_out, ff_out_out, head_out, gains_out,
    wide_a, wide_b, inner_all, pre_all, slope, mixed_all, outer_all, merged_all, stacked_all,
    result_all, merge_sum, ff_in_sum, ff_out_sum,
):
    row = pl.program_id(0)
    length, width = trend_ref.shape
    hidden = ff_in_ref.shape[1]
    tile, chunk = 256, 512
    stride_a, per_a = lifted_a_ref.shape[0], lifted_a_ref.shape[1]
    stride_b, per_b = lifted_b_ref.shape[0], lifted_b_ref.shape[1]

    @pl.when(row == 0)
    def _():
        merge_sum[...] = jnp.zeros_like(merge_sum)
        ff_in_sum[...] = jnp.zeros_like(ff_in_sum)
        ff_out_sum[...] = jnp.zeros_like(ff_out_sum)
        head_out[...] = jnp.zeros_like(head_out)
        gains_out[...] = jnp.zeros_like(gains_out)

    for j in range(stride_a):
        placed(wide_a, pl.ds(j, per_a, stride=stride_a), lifted_a_ref[j].astype(F32))
    for j in range(stride_b):
        placed(wide_b, pl.ds(j, per_b, stride=stride_b), lifted_b_ref[j].astype(F32))
    gain_0, gain_1, gain_2 = gains_ref[0:1, :], gains_ref[1:2, :], gains_ref[2:3, :]

    def part(at, carry):
        rows = pl.ds(pl.multiple_of(at * tile, tile), tile)
        seasonal = picked(seasonal_ref, rows)
        unit_a, scale_a = norm_parts(picked(wide_a, rows) + seasonal)
        unit_b, scale_b = norm_parts(picked(wide_b, rows) + seasonal)
        branch_a = (unit_a * gain_0).astype(BF16)
        branch_b = (unit_b * gain_0).astype(BF16)
        stacked_all[rows, 0:width] = branch_a
        stacked_all[rows, width : 2 * width] = branch_b
        merged = nn(branch_a, merge_ref[0:width, :]) + nn(branch_b, merge_ref[width:, :])
        unit_1, scale_1 = norm_parts(merged)
        mixed = unit_1 * gain_1
        mixed_low = mixed.astype(BF16)
        mixed_all[rows, :] = mixed_low
        total = mixed
        for c in range(0, hidden, chunk):
            inner, fall = gelu_pair(nn(mixed_low, ff_in_ref[:, c : c + chunk]))
            inner_low = inner.astype(BF16)
            inner_all[rows, c : c + chunk] = inner_low
            slope[:, c : c + chunk] = fall.astype(BF16)
            total = total + nn(inner_low, ff_out_ref[c : c + chunk, :])
        unit_2, scale_2 = norm_parts(total)
        result_low = (unit_2 * gain_2 + trend_ref[rows, :]).astype(BF16)
        result_all[rows, :] = result_low
        pred_ref[rows, :] = nn(result_low, head_ref[...])
        result_grad = nt(cot_ref[rows, :], head_ref[...]).astype(BF16).astype(F32)
        final_grad, gain_grad_2 = norm_back(result_grad, unit_2, scale_2, gain_2)
        outer_low = final_grad.astype(BF16)
        outer_all[rows, :] = outer_low
        mixed_grad = final_grad
        for c in range(0, hidden, chunk):
            back = nt(outer_low, ff_out_ref[c : c + chunk, :])
            pre_low = (back * slope[:, c : c + chunk].astype(F32)).astype(BF16)
            pre_all[rows, c : c + chunk] = pre_low
            mixed_grad = mixed_grad + nt(pre_low, ff_in_ref[:, c : c + chunk])
        merged_grad, gain_grad_1 = norm_back(mixed_grad, unit_1, scale_1, gain_1)
        merged_low = merged_grad.astype(BF16)
        merged_all[rows, :] = merged_low
        lifted_a_grad, gain_grad_a = norm_back(
            nt(merged_low, merge_ref[0:width, :]), unit_a, scale_a, gain_0
        )
        lifted_b_grad, gain_grad_b = norm_back(
            nt(merged_low, merge_ref[width:, :]), unit_b, scale_b, gain_0
        )
        sres_ref[rows, :] = lifted_a_grad + lifted_b_grad
        value = picked(wide_a, rows)
        placed(wide_a, rows, lifted_a_grad * (1.0 - value * value))
        value = picked(wide_b, rows)
        placed(wide_b, rows, lifted_b_grad * (1.0 - value * value))
        gains_out[0:1, :] += gain_grad_a + gain_grad_b
        gains_out[1:2, :] += gain_grad_1
        gains_out[2:3, :] += gain_grad_2
        return carry

    lax.fori_loop(0, length // tile, part, 0)
    for j in range(stride_a):
        up_a_ref[j] = picked(wide_a, pl.ds(j, per_a, stride=stride_a)).astype(BF16)
    for j in range(stride_b):
        up_b_ref[j] = picked(wide_b, pl.ds(j, per_b, stride=stride_b)).astype(BF16)
    mixed_t, outer_t, merged_t = flip(mixed_all[...]), flip(outer_all[...]), flip(merged_all[...])
    for c in range(0, hidden, chunk):
        ff_in_sum[:, c : c + chunk] += nn(mixed_t, pre_all[:, c : c + chunk])
        ff_out_sum[:, c : c + chunk] += nn(outer_t, inner_all[:, c : c + chunk])
    for c in range(0, 2 * width, chunk):
        merge_sum[:, c : c + chunk] += nn(merged_t, stacked_all[:, c : c + chunk])
    head_out[...] += tn(result_all[...], cot_ref[...])

    @pl.when(row == pl.num_programs(0) - 1)
    def _():
        for k in range(merge_out.shape[0]):
            size = merge_out.shape[2]
            merge_out[k] = merge_sum[:, k * size : (k + 1) * size].astype(BF16)
        for k in range(ff_in_out.shape[0]):
            size = ff_in_out.shape[2]
            ff_in_out[k] = ff_in_sum[:, k * size : (k + 1) * size].astype(BF16)
        for k in range(ff_out_out.shape[0]):
            size = ff_out_out.shape[2]
            ff_out_out[k] = ff_out_sum[:, k * size : (k + 1) * size].astype(BF16)


def tail(lifted_a, lifted_b, seasonal, trend, cot, merge, ff_in, ff_out, head, gains, length):
    positions, width = trend.shape
    hidden = ff_in.shape[1]
    outs = cot.shape[1]
    stride_a, stride_b = lifted_a.shape[0], lifted_b.shape[0]
    per_a, per_b = length // stride_a, length // stride_b
    fixed = lambda shape: pl.BlockSpec(
        shape, lambda i: (0,) * len(shape), pipeline_mode=pl.Buffered(1)
    )
    kept = lambda shape: pl.BlockSpec(shape, lambda i: (0,) * len(shape))
    by_row = lambda size: pl.BlockSpec((length, size), lambda i: (i, 0))
    by_tap = lambda taps, per: pl.BlockSpec((taps, per, width), lambda i: (0, i, 0))
    pieces = ((8, width, 128), (4, width, 512), (8, width, 256))
    return pl.pallas_call(
        tail_kernel,
        grid=(positions // length,),
        in_specs=[
            by_tap(stride_a, per_a), by_tap(stride_b, per_b),
            pl.BlockSpec((width // LANES, length, LANES), lambda i: (0, i, 0)), by_row(width),
            by_row(outs), fixed(merge.shape), fixed(ff_in.shape), fixed(ff_out.shape),
            fixed(head.shape), fixed(gains.shape),
        ],
        out_specs=[
            by_row(outs), by_tap(stride_a, per_a), by_tap(stride_b, per_b), by_row(width),
            *[fixed(piece) for piece in pieces], kept((width, outs)), kept(gains.shape),
        ],
        out_shape=[
            jax.ShapeDtypeStruct((positions, outs), F32),
            jax.ShapeDtypeStruct(lifted_a.shape, BF16),
            jax.ShapeDtypeStruct(lifted_b.shape, BF16),
            jax.ShapeDtypeStruct((positions, width), F32),
            *[jax.ShapeDtypeStruct(piece, BF16) for piece in pieces],
            jax.ShapeDtypeStruct((width, outs), F32),
            jax.ShapeDtypeStruct(gains.shape, F32),
        ],
        scratch_shapes=[
            pltpu.VMEM((width // LANES, length, LANES), F32),
            pltpu.VMEM((width // LANES, length, LANES), F32),
            pltpu.VMEM((length, hidden), BF16), pltpu.VMEM((length, hidden), BF16),
            pltpu.VMEM((256, hidden), BF16), pltpu.VMEM((length, width), BF16),
            pltpu.VMEM((length, width), BF16), pltpu.VMEM((length, width), BF16),
            pltpu.VMEM((length, 2 * width), BF16), pltpu.VMEM((length, width), BF16),
            pltpu.VMEM((width, 2 * width), F32), pltpu.VMEM((width, hidden), F32),
            pltpu.VMEM((width, hidden), F32),
        ],
        compiler_params=pltpu.CompilerParams(vmem_limit_bytes=VMEM_LIMIT),
        name="tail",
    )(lifted_a, lifted_b, seasonal, trend, cot, merge, ff_in, ff_out, head, gains)


def scale_backward_kernel(
    stride, taps, step_taps,
    pre_ref, up_ref, iso_ref, down_ref, act_ref, second_ref, since_ref, gain_ref,
    iso_pre_ref, down_pre_ref, block_ref, gain_out,
    total, spread,
):
    step = pl.program_id(0)
    blocks, width = act_ref.shape
    up_steps, iso_steps = stride // step_taps, taps // step_taps

    @pl.when(step == 0)
    def _():
        total[...] = jnp.zeros_like(total)
        spread[...] = jnp.zeros_like(spread)

    @pl.when(step < up_steps)
    def _():
        sums = total[...]
        for k in range(step_taps):
            sums = sums + nt(pre_ref[k], up_ref[:, k * width : (k + 1) * width])
        total[...] = sums

    @pl.when(step == up_steps - 1)
    def _():
        second = second_ref[...]
        unit, scale = norm_parts(second + act_ref[...])
        sum_grad, gain_grad = norm_back(total[...], unit, scale, gain_ref[0:1, :])
        gain_out[...] = gain_grad
        iso_pre_ref[...] = (sum_grad * (1.0 - second * second)).astype(BF16)
        spread[...] = sum_grad

    @pl.when(jnp.logical_and(step >= up_steps, step < up_steps + iso_steps))
    def _():
        for k in range(step_taps):
            back = taps - 1 - ((step - up_steps) * step_taps + k)
            grad = nt(iso_pre_ref[...], iso_ref[k * width : (k + 1) * width, :])
            grad = jnp.where(since_ref[...] >= back, grad, 0.0)
            spread[...] += pltpu.roll(grad, blocks - back, 0)

    @pl.when(step == up_steps + iso_steps - 1)
    def _():
        active = act_ref[...]
        down_pre_ref[...] = (spread[...] * (1.0 - active * active)).astype(BF16)

    @pl.when(step >= up_steps + iso_steps)
    def _():
        for k in range(step_taps):
            block_ref[k] = nt(
                down_pre_ref[...], down_ref[k * width : (k + 1) * width, :]
            ).astype(BF16)


def scale_backward(pre, up, iso, down, act, second, since, gains):
    stride, blocks, width = pre.shape
    taps = iso.shape[0] // width
    step_taps = 2
    us, isteps = stride // step_taps, taps // step_taps
    whole = lambda shape: pl.BlockSpec(
        shape, lambda t: (0,) * len(shape), pipeline_mode=pl.Buffered(1)
    )
    clip = lambda value, top: jnp.minimum(jnp.maximum(value, 0), top)
    return pl.pallas_call(
        functools.partial(scale_backward_kernel, stride, taps, step_taps),
        grid=(2 * us + isteps,),
        in_specs=[
            pl.BlockSpec((step_taps, blocks, width), lambda t: (clip(t, us - 1), 0, 0)),
            pl.BlockSpec((width, step_taps * width), lambda t: (0, clip(t, us - 1))),
            pl.BlockSpec((step_taps * width, width), lambda t: (clip(t - us, isteps - 1), 0)),
            pl.BlockSpec(
                (step_taps * width, width), lambda t: (clip(t - us - isteps, us - 1), 0)
            ),
            whole(act.shape), whole(second.shape), whole(since.shape), whole(gains.shape),
        ],
        out_specs=[
            pl.BlockSpec((blocks, width), lambda t: (0, 0)),
            pl.BlockSpec((blocks, width), lambda t: (0, 0)),
            pl.BlockSpec(
                (step_taps, blocks, width), lambda t: (clip(t - us - isteps, us - 1), 0, 0)
            ),
            pl.BlockSpec((1, width), lambda t: (0, 0)),
        ],
        out_shape=[
            jax.ShapeDtypeStruct((blocks, width), BF16),
            jax.ShapeDtypeStruct((blocks, width), BF16),
            jax.ShapeDtypeStruct((stride, blocks, width), BF16),
            jax.ShapeDtypeStruct((1, width), F32),
        ],
        scratch_shapes=[pltpu.VMEM((blocks, width), F32), pltpu.VMEM((blocks, width), F32)],
        compiler_params=pltpu.CompilerParams(vmem_limit_bytes=VMEM_LIMIT),
        name="scale_backward",
    )(pre, up, iso, down, act, second, since, gains)


def up_grad_kernel(joined_ref, pre_ref, out_ref, turned):
    @pl.when(pl.program_id(0) == 0)
    def _():
        turned[...] = flip(joined_ref[...])

    for k in range(pre_ref.shape[0]):
        out_ref[k] = nn(turned[...], pre_ref[k]).astype(BF16)


def up_grad(joined, pre):
    stride, blocks, width = pre.shape
    step_taps = 2
    return pl.pallas_call(
        up_grad_kernel,
        grid=(stride // step_taps,),
        in_specs=[
            pl.BlockSpec((blocks, width), lambda t: (0, 0)),
            pl.BlockSpec((step_taps, blocks, width), lambda t: (t, 0, 0)),
        ],
        out_specs=pl.BlockSpec((step_taps, width, width), lambda t: (t, 0, 0)),
        out_shape=jax.ShapeDtypeStruct((stride, width, width), BF16),
        scratch_shapes=[pltpu.VMEM((width, blocks), BF16)],
        compiler_params=pltpu.CompilerParams(vmem_limit_bytes=VMEM_LIMIT),
        name="up_grad",
    )(joined, pre)


def store_halves(out_ref, k, product):
    half = out_ref.shape[2]
    out_ref[2 * k] = product[:, :half].astype(BF16)
    out_ref[2 * k + 1] = product[:, half:].astype(BF16)


def iso_grad_kernel(taps, step_taps, pre_ref, act_ref, since_ref, out_ref, turned):
    step = pl.program_id(0)
    blocks, width = act_ref.shape

    @pl.when(step == 0)
    def _():
        turned[...] = flip(pre_ref[...])

    for k in range(step_taps):
        back = taps - 1 - (step * step_taps + k)
        rows = pltpu.roll(act_ref[...], back, 0)
        rows = jnp.where(since_ref[...] >= back, rows, 0.0).astype(BF16)
        store_halves(out_ref, k, nn(turned[...], rows))


def iso_grad(pre, act, since, taps):
    blocks, width = act.shape
    step_taps = 2
    whole = lambda shape: pl.BlockSpec(shape, lambda t: (0,) * len(shape))
    return pl.pallas_call(
        functools.partial(iso_grad_kernel, taps, step_taps),
        grid=(taps // step_taps,),
        in_specs=[whole(pre.shape), whole(act.shape), whole(since.shape)],
        out_specs=pl.BlockSpec((2 * step_taps, width, width // 2), lambda t: (t, 0, 0)),
        out_shape=jax.ShapeDtypeStruct((2 * taps, width, width // 2), BF16),
        scratch_shapes=[pltpu.VMEM((width, blocks), BF16)],
        compiler_params=pltpu.CompilerParams(vmem_limit_bytes=VMEM_LIMIT),
        name="iso_grad",
    )(pre, act, since)


def down_grad_kernel(stride, step_taps, pre_ref, seasonal_ref, out_ref, turned):
    step = pl.program_id(0)
    blocks = pre_ref.shape[0]

    @pl.when(step == 0)
    def _():
        turned[...] = flip(pre_ref[...])

    for k in range(step_taps):
        rows = picked(seasonal_ref, pl.ds(step * step_taps + k, blocks, stride=stride))
        store_halves(out_ref, k, nn(turned[...], rows.astype(BF16)))


def down_grad(pre, seasonal):
    blocks, width = pre.shape
    stride = seasonal.shape[1] // blocks
    step_taps = 2
    whole = lambda shape: pl.BlockSpec(
        shape, lambda t: (0,) * len(shape), pipeline_mode=pl.Buffered(1)
    )
    return pl.pallas_call(
        functools.partial(down_grad_kernel, stride, step_taps),
        grid=(stride // step_taps,),
        in_specs=[whole(pre.shape), whole(seasonal.shape)],
        out_specs=pl.BlockSpec((2 * step_taps, width, width // 2), lambda t: (t, 0, 0)),
        out_shape=jax.ShapeDtypeStruct((2 * stride, width, width // 2), BF16),
        scratch_shapes=[pltpu.VMEM((width, blocks), BF16)],
        compiler_params=pltpu.CompilerParams(vmem_limit_bytes=VMEM_LIMIT),
        name="down_grad",
    )(pre, seasonal)


def back_kernel(
    sres_ref, block_a_ref, block_b_ref, cot_ref, head_ref, signal_ref, flags_ref, marks_ref,
    weight_ref, series_ref, embed_ref, season, low_near, low_wide, hidden,
):
    length, width = sres_ref.shape
    variates = signal_ref.shape[1]
    stride_a, per_a = block_a_ref.shape[0], block_a_ref.shape[1]
    stride_b, per_b = block_b_ref.shape[0], block_b_ref.shape[1]

    @pl.when(pl.program_id(0) == 0)
    def _():
        embed_ref[...] = jnp.zeros_like(embed_ref)

    placed(season, slice(0, length), sres_ref[...])
    for j in range(stride_a):
        at = pl.ds(j, per_a, stride=stride_a)
        placed(season, at, picked(season, at) + block_a_ref[j].astype(F32))
    for j in range(stride_b):
        at = pl.ds(j, per_b, stride=stride_b)
        placed(season, at, picked(season, at) + block_b_ref[j].astype(F32))
    result_grad = nt(cot_ref[...], head_ref[...]).astype(BF16).astype(F32)
    gap = result_grad - picked(season, slice(0, length))
    low_near[...] = (gap * flags_ref[:, 2:3]).astype(BF16)
    low_wide[...] = (gap * flags_ref[:, 3:4]).astype(BF16)
    for at, low, tile, span in tiles_of(length):
        near, wide = bands(
            flags_ref[at : at + tile, 4:5], marks_ref[0, :, low : low + span], at, low
        )
        total = picked(season, slice(at, at + tile)) + nn(near, low_near[low : low + span, :])
        total = total + nn(wide, low_wide[low : low + span, :])
        hidden[at : at + tile, :] = total.astype(BF16)
    grad = hidden[...]
    first = nt(grad, weight_ref[0:variates, :]) * flags_ref[:, 0:1]
    last = nt(grad, weight_ref[2 * variates :, :]) * flags_ref[:, 1:2]
    series_ref[...] = (
        nt(grad, weight_ref[variates : 2 * variates, :])
        + pltpu.roll(first, length - 1, 0)
        + pltpu.roll(last, 1, 0)
    )
    signal = signal_ref[...].astype(F32)
    before = (pltpu.roll(signal, 1, 0) * flags_ref[:, 0:1]).astype(BF16)
    after = (pltpu.roll(signal, length - 1, 0) * flags_ref[:, 1:2]).astype(BF16)
    embed_ref[0:variates, :] += tn(before, grad)
    embed_ref[variates : 2 * variates, :] += tn(signal_ref[...], grad)
    embed_ref[2 * variates :, :] += tn(after, grad)


def back(sres, block_a, block_b, cot, head, signal, flags, marks_row, weight, length):
    positions, width = sres.shape
    variates = signal.shape[1]
    stride_a, stride_b = block_a.shape[0], block_b.shape[0]
    whole = lambda shape: pl.BlockSpec(shape, lambda i: (0,) * len(shape))
    by_row = lambda size: pl.BlockSpec((length, size), lambda i: (i, 0))
    return pl.pallas_call(
        back_kernel,
        grid=(positions // length,),
        in_specs=[
            by_row(width),
            pl.BlockSpec((stride_a, length // stride_a, width), lambda i: (0, i, 0)),
            pl.BlockSpec((stride_b, length // stride_b, width), lambda i: (0, i, 0)),
            by_row(cot.shape[1]), whole(head.shape), by_row(variates), by_row(flags.shape[1]),
            pl.BlockSpec((1, 1, length), lambda i: (i, 0, 0)), whole(weight.shape),
        ],
        out_specs=[by_row(variates), whole(weight.shape)],
        out_shape=[
            jax.ShapeDtypeStruct((positions, variates), F32),
            jax.ShapeDtypeStruct(weight.shape, F32),
        ],
        scratch_shapes=[
            pltpu.VMEM((width // LANES, length, LANES), F32), pltpu.VMEM((length, width), BF16),
            pltpu.VMEM((length, width), BF16), pltpu.VMEM((length, width), BF16),
        ],
        compiler_params=pltpu.CompilerParams(vmem_limit_bytes=VMEM_LIMIT),
        name="back",
    )(sres, block_a, block_b, cot, head, signal, flags, marks_row, weight)


def block_diagonal(pieces):
    count, height, width = pieces.shape
    eye = jnp.eye(count, dtype=pieces.dtype)
    spread = pieces[:, :, None, :] * eye[:, None, :, None]
    return spread.reshape(count * height, count * width)


def diagonal_blocks(matrix, count):
    height, width = matrix.shape[0] // count, matrix.shape[1] // count
    blocks = matrix.reshape(count, height, count, width)
    return jnp.stack([blocks[at, :, at, :] for at in range(count)])


def same_window(marks, offset):
    length = marks.shape[1]
    filler = jnp.full_like(marks[:, : abs(offset)], -1)
    if offset > 0:
        moved = jnp.concatenate([filler, marks[:, : length - offset]], axis=1)
    else:
        moved = jnp.concatenate([marks[:, -offset:], filler], axis=1)
    return (moved == marks).astype(F32)


def window_flags(marks):
    near = jnp.ones(marks.shape, F32)
    for offset in range(1, 7):
        near = near + same_window(marks, offset) + same_window(marks, -offset)
    wide = near
    for offset in range(7, 9):
        wide = wide + same_window(marks, offset) + same_window(marks, -offset)
    zero = jnp.zeros_like(near)
    columns = [
        same_window(marks, 1), same_window(marks, -1), 0.5 / near, 0.5 / wide,
        marks.astype(F32), zero, zero, zero,
    ]
    return jnp.stack(columns, axis=-1).reshape(-1, len(columns))


def blocks_since_start(marks, stride, taps):
    coarse = marks[:, ::stride]
    since = jnp.zeros(coarse.shape, F32)
    for offset in range(1, taps):
        since = since + same_window(coarse, offset)
    return since.astype(jnp.int32).reshape(-1, 1)


def log2_of(size):
    return size.bit_length() - 1


def exchange(parts, axis, bit_axis, bit):
    rows, columns = lax.axis_size("rows"), lax.axis_size("var")
    mine = (lax.axis_index(bit_axis) >> bit) & 1
    pairs = []
    for r in range(rows):
        for c in range(columns):
            to = (r ^ (1 << bit), c) if bit_axis == "rows" else (r, c ^ (1 << bit))
            pairs.append((r * columns + c, to[0] * columns + to[1]))
    sent = lax.dynamic_index_in_dim(parts, 1 - mine, axis, keepdims=False)
    kept = lax.dynamic_index_in_dim(parts, mine, axis, keepdims=False)
    got = lax.ppermute(sent, ("rows", "var"), pairs)
    return (kept.astype(F32) + got.astype(F32)).astype(BF16)


def scatter_sum(grad, by_rows, order, shape):
    rows, columns = lax.axis_size("rows"), lax.axis_size("var")
    count, width, size = grad.shape
    outer, inner = (rows, columns) if by_rows else (columns, rows)
    names = ("rows", "var") if by_rows else ("var", "rows")
    if count % outer or width % (16 * inner) or rows & (rows - 1) or columns & (columns - 1):
        full = grad.transpose(1, 0, 2).reshape(width, count * size)
        full = full.T if by_rows else full
        height, depth = full.shape
        full = full.reshape(rows, height // rows, columns, depth // columns)
        full = full.transpose(0, 2, 1, 3).reshape(-1, depth // columns)
        return lax.psum_scatter(full, ("rows", "var"), scatter_dimension=0, tiled=True).astype(F32)
    labels = [(names[0], bit) for bit in reversed(range(log2_of(outer)))]
    labels += [None]
    labels += [(names[1], bit) for bit in reversed(range(log2_of(inner)))]
    parts = grad.reshape(
        (2,) * log2_of(outer) + (count // outer,) + (2,) * log2_of(inner) + (width // inner, size)
    )
    for label in order(log2_of(rows), log2_of(columns)):
        axis = labels.index(label)
        parts = exchange(parts, axis, *label)
        labels.pop(axis)
    parts = parts.astype(F32)
    if by_rows:
        return parts.transpose(0, 2, 1).reshape(shape)
    return parts.transpose(1, 0, 2).reshape(shape)


def across_first(row_bits, column_bits):
    return [("var", bit) for bit in range(column_bits)] + [("rows", bit) for bit in range(row_bits)]


def rows_first(row_bits, column_bits):
    return (
        [("var", 0), ("rows", 0)]
        + [("var", bit) for bit in range(1, column_bits)]
        + [("rows", bit) for bit in range(1, row_bits)]
    )


def body(
    signal_matrix, frame_numbers, variate_order, embed_weight, head_weight,
    down_a, iso_a, up_a, down_b, iso_b, up_b, merge_weight, ff_in, ff_out,
    norm_gains, estimate_cotangent,
):
    rows, columns = lax.axis_size("rows"), lax.axis_size("var")
    var_index = lax.axis_index("var")
    local_rows, length, variates = signal_matrix.shape
    local_groups = embed_weight.shape[0]
    per_group = head_weight.shape[2]
    groups = local_groups * columns
    time_rows = local_rows // columns
    width = norm_gains.shape[1]
    embed_all, head_all = lax.all_gather((embed_weight, head_weight), "var", axis=0, tiled=True)
    cotangent = lax.all_to_all(
        estimate_cotangent, "var", split_axis=0, concat_axis=2, tiled=True
    ).reshape(-1, variates)
    pick = jax.nn.one_hot(variate_order, variates, dtype=BF16)
    by_group = [
        block_diagonal(embed_all[:, tap * per_group : (tap + 1) * per_group]) for tap in range(3)
    ]
    by_signal = jnp.concatenate([tn(pick, part).astype(BF16) for part in by_group], axis=0)
    by_group = jnp.concatenate(by_group, axis=0)
    head_matrix = block_diagonal(head_all)
    signal = lax.dynamic_slice_in_dim(signal_matrix, var_index * time_rows, time_rows, 0)
    signal = signal.reshape(-1, variates)
    marks = lax.dynamic_slice_in_dim(frame_numbers, var_index * time_rows, time_rows, 0)
    flags = window_flags(marks)
    marks_row = marks.astype(F32).reshape(time_rows, 1, length)
    since_a = blocks_since_start(marks, SA, iso_a.shape[0] // width)
    since_b = blocks_since_start(marks, SB, iso_b.shape[0] // width)

    trend, seasonal = front(signal, flags, marks_row, by_signal, length)
    lifted_a, act_a, second_a, joined_a = scale_forward(
        seasonal, down_a, iso_a, up_a, since_a, norm_gains, SA
    )
    lifted_b, act_b, second_b, joined_b = scale_forward(
        seasonal, down_b, iso_b, up_b, since_b, norm_gains, SB
    )
    (
        predicted, pre_a, pre_b, sres, merge_parts, ff_in_parts, ff_out_parts, head_full, gains_late,
    ) = tail(
        lifted_a, lifted_b, seasonal, trend, cotangent, merge_weight, ff_in, ff_out,
        head_matrix, norm_gains, length,
    )
    up_a_parts = up_grad(joined_a, pre_a)
    up_b_parts = up_grad(joined_b, pre_b)
    iso_pre_a, down_pre_a, block_a, gain_a = scale_backward(
        pre_a, up_a, iso_a, down_a, act_a, second_a, since_a, norm_gains
    )
    iso_pre_b, down_pre_b, block_b, gain_b = scale_backward(
        pre_b, up_b, iso_b, down_b, act_b, second_b, since_b, norm_gains
    )
    iso_a_parts = iso_grad(iso_pre_a, act_a, since_a, iso_a.shape[0] // width)
    iso_b_parts = iso_grad(iso_pre_b, act_b, since_b, iso_b.shape[0] // width)
    down_a_parts = down_grad(down_pre_a, seasonal)
    down_b_parts = down_grad(down_pre_b, seasonal)
    series_grad, embed_full = back(
        sres, block_a, block_b, cotangent, head_matrix, signal, flags, marks_row, by_group, length
    )
    gains_grad = jnp.concatenate([gains_late[0:1] + gain_a + gain_b, gains_late[1:]], axis=0)
    embed_full = jnp.einsum(
        "cv,tvd->tcd", pick.astype(F32), embed_full.reshape(3, variates, width),
        precision=lax.Precision.HIGHEST,
    )
    embed_grad = jnp.concatenate([diagonal_blocks(embed_full[tap], groups) for tap in range(3)], 1)
    head_grad = diagonal_blocks(head_full, groups)
    outward = jnp.stack([predicted, series_grad]).reshape(2, time_rows, length, variates)
    outward = lax.all_to_all(outward, "var", split_axis=3, concat_axis=1, tiled=True)
    embed_sum, head_sum, gains_sum = lax.psum((embed_grad, head_grad, gains_grad), ("rows", "var"))
    embed_sum = lax.dynamic_slice_in_dim(embed_sum, var_index * local_groups, local_groups, 0)
    head_sum = lax.dynamic_slice_in_dim(head_sum, var_index * local_groups, local_groups, 0)

    def shard(weight):
        return (weight.shape[0] // rows, weight.shape[1] // columns)

    summed = (
        scatter_sum(down_a_parts, True, across_first, shard(down_a)),
        scatter_sum(iso_a_parts, True, rows_first, shard(iso_a)),
        scatter_sum(up_a_parts, False, across_first, shard(up_a)),
        scatter_sum(down_b_parts, True, rows_first, shard(down_b)),
        scatter_sum(iso_b_parts, True, across_first, shard(iso_b)),
        scatter_sum(up_b_parts, False, rows_first, shard(up_b)),
        scatter_sum(merge_parts, True, across_first, shard(merge_weight)),
        scatter_sum(ff_in_parts, False, rows_first, shard(ff_in)),
        scatter_sum(ff_out_parts, True, across_first, shard(ff_out)),
    )
    return (outward[0], outward[1], embed_sum, head_sum, *summed, gains_sum)


def solution(mesh):
    placed = (
        P("rows", None, None),
        P("rows", None),
        P(),
        P("var", None, None),
        P("var", None, None),
        P(),
        P(),
        P(),
        P(),
        P(),
        P(),
        P(),
        P(),
        P(),
        P(),
        P("rows", None, "var"),
    )
    return jax.shard_map(
        body,
        mesh=mesh,
        in_specs=placed,
        out_specs=(
            P("rows", None, "var"),
            P("rows", None, "var"),
            P("var", None, None),
            P("var", None, None),
            P("rows", "var"),
            P("rows", "var"),
            P("rows", "var"),
            P("rows", "var"),
            P("rows", "var"),
            P("rows", "var"),
            P("rows", "var"),
            P("rows", "var"),
            P("rows", "var"),
            P(),
        ),
        check_vma=False,
    )
```

time: 1630 us -> 800 us (0.49)
  waiting for transfers between devices: 605 us -> 243 us
  other arithmetic: 388 us -> 56.2 us
  Pallas kernels: 0 us -> 285 us
  matrix products: 252 us -> 3.95 us
  local copies, waits for them, and re-layouts: 287 us -> 85.6 us
  starting transfers between devices: 9.38 us -> 55.8 us
    reduce_scatter x9 -> x0, waiting for transfers between devices: 604 us -> none  [scatter_sum(): lax.psum_scatter(pieces, ('rows', 'var'), scatter_dimension=0, tiled=True)]
    pallas_call x0 -> x13, Pallas kernels: none -> 285 us  [the longest x1 112 us: tail(): pl.pallas_call(tail_kernel, grid=(positions // length,), in_specs=[by_tap...]
    dot_general x34 -> x4, matrix products: 252 us -> 3.95 us  [the longest x3 2.74 us: tn(): lax.dot_general(left, right, (((0,), (0,)), ((), ())), preferred_element_...]
    ppermute x0 -> x45, waiting for transfers between devices: none -> 243 us  [exchange(): got = lax.ppermute(sent, ('rows', 'var'), pairs)]
    convert_element_type x25 -> x39, other arithmetic: 185 us -> 49.6 us  [the longest x36 48.6 us: exchange(): return (kept.astype(F32) + got.astype(F32)).astype(BF16)]
    mul x36 -> x0, other arithmetic: 127 us -> none  [the longest x8 124 us: window_mean(): running = running + shift_rows(values, offset) * inside[..., None]]
    reshape x15 -> x10, local copies, waits for them, and re-layouts: 122 us -> 8.76 us  [the longest x4 3.82 us: scatter_sum(): return parts.transpose(0, 2, 1).reshape(shape)]
    transpose x9 -> x0, local copies, waits for them, and re-layouts: 55.4 us -> none  [scatter_sum(): pieces = pieces.transpose(0, 2, 1, 3).reshape(-1, width // column_shards)]
  transfers between devices with their start and end apart: 11 -> 47, of which waited for: 5 -> 28; matrix products, arithmetic and copies ran while one was open for 52% -> 17% of each run, Pallas kernels for 0% -> 22%
where the time goes in v2:
time: 800 us; the launch traced here: 790 us
  Pallas kernels  285 us (36%)
  waiting for transfers between devices  243 us (30%)
  local copies, waits for them, and re-layouts  85.6 us (11%)
  blocking collectives  59 us (7%)
  other arithmetic  56.2 us (7%)
  starting transfers between devices  55.8 us (7%)
    ppermute x45, waiting for transfers between devices, exchange(): got = lax.ppermute(sent, ('rows', 'var'), pairs)  243 us
    pallas_call x1, Pallas kernels, tail(): pl.pallas_call(tail_kernel, grid=(positions // length,), in_specs=[by_tap...  112 us
    pallas_call x2, Pallas kernels, scale_forward(): pl.pallas_call(functools.partial(scale_forward_kernel, stride, taps, step...  48.9 us
    convert_element_type x36, other arithmetic, exchange(): return (kept.astype(F32) + got.astype(F32)).astype(BF16)  48.6 us
    psum x1, blocking collectives, body(): lax.psum((embed_grad, head_grad, gains_grad), ('rows', 'var'))  48.1 us
    ppermute x45, starting transfers between devices, exchange(): got = lax.ppermute(sent, ('rows', 'var'), pairs)  47.9 us
    pallas_call x2, Pallas kernels, scale_backward(): pl.pallas_call(functools.partial(scale_backward_kernel, stride, taps, ste...  47.7 us
    squeeze x42, local copies, waits for them, and re-layouts, exchange(): sent = lax.dynamic_index_in_dim(parts, 1 - mine, axis, keepdims=False)  38.7 us
  transfers between devices with their start and end apart: 47, of which 28 were waited for; matrix products, arithmetic and copies ran while one was open for 17% of the time, Pallas kernels for 22%

profile of v2, /device:TPU:0, one launch (start us, length us, event | category | flops | bytes accessed | tf_op | source)
XLA Modules:
  0.0 790.5 jit_solution(17789649678575268139)
XLA Ops:
  22.7 5.6 all_gather.7
  35.3 9.8 %front.1 = (f32[3072,512]{1,0:T(8,128)}, f32[4,3072,128]{2,1,0:T(8,128)}) custom-call(bf16[3072,32]{1,0:T(8,128)(2,1)} %bitcast.502, f32[3072,8]{1,0:T(8,128)} %copy.229.flags_ref, f32[4,1,768]{2,1,0:T(1,128)} %reshape.447.marks_ref, bf16[96,512]{1,0:T(8,128)(2,1)} %pad_maximum_fusion.1.weight_ref), custom_call_target="tpu_custom_call" | custom-call | tf_op jit(solution)/shard_map/front/pallas_call | solution.py:113
  45.2 25.0 %scale_forward.3 = (bf16[16,192,512]{2,1,0:T(8,128)(2,1)}, f32[192,512]{1,0:T(8,128)}, f32[192,512]{1,0:T(8,128)}, bf16[192,512]{1,0:T(8,128)(2,1)}) custom-call(f32[4,3072,128]{2,1,0:T(8,128)} %get-tuple-element.43.seasonal_ref, bf16[8192,512]{1,0:T(8,128)(2,1)} %down_ref.7, bf16[6144,512]{1,0:T(8,128)(2,1)} %iso_ref.7, bf16[512,8192]{1,0:T(8,128)(2,1)} %up_ref.7, ...), custom_call_target="tpu_custom_call" | custom-call | tf_op jit(solution)/shard_map/scale_forward/pallas_call | solution.py:198
  70.2 23.9 %scale_forward.2 = (bf16[12,256,512]{2,1,0:T(8,128)(2,1)}, f32[256,512]{1,0:T(8,128)}, f32[256,512]{1,0:T(8,128)}, bf16[256,512]{1,0:T(8,128)(2,1)}) custom-call(f32[4,3072,128]{2,1,0:T(8,128)} %get-tuple-element.43.seasonal_ref, bf16[6144,512]{1,0:T(8,128)(2,1)} %down_ref.6, bf16[8192,512]{1,0:T(8,128)(2,1)} %iso_ref.6, bf16[512,6144]{1,0:T(8,128)(2,1)} %up_ref.6, ...), custom_call_target="tpu_custom_call" | custom-call | tf_op jit(solution)/shard_map/scale_forward/pallas_call | solution.py:198
  96.0 111.8 %tail.1 = (f32[3072,32]{1,0:T(8,128)}, bf16[12,256,512]{2,1,0:T(8,128)(2,1)}, bf16[16,192,512]{2,1,0:T(8,128)(2,1)}, f32[3072,512]{1,0:T(8,128)}, bf16[8,512,128...) custom-call(bf16[12,256,512]{2,1,0:T(8,128)(2,1)} %get-tuple-element, ...), custom_call_target="tpu_custom_call" | custom-call | tf_op jit(solution)/shard_map/tail/pallas_call | solution.py:351
  216.7 8.7 %up_grad.3 = bf16[16,512,512]{2,1,0:T(8,128)(2,1)} custom-call(bf16[192,512]{1,0:T(8,128)(2,1)} %get-tuple-element.65.joined_ref, bf16[16,192,512]{2,1,0:T(8,128)(2,1)} %get-tuple-element.53.pre_ref), custom_call_target="tpu_custom_call" | custom-call | tf_op jit(solution)/shard_map/up_grad/pallas_call | solution.py:493
  230.2 24.5 %scale_backward.3 = (bf16[192,512]{1,0:T(8,128)(2,1)}, bf16[192,512]{1,0:T(8,128)(2,1)}, bf16[16,192,512]{2,1,0:T(8,128)(2,1)}, f32[1,512]{1,0:T(1,128)}) custom-call(bf16[16,192,512]{2,1,0:T(8,128)(2,1)} %get-tuple-element.53.pre_ref, bf16[512,8192]{1,0:T(8,128)(2,1)} %up_ref.7, bf16[6144,512]{1,0:T(8,128)(2,1)} %iso_ref.7, bf16[8192,512]{1,0:T(8,128)(2,1)} %down_ref.7, ...), custom_call_target="tpu_custom_call" | custom-call | tf_op jit(solution)/shard_map/scale_backward/pallas_call | solution.py:449
  254.8 6.7 iso_grad.3
  261.4 10.6 %down_grad.3 = bf16[32,512,256]{2,1,0:T(8,128)(2,1)} custom-call(bf16[192,512]{1,0:T(8,128)(2,1)} %get-tuple-element.63.pre_ref, f32[4,3072,128]{2,1,0:T(8,128)} %get-tuple-element.43.seasonal_ref), custom_call_target="tpu_custom_call" | custom-call | tf_op jit(solution)/shard_map/down_grad/pallas_call | solution.py:565
  276.6 7.0 up_grad.2
  287.6 23.1 %scale_backward.2 = (bf16[256,512]{1,0:T(8,128)(2,1)}, bf16[256,512]{1,0:T(8,128)(2,1)}, bf16[12,256,512]{2,1,0:T(8,128)(2,1)}, f32[1,512]{1,0:T(1,128)}) custom-call(bf16[12,256,512]{2,1,0:T(8,128)(2,1)} %get-tuple-element.49.pre_ref, bf16[512,6144]{1,0:T(8,128)(2,1)} %up_ref.6, bf16[8192,512]{1,0:T(8,128)(2,1)} %iso_ref.6, bf16[6144,512]{1,0:T(8,128)(2,1)} %down_ref.6, ...), custom_call_target="tpu_custom_call" | custom-call | tf_op jit(solution)/shard_map/scale_backward/pallas_call | solution.py:449
  310.8 8.8 %iso_grad.2 = bf16[32,512,256]{2,1,0:T(8,128)(2,1)} custom-call(bf16[256,512]{1,0:T(8,128)(2,1)} %get-tuple-element.61.pre_ref, f32[256,512]{1,0:T(8,128)} %get-tuple-element.50.act_ref, s32[256,1]{1,0:T(8,128)} %reshape.549.since_ref), custom_call_target="tpu_custom_call" | custom-call | tf_op jit(solution)/shard_map/iso_grad/pallas_call | solution.py:533
  324.2 7.9 %down_grad.2 = bf16[24,512,256]{2,1,0:T(8,128)(2,1)} custom-call(bf16[256,512]{1,0:T(8,128)(2,1)} %get-tuple-element.60.pre_ref, f32[4,3072,128]{2,1,0:T(8,128)} %get-tuple-element.43.seasonal_ref), custom_call_target="tpu_custom_call" | custom-call | tf_op jit(solution)/shard_map/down_grad/pallas_call | solution.py:565
  336.1 16.8 %back.1 = (f32[3072,32]{1,0:T(8,128)}, f32[96,512]{1,0:T(8,128)}) custom-call(f32[3072,512]{1,0:T(8,128)} %get-tuple-element.48.sres_ref, bf16[12,256,512]{2,1,0:T(8,128)(2,1)} %get-tuple-element.52.block_a_ref, bf16[16,192,512]{2,1,0:T(8,128)(2,1)} %get-tuple-element.56.block_b_ref, bf16[3072,32]{1,0:T(8,128)(2,1)} %copy.234.cot_ref, ...), custom_call_target="tpu_custom_call" | custom-call | tf_op jit(solution)/shard_map/back/pallas_call | solution.py:630
  377.8 6.0 collective-permute-done.31
  397.7 9.1 %collective-permute-done.41 = bf16[2,2,2,1,128,256]{4,5,0,1,3,2:T(8,128)(2,1)S(1)} collective-permute-done((bf16[2,2,2,1,128,256]{4,5,0,1,3,2:T(8,128)(2,1)S(1)}, bf16[2,2,2,1,128,256]{4,5,0,1,3,2:T(8,128)(2,1)S(1)}, u32[]{:S(2)}, u32[]{:S(2)}) %collective-permute-start.41) | collective-permute-done | bytes 524320 | tf_op jit(solution)/shard_map/ppermute | solution.py:714
  411.6 5.6 collective-permute-done.42
  447.0 48.1 %all-reduce.42 = (f32[8,12,64]{2,0,1:T(8,128)S(1)}, f32[8,64,4]{1,2,0:T(4,128)S(1)}, f32[3,512]{1,0:T(4,128)}) all-reduce(f32[8,12,64]{2,0,1:T(8,128)S(1)} %pad_maximum_fusion.3, f32[8,64,4]{1,2,0:T(4,128)S(1)} %constant_dynamic-update-slice_fusion, f32[3,512]{1,0:T(4,128)S(1)} %pad_maximum_fusion.4), channel_id=1, replica_groups=mesh['rows'=8,'var'=4] {'rows','var'}, use_global_device_ids=true, to_apply=%region_0.1 | all-reduce | flops 9728 | bytes 77824 | tf_op jit(solution)/shard_map/psum | solution.py:827
  529.6 6.3 fusion.1
  549.2 29.6 %collective-permute-done.11 = bf16[3,2,2,2,64,512]{5,4,3,2,1,0:T(8,128)(2,1)} collective-permute-done((bf16[3,2,2,2,64,512]{5,4,3,2,1,0:T(8,128)(2,1)}, bf16[3,2,2,2,64,512]{5,4,3,2,1,0:T(8,128)(2,1)}, u32[]{:S(2)}, u32[]{:S(2)}) %collective-permute-start.11) | collective-permute-done | bytes 1572896 | tf_op jit(solution)/shard_map/ppermute | solution.py:714
  583.0 27.4 %collective-permute-done.1 = bf16[2,2,2,3,128,256]{5,4,3,2,1,0:T(8,128)(2,1)} collective-permute-done((bf16[2,2,2,3,128,256]{5,4,3,2,1,0:T(8,128)(2,1)}, bf16[2,2,2,3,128,256]{5,4,3,2,1,0:T(8,128)(2,1)}, u32[]{:S(2)}, u32[]{:S(2)}) %collective-permute-start.1) | collective-permute-done | bytes 1572896 | tf_op jit(solution)/shard_map/ppermute | solution.py:714
  614.0 25.0 %collective-permute-done.22 = bf16[2,2,3,128,256]{4,3,2,1,0:T(8,128)(2,1)S(1)} collective-permute-done((bf16[2,2,3,128,256]{4,3,2,1,0:T(8,128)(2,1)S(1)}, bf16[2,2,3,128,256]{4,3,2,1,0:T(8,128)(2,1)S(1)}, u32[]{:S(2)}, u32[]{:S(2)}) %collective-permute-start.22) | collective-permute-done | bytes 786464 | tf_op jit(solution)/shard_map/ppermute | solution.py:714
  640.6 15.2 %collective-permute-done.12 = bf16[3,2,2,64,512]{4,3,2,1,0:T(8,128)(2,1)S(1)} collective-permute-done((bf16[3,2,2,64,512]{4,3,2,1,0:T(8,128)(2,1)S(1)}, bf16[3,2,2,64,512]{4,3,2,1,0:T(8,128)(2,1)S(1)}, u32[]{:S(2)}, u32[]{:S(2)}) %collective-permute-start.12) | collective-permute-done | bytes 786464 | tf_op jit(solution)/shard_map/ppermute | solution.py:714
  656.1 16.6 %collective-permute-done.2 = bf16[2,2,3,128,256]{4,3,2,1,0:T(8,128)(2,1)S(1)} collective-permute-done((bf16[2,2,3,128,256]{4,3,2,1,0:T(8,128)(2,1)S(1)}, bf16[2,2,3,128,256]{4,3,2,1,0:T(8,128)(2,1)S(1)}, u32[]{:S(2)}, u32[]{:S(2)}) %collective-permute-start.2) | collective-permute-done | bytes 786464 | tf_op jit(solution)/shard_map/ppermute | solution.py:714
  675.2 8.8 %collective-permute-done.13 = bf16[3,2,64,512]{3,2,1,0:T(8,128)(2,1)S(1)} collective-permute-done((bf16[3,2,64,512]{3,2,1,0:T(8,128)(2,1)S(1)}, bf16[3,2,64,512]{3,2,1,0:T(8,128)(2,1)S(1)}, u32[]{:S(2)}, u32[]{:S(2)}) %collective-permute-start.13) | collective-permute-done | bytes 393248 | tf_op jit(solution)/shard_map/ppermute | solution.py:714
  684.5 7.0 collective-permute-done.3
  706.0 8.6 %collective-permute-done.6 = bf16[2,2,4,2,128,256]{5,4,3,2,1,0:T(8,128)(2,1)S(1)} collective-permute-done((bf16[2,2,4,2,128,256]{5,4,3,2,1,0:T(8,128)(2,1)S(1)}, bf16[2,2,4,2,128,256]{5,4,3,2,1,0:T(8,128)(2,1)S(1)}, u32[]{:S(2)}, u32[]{:S(2)}) %collective-permute-start.6) | collective-permute-done | bytes 2097184 | tf_op jit(solution)/shard_map/ppermute | solution.py:714
  720.9 5.9 collective-permute-done.27
  733.3 13.9 %collective-permute-done.17 = bf16[2,2,4,128,256]{4,3,2,1,0:T(8,128)(2,1)} collective-permute-done((bf16[2,2,4,128,256]{4,3,2,1,0:T(8,128)(2,1)}, bf16[2,2,4,128,256]{4,3,2,1,0:T(8,128)(2,1)}, u32[]{:S(2)}, u32[]{:S(2)}) %collective-permute-start.17) | collective-permute-done | bytes 1048608 | tf_op jit(solution)/shard_map/ppermute | solution.py:714
  748.8 9.5 %collective-permute-done.7 = bf16[2,2,4,128,256]{4,3,2,1,0:T(8,128)(2,1)} collective-permute-done((bf16[2,2,4,128,256]{4,3,2,1,0:T(8,128)(2,1)}, bf16[2,2,4,128,256]{4,3,2,1,0:T(8,128)(2,1)}, u32[]{:S(2)}, u32[]{:S(2)}) %collective-permute-start.7) | collective-permute-done | bytes 1048608 | tf_op jit(solution)/shard_map/ppermute | solution.py:714
  762.4 6.7 collective-permute-done.18
  776.3 9.9 %collective-permute-done.19 = bf16[4,128,256]{2,1,0:T(8,128)(2,1)S(1)} collective-permute-done((bf16[4,128,256]{2,1,0:T(8,128)(2,1)S(1)}, bf16[4,128,256]{2,1,0:T(8,128)(2,1)S(1)}, u32[]{:S(2)}, u32[]{:S(2)}) %collective-permute-start.19) | collective-permute-done | bytes 262176 | tf_op jit(solution)/shard_map/ppermute | solution.py:714
  (324 shorter events, 238.9 us)
Async XLA Ops:
  0.7 94.1 %all-to-all-start = ((bf16[16,768,8]{1,2,0:T(8,128)(2,1)}), bf16[16,768,8]{1,2,0:T(8,128)(2,1)S(1)}, u32[]{:S(2)}, u32[]{:S(2)}) async-start(bf16[16,768,8]{1,2,0:T(8,128)(2,1)} %param.31), calls=%async_computation | async-start | bytes 393216 | tf_op jit(solution)/shard_map/all_to_all | solution.py:772
  210.9 178.3 %collective-permute-start.40 = (bf16[2,2,2,1,2,128,256]{5,6,0,1,2,4,3:T(8,128)(2,1)}, bf16[2,2,2,1,2,128,256]{5,6,0,1,2,4,3:T(8,128)(2,1)}, u32[]{:S(2)}, u32[]{:S(2)}) collective-permute-start(bf16[2,2,2,1,2,128,256]{5,6,0,1,2,4,3:T(8,128)(2,1)} %bitcast.509), channel_id=1, source_target_pairs={{0,1},{1,0},{2,3},{3,2},{4,5},{5,4},{6,7},{7,6},{8,9},{9,8},{10,11... | collective-permute-start | bytes 3145736 | tf_op jit(solution)/shard_map/ppermute | solution.py:714
  214.8 177.9 %collective-permute-start.35 = (bf16[2,1,2,2,2,64,512]{6,5,2,3,0,4,1:T(8,128)(2,1)}, bf16[2,1,2,2,2,64,512]{6,5,2,3,0,4,1:T(8,128)(2,1)}, u32[]{:S(2)}, u32[]{:S(2)}) collective-permute-start(bf16[2,1,2,2,2,64,512]{6,5,2,3,0,4,1:T(8,128)(2,1)} %bitcast.451), channel_id=1, source_target_pairs={{0,1},{1,0},{2,3},{3,2},{4,5},{5,4},{6,7},{7,6},{8,9},{9,8},{10,11... | collective-permute-start | bytes 3145736 | tf_op jit(solution)/shard_map/ppermute | solution.py:714
  216.1 157.9 %collective-permute-start.30 = (bf16[2,2,2,1,2,128,128]{5,6,0,1,2,4,3:T(8,128)(2,1)}, bf16[2,2,2,1,2,128,128]{5,6,0,1,2,4,3:T(8,128)(2,1)}, u32[]{:S(2)}, u32[]{:S(2)}) collective-permute-start(bf16[2,2,2,1,2,128,128]{5,6,0,1,2,4,3:T(8,128)(2,1)} %bitcast.529), channel_id=1, source_target_pairs={{0,1},{1,0},{2,3},{3,2},{4,5},{5,4},{6,7},{7,6},{8,9},{9,8},{10,11... | collective-permute-start | bytes 1572872 | tf_op jit(solution)/shard_map/ppermute | solution.py:714
  230.1 290.2 %collective-permute-start.25 = (bf16[2,4,2,2,2,64,512]{6,5,4,3,2,1,0:T(8,128)(2,1)}, bf16[2,4,2,2,2,64,512]{6,5,4,3,2,1,0:T(8,128)(2,1)}, u32[]{:S(2)}, u32[]{:S(2)}) collective-permute-start(bf16[2,4,2,2,2,64,512]{6,5,4,3,2,1,0:T(8,128)(2,1)} %dynamic-slice_bitcast_fusion), channel_id=1, source_target_pairs={{0,1},{1,0},{2,3},{3,2},{4,5},{5,4},{6,7},{7,6},{8,9},{9,8},{10,11... | collective-permute-start | bytes 12582920 | tf_op jit(solution)/shard_map/ppermute | solution.py:714
  360.3 136.0 %all-to-all-start.1 = ((f32[2,4,768,32]{2,1,0,3:T(4,128)}), f32[2,4,768,32]{2,1,0,3:T(4,128)S(1)}, u32[]{:S(2)}, u32[]{:S(2)}) async-start(f32[2,4,768,32]{2,1,0,3:T(4,128)} %pad_maximum_fusion), calls=%async_computation.1 | async-start | bytes 1572864 | tf_op jit(solution)/shard_map/all_to_all | solution.py:826
  368.4 78.0 %collective-permute-start.20 = (bf16[2,2,2,3,2,128,256]{6,5,4,3,2,1,0:T(8,128)(2,1)}, bf16[2,2,2,3,2,128,256]{6,5,4,3,2,1,0:T(8,128)(2,1)}, u32[]{:S(2)}, u32[]{:S(2)}) collective-permute-start(bf16[2,2,2,3,2,128,256]{6,5,4,3,2,1,0:T(8,128)(2,1)} %dynamic-slice_bitcast_fusion.3), channel_id=1, source_target_pairs={{0,1},{1,0},{2,3},{3,2},{4,5},{5,4},{6,7},{7,6},{8,9},{9,8},{10,11... | collective-permute-start | bytes 9437192 | tf_op jit(solution)/shard_map/ppermute | solution.py:714
  389.0 118.3 %collective-permute-start.10 = (bf16[2,3,2,2,2,64,512]{6,5,4,3,2,1,0:T(8,128)(2,1)}, bf16[2,3,2,2,2,64,512]{6,5,4,3,2,1,0:T(8,128)(2,1)}, u32[]{:S(2)}, u32[]{:S(2)}) collective-permute-start(bf16[2,3,2,2,2,64,512]{6,5,4,3,2,1,0:T(8,128)(2,1)} %dynamic-slice_bitcast_fusion.4), channel_id=1, source_target_pairs={{0,1},{1,0},{2,3},{3,2},{4,5},{5,4},{6,7},{7,6},{8,9},{9,8},{10,11... | collective-permute-start | bytes 9437192 | tf_op jit(solution)/shard_map/ppermute | solution.py:714
  406.8 30.6 %collective-permute-start.34 = (bf16[1,128,128]{1,2,0:T(8,128)(2,1)S(1)}, bf16[1,128,128]{1,2,0:T(8,128)(2,1)S(1)}, u32[]{:S(2)}, u32[]{:S(2)}) collective-permute-start(bf16[1,128,128]{1,2,0:T(8,128)(2,1)S(1)} %dynamic-slice_bitcast_fusion.41), channel_id=1, source_target_pairs={{0,16},{1,17},{2,18},{3,19},{4,20},{5,21},{6,22},{7,23},{8,24},{9,... | collective-permute-start | bytes 98312 | tf_op jit(solution)/shard_map/ppermute | solution.py:714
  437.5 76.6 %collective-permute-start = (bf16[2,2,2,3,2,128,256]{6,5,4,3,2,1,0:T(8,128)(2,1)}, bf16[2,2,2,3,2,128,256]{6,5,4,3,2,1,0:T(8,128)(2,1)}, u32[]{:S(2)}, u32[]{:S(2)}) collective-permute-start(bf16[2,2,2,3,2,128,256]{6,5,4,3,2,1,0:T(8,128)(2,1)} %dynamic-slice_bitcast_fusion.5), channel_id=1, source_target_pairs={{0,1},{1,0},{2,3},{3,2},{4,5},{5,4},{6,7},{7,6},{8,9},{9,8},{10,11... | collective-permute-start | bytes 9437192 | tf_op jit(solution)/shard_map/ppermute | solution.py:714
  446.1 82.3 %collective-permute-start.15 = (bf16[2,2,2,4,2,128,256]{6,5,4,3,2,1,0:T(8,128)(2,1)}, bf16[2,2,2,4,2,128,256]{6,5,4,3,2,1,0:T(8,128)(2,1)}, u32[]{:S(2)}, u32[]{:S(2)}) collective-permute-start(bf16[2,2,2,4,2,128,256]{6,5,4,3,2,1,0:T(8,128)(2,1)} %dynamic-slice_bitcast_fusion.1), channel_id=1, source_target_pairs={{0,1},{1,0},{2,3},{3,2},{4,5},{5,4},{6,7},{7,6},{8,9},{9,8},{10,11... | collective-permute-start | bytes 12582920 | tf_op jit(solution)/shard_map/ppermute | solution.py:714
  446.4 92.7 %collective-permute-start.5 = (bf16[2,2,2,4,2,128,256]{6,5,4,3,2,1,0:T(8,128)(2,1)}, bf16[2,2,2,4,2,128,256]{6,5,4,3,2,1,0:T(8,128)(2,1)}, u32[]{:S(2)}, u32[]{:S(2)}) collective-permute-start(bf16[2,2,2,4,2,128,256]{6,5,4,3,2,1,0:T(8,128)(2,1)} %dynamic-slice_bitcast_fusion.2), channel_id=1, source_target_pairs={{0,1},{1,0},{2,3},{3,2},{4,5},{5,4},{6,7},{7,6},{8,9},{9,8},{10,11... | collective-permute-start | bytes 12582920 | tf_op jit(solution)/shard_map/ppermute | solution.py:714
  507.3 37.8 %collective-permute-start.21 = (bf16[2,2,2,3,128,256]{5,4,3,2,1,0:T(8,128)(2,1)}, bf16[2,2,2,3,128,256]{5,4,3,2,1,0:T(8,128)(2,1)}, u32[]{:S(2)}, u32[]{:S(2)}) collective-permute-start(bf16[2,2,2,3,128,256]{5,4,3,2,1,0:T(8,128)(2,1)} %dynamic-slice_bitcast_fusion.9), channel_id=1, source_target_pairs={{0,2},{1,3},{2,0},{3,1},{4,6},{5,7},{6,4},{7,5},{8,10},{9,11},{10,... | collective-permute-start | bytes 4718600 | tf_op jit(solution)/shard_map/ppermute | solution.py:714
  514.0 64.8 %collective-permute-start.11 = (bf16[3,2,2,2,64,512]{5,4,3,2,1,0:T(8,128)(2,1)}, bf16[3,2,2,2,64,512]{5,4,3,2,1,0:T(8,128)(2,1)}, u32[]{:S(2)}, u32[]{:S(2)}) collective-permute-start(bf16[3,2,2,2,64,512]{5,4,3,2,1,0:T(8,128)(2,1)} %dynamic-slice_bitcast_fusion.10), channel_id=1, source_target_pairs={{0,2},{1,3},{2,0},{3,1},{4,6},{5,7},{6,4},{7,5},{8,10},{9,11},{10,... | collective-permute-start | bytes 4718600 | tf_op jit(solution)/shard_map/ppermute | solution.py:714
  521.4 89.0 %collective-permute-start.1 = (bf16[2,2,2,3,128,256]{5,4,3,2,1,0:T(8,128)(2,1)}, bf16[2,2,2,3,128,256]{5,4,3,2,1,0:T(8,128)(2,1)}, u32[]{:S(2)}, u32[]{:S(2)}) collective-permute-start(bf16[2,2,2,3,128,256]{5,4,3,2,1,0:T(8,128)(2,1)} %dynamic-slice_bitcast_fusion.11), channel_id=1, source_target_pairs={{0,2},{1,3},{2,0},{3,1},{4,6},{5,7},{6,4},{7,5},{8,10},{9,11},{10,... | collective-permute-start | bytes 4718600 | tf_op jit(solution)/shard_map/ppermute | solution.py:714
  528.4 168.3 %collective-permute-start.26 = (bf16[2,4,2,2,64,512]{5,4,3,2,1,0:T(8,128)(2,1)}, bf16[2,4,2,2,64,512]{5,4,3,2,1,0:T(8,128)(2,1)}, u32[]{:S(2)}, u32[]{:S(2)}) collective-permute-start(bf16[2,4,2,2,64,512]{5,4,3,2,1,0:T(8,128)(2,1)} %dynamic-slice_bitcast_fusion.6), channel_id=1, source_target_pairs={{0,4},{1,5},{2,6},{3,7},{4,0},{5,1},{6,2},{7,3},{8,12},{9,13},{10,... | collective-permute-start | bytes 6291464 | tf_op jit(solution)/shard_map/ppermute | solution.py:714
  539.1 161.6 %collective-permute-start.16 = (bf16[2,2,4,2,128,256]{5,4,3,2,1,0:T(8,128)(2,1)}, bf16[2,2,4,2,128,256]{5,4,3,2,1,0:T(8,128)(2,1)}, u32[]{:S(2)}, u32[]{:S(2)}) collective-permute-start(bf16[2,2,4,2,128,256]{5,4,3,2,1,0:T(8,128)(2,1)} %dynamic-slice_bitcast_fusion.7), channel_id=1, source_target_pairs={{0,4},{1,5},{2,6},{3,7},{4,0},{5,1},{6,2},{7,3},{8,12},{9,13},{10,... | collective-permute-start | bytes 6291464 | tf_op jit(solution)/shard_map/ppermute | solution.py:714
  547.2 91.8 %collective-permute-start.22 = (bf16[2,2,3,128,256]{4,3,2,1,0:T(8,128)(2,1)S(1)}, bf16[2,2,3,128,256]{4,3,2,1,0:T(8,128)(2,1)S(1)}, u32[]{:S(2)}, u32[]{:S(2)}) collective-permute-start(bf16[2,2,3,128,256]{4,3,2,1,0:T(8,128)(2,1)S(1)} %dynamic-slice_bitcast_fusion.15), channel_id=1, source_target_pairs={{0,4},{1,5},{2,6},{3,7},{4,0},{5,1},{6,2},{7,3},{8,12},{9,13},{10,... | collective-permute-start | bytes 2359304 | tf_op jit(solution)/shard_map/ppermute | solution.py:714
  580.9 74.9 %collective-permute-start.12 = (bf16[3,2,2,64,512]{4,3,2,1,0:T(8,128)(2,1)S(1)}, bf16[3,2,2,64,512]{4,3,2,1,0:T(8,128)(2,1)S(1)}, u32[]{:S(2)}, u32[]{:S(2)}) collective-permute-start(bf16[3,2,2,64,512]{4,3,2,1,0:T(8,128)(2,1)S(1)} %dynamic-slice_bitcast_fusion.16), channel_id=1, source_target_pairs={{0,4},{1,5},{2,6},{3,7},{4,0},{5,1},{6,2},{7,3},{8,12},{9,13},{10,... | collective-permute-start | bytes 2359304 | tf_op jit(solution)/shard_map/ppermute | solution.py:714
  612.3 60.3 %collective-permute-start.2 = (bf16[2,2,3,128,256]{4,3,2,1,0:T(8,128)(2,1)S(1)}, bf16[2,2,3,128,256]{4,3,2,1,0:T(8,128)(2,1)S(1)}, u32[]{:S(2)}, u32[]{:S(2)}) collective-permute-start(bf16[2,2,3,128,256]{4,3,2,1,0:T(8,128)(2,1)S(1)} %dynamic-slice_bitcast_fusion.17), channel_id=1, source_target_pairs={{0,4},{1,5},{2,6},{3,7},{4,0},{5,1},{6,2},{7,3},{8,12},{9,13},{10,... | collective-permute-start | bytes 2359304 | tf_op jit(solution)/shard_map/ppermute | solution.py:714
  638.9 75.6 %collective-permute-start.6 = (bf16[2,2,4,2,128,256]{5,4,3,2,1,0:T(8,128)(2,1)S(1)}, bf16[2,2,4,2,128,256]{5,4,3,2,1,0:T(8,128)(2,1)S(1)}, u32[]{:S(2)}, u32[]{:S(2)}) collective-permute-start(bf16[2,2,4,2,128,256]{5,4,3,2,1,0:T(8,128)(2,1)S(1)} %dynamic-slice_bitcast_fusion.8), channel_id=1, source_target_pairs={{0,4},{1,5},{2,6},{3,7},{4,0},{5,1},{6,2},{7,3},{8,12},{9,13},{10,... | collective-permute-start | bytes 6291464 | tf_op jit(solution)/shard_map/ppermute | solution.py:714
  655.8 17.1 %collective-permute-start.23 = (bf16[2,3,128,256]{3,2,1,0:T(8,128)(2,1)S(1)}, bf16[2,3,128,256]{3,2,1,0:T(8,128)(2,1)S(1)}, u32[]{:S(2)}, u32[]{:S(2)}) collective-permute-start(bf16[2,3,128,256]{3,2,1,0:T(8,128)(2,1)S(1)} %dynamic-slice_bitcast_fusion.23), channel_id=1, source_target_pairs={{0,8},{1,9},{2,10},{3,11},{4,12},{5,13},{6,14},{7,15},{8,0},{9,1},... | collective-permute-start | bytes 1179656 | tf_op jit(solution)/shard_map/ppermute | solution.py:714
  672.9 18.6 %collective-permute-start.3 = (bf16[2,3,128,256]{3,2,1,0:T(8,128)(2,1)S(1)}, bf16[2,3,128,256]{3,2,1,0:T(8,128)(2,1)S(1)}, u32[]{:S(2)}, u32[]{:S(2)}) collective-permute-start(bf16[2,3,128,256]{3,2,1,0:T(8,128)(2,1)S(1)} %dynamic-slice_bitcast_fusion.25), channel_id=1, source_target_pairs={{0,8},{1,9},{2,10},{3,11},{4,12},{5,13},{6,14},{7,15},{8,0},{9,1},... | collective-permute-start | bytes 1179656 | tf_op jit(solution)/shard_map/ppermute | solution.py:714
  691.5 25.7 %collective-permute-start.14 = (bf16[3,64,512]{2,1,0:T(8,128)(2,1)S(1)}, bf16[3,64,512]{2,1,0:T(8,128)(2,1)S(1)}, u32[]{:S(2)}, u32[]{:S(2)}) collective-permute-start(bf16[3,64,512]{2,1,0:T(8,128)(2,1)S(1)} %dynamic-slice_bitcast_fusion.33), channel_id=1, source_target_pairs={{0,16},{1,17},{2,18},{3,19},{4,20},{5,21},{6,22},{7,23},{8,24},{9,... | collective-permute-start | bytes 589832 | tf_op jit(solution)/shard_map/ppermute | solution.py:714
  696.7 22.3 %collective-permute-start.4 = (bf16[3,128,256]{2,1,0:T(8,128)(2,1)S(1)}, bf16[3,128,256]{2,1,0:T(8,128)(2,1)}, u32[]{:S(2)}, u32[]{:S(2)}) collective-permute-start(bf16[3,128,256]{2,1,0:T(8,128)(2,1)S(1)} %dynamic-slice_bitcast_fusion.34), channel_id=1, source_target_pairs={{0,16},{1,17},{2,18},{3,19},{4,20},{5,21},{6,22},{7,23},{8,24},{9,... | collective-permute-start | bytes 589832 | tf_op jit(solution)/shard_map/ppermute | solution.py:714
  700.4 26.3 %collective-permute-start.27 = (bf16[4,2,2,64,512]{4,3,2,1,0:T(8,128)(2,1)}, bf16[4,2,2,64,512]{4,3,2,1,0:T(8,128)(2,1)}, u32[]{:S(2)}, u32[]{:S(2)}) collective-permute-start(bf16[4,2,2,64,512]{4,3,2,1,0:T(8,128)(2,1)} %dynamic-slice_bitcast_fusion.12), channel_id=1, source_target_pairs={{0,2},{1,3},{2,0},{3,1},{4,6},{5,7},{6,4},{7,5},{8,10},{9,11},{10,... | collective-permute-start | bytes 3145736 | tf_op jit(solution)/shard_map/ppermute | solution.py:714
  704.2 42.9 %collective-permute-start.17 = (bf16[2,2,4,128,256]{4,3,2,1,0:T(8,128)(2,1)}, bf16[2,2,4,128,256]{4,3,2,1,0:T(8,128)(2,1)}, u32[]{:S(2)}, u32[]{:S(2)}) collective-permute-start(bf16[2,2,4,128,256]{4,3,2,1,0:T(8,128)(2,1)} %dynamic-slice_bitcast_fusion.13), channel_id=1, source_target_pairs={{0,2},{1,3},{2,0},{3,1},{4,6},{5,7},{6,4},{7,5},{8,10},{9,11},{10,... | collective-permute-start | bytes 3145736 | tf_op jit(solution)/shard_map/ppermute | solution.py:714
  716.5 41.9 %collective-permute-start.7 = (bf16[2,2,4,128,256]{4,3,2,1,0:T(8,128)(2,1)}, bf16[2,2,4,128,256]{4,3,2,1,0:T(8,128)(2,1)}, u32[]{:S(2)}, u32[]{:S(2)}) collective-permute-start(bf16[2,2,4,128,256]{4,3,2,1,0:T(8,128)(2,1)} %dynamic-slice_bitcast_fusion.14), channel_id=1, source_target_pairs={{0,2},{1,3},{2,0},{3,1},{4,6},{5,7},{6,4},{7,5},{8,10},{9,11},{10,... | collective-permute-start | bytes 3145736 | tf_op jit(solution)/shard_map/ppermute | solution.py:714
  728.7 31.4 %collective-permute-start.28 = (bf16[4,2,64,512]{3,2,1,0:T(8,128)(2,1)S(1)}, bf16[4,2,64,512]{3,2,1,0:T(8,128)(2,1)S(1)}, u32[]{:S(2)}, u32[]{:S(2)}) collective-permute-start(bf16[4,2,64,512]{3,2,1,0:T(8,128)(2,1)S(1)} %dynamic-slice_bitcast_fusion.20), channel_id=1, source_target_pairs={{0,8},{1,9},{2,10},{3,11},{4,12},{5,13},{6,14},{7,15},{8,0},{9,1},... | collective-permute-start | bytes 1572872 | tf_op jit(solution)/shard_map/ppermute | solution.py:714
  748.8 20.3 %collective-permute-start.18 = (bf16[2,4,128,256]{3,2,1,0:T(8,128)(2,1)S(1)}, bf16[2,4,128,256]{3,2,1,0:T(8,128)(2,1)S(1)}, u32[]{:S(2)}, u32[]{:S(2)}) collective-permute-start(bf16[2,4,128,256]{3,2,1,0:T(8,128)(2,1)S(1)} %dynamic-slice_bitcast_fusion.21), channel_id=1, source_target_pairs={{0,8},{1,9},{2,10},{3,11},{4,12},{5,13},{6,14},{7,15},{8,0},{9,1},... | collective-permute-start | bytes 1572872 | tf_op jit(solution)/shard_map/ppermute | solution.py:714
  760.3 15.1 %collective-permute-start.29 = (bf16[4,64,512]{2,1,0:T(8,128)(2,1)S(1)}, bf16[4,64,512]{2,1,0:T(8,128)(2,1)S(1)}, u32[]{:S(2)}, u32[]{:S(2)}) collective-permute-start(bf16[4,64,512]{2,1,0:T(8,128)(2,1)S(1)} %dynamic-slice_bitcast_fusion.29), channel_id=1, source_target_pairs={{0,16},{1,17},{2,18},{3,19},{4,20},{5,21},{6,22},{7,23},{8,24},{9,... | collective-permute-start | bytes 786440 | tf_op jit(solution)/shard_map/ppermute | solution.py:714
  769.3 16.9 %collective-permute-start.19 = (bf16[4,128,256]{2,1,0:T(8,128)(2,1)S(1)}, bf16[4,128,256]{2,1,0:T(8,128)(2,1)S(1)}, u32[]{:S(2)}, u32[]{:S(2)}) collective-permute-start(bf16[4,128,256]{2,1,0:T(8,128)(2,1)S(1)} %dynamic-slice_bitcast_fusion.30), channel_id=1, source_target_pairs={{0,16},{1,17},{2,18},{3,19},{4,20},{5,21},{6,22},{7,23},{8,24},{9,... | collective-permute-start | bytes 786440 | tf_op jit(solution)/shard_map/ppermute | solution.py:714
  (42 other events, 506.2 us)

commit v3 on v2

--- a/solution.py
+++ b/solution.py
@@ -31,6 +31,25 @@
 
 
 LANES = 128
+ROW_PARTS = 8
+COLUMN_PARTS = 4
+ORDERS = {
+    "x": ("x", "y", "near", "far"),
+    "y": ("y", "near", "x", "far"),
+    "z": ("near", "x", "y", "far"),
+}
+
+
+def part_at(order, r, x):
+    place = {"far": r // 4, "near": r // 2 % 2, "y": r % 2, "x": x}
+    return tuple(place[label] for label in ORDERS[order])
+
+
+def from_part_order(values, order):
+    labels = ("far", "near", "y", "x")
+    places = [ORDERS[order].index(label) for label in labels]
+    back = values.transpose(*places, *range(4, values.ndim))
+    return back.reshape(8, 2, *values.shape[4:])
 
 
 def picked(ref, rows):
@@ -228,9 +247,9 @@
 
 def tail_kernel(
     lifted_a_ref, lifted_b_ref, seasonal_ref, trend_ref, cot_ref,
-    merge_ref, ff_in_ref, ff_out_ref, head_ref, gains_ref,
+    merge_ref, ff_in_ref, ff_out_ref, head_ref, gains_ref, mine_ref,
     pred_ref, up_a_ref, up_b_ref, sres_ref,
-    merge_out, ff_in_out, ff_out_out, head_out, gains_out,
+    parts_out, head_out, gains_out,
     wide_a, wide_b, inner_all, pre_all, slope, mixed_all, outer_all, merged_all, stacked_all,
     result_all, merge_sum, ff_in_sum, ff_out_sum,
 ):
@@ -324,18 +343,38 @@
 
     @pl.when(row == pl.num_programs(0) - 1)
     def _():
-        for k in range(merge_out.shape[0]):
-            size = merge_out.shape[2]
-            merge_out[k] = merge_sum[:, k * size : (k + 1) * size].astype(BF16)
-        for k in range(ff_in_out.shape[0]):
-            size = ff_in_out.shape[2]
-            ff_in_out[k] = ff_in_sum[:, k * size : (k + 1) * size].astype(BF16)
-        for k in range(ff_out_out.shape[0]):
-            size = ff_out_out.shape[2]
-            ff_out_out[k] = ff_out_sum[:, k * size : (k + 1) * size].astype(BF16)
-
-
-def tail(lifted_a, lifted_b, seasonal, trend, cot, merge, ff_in, ff_out, head, gains, length):
+        height = width // ROW_PARTS
+        merge_size, out_size = 2 * width // ROW_PARTS, hidden // ROW_PARTS
+
+        def store(r, carry):
+            far, near, y = r // 4, r // 2 % 2, r % 2
+            for v in range(COLUMN_PARTS):
+                x, core = divmod(v, 2)
+                side = jnp.where(mine_ref[0] == core, 0, 1)
+                lines = slice(v * LANES, (v + 1) * LANES)
+                blocks = []
+                for p in range(merge_size // LANES):
+                    low = pl.multiple_of(r * merge_size + p * LANES, LANES)
+                    blocks.append(merge_sum[lines, pl.ds(low, LANES)])
+                for p in range(hidden // (COLUMN_PARTS * LANES)):
+                    low = v * (hidden // COLUMN_PARTS) + p * LANES
+                    there = pl.ds(pl.multiple_of(r * height, height), height)
+                    blocks.append(ff_in_sum[there, low : low + LANES])
+                for p in range(out_size // LANES):
+                    low = pl.multiple_of(r * out_size + p * LANES, LANES)
+                    blocks.append(ff_out_sum[lines, pl.ds(low, LANES)])
+                at = 0
+                for block in blocks:
+                    parts_out[side, near, x, y, far, at : at + block.shape[0], :] = block.astype(BF16)
+                    at += block.shape[0]
+            return carry
+
+        lax.fori_loop(0, ROW_PARTS, store, 0)
+
+
+def tail(
+    lifted_a, lifted_b, seasonal, trend, cot, merge, ff_in, ff_out, head, gains, mine, length
+):
     positions, width = trend.shape
     hidden = ff_in.shape[1]
     outs = cot.shape[1]
@@ -347,7 +386,8 @@
     kept = lambda shape: pl.BlockSpec(shape, lambda i: (0,) * len(shape))
     by_row = lambda size: pl.BlockSpec((length, size), lambda i: (i, 0))
     by_tap = lambda taps, per: pl.BlockSpec((taps, per, width), lambda i: (0, i, 0))
-    pieces = ((8, width, 128), (4, width, 512), (8, width, 256))
+    lines = width * (2 * width + 2 * hidden) // (ROW_PARTS * COLUMN_PARTS * LANES)
+    parts = (2, 2, 2, 2, 2, lines, LANES)
     return pl.pallas_call(
         tail_kernel,
         grid=(positions // length,),
@@ -355,18 +395,18 @@
             by_tap(stride_a, per_a), by_tap(stride_b, per_b),
             pl.BlockSpec((width // LANES, length, LANES), lambda i: (0, i, 0)), by_row(width),
             by_row(outs), fixed(merge.shape), fixed(ff_in.shape), fixed(ff_out.shape),
-            fixed(head.shape), fixed(gains.shape),
+            fixed(head.shape), fixed(gains.shape), pl.BlockSpec(memory_space=pltpu.SMEM),
         ],
         out_specs=[
             by_row(outs), by_tap(stride_a, per_a), by_tap(stride_b, per_b), by_row(width),
-            *[fixed(piece) for piece in pieces], kept((width, outs)), kept(gains.shape),
+            fixed(parts), kept((width, outs)), kept(gains.shape),
         ],
         out_shape=[
             jax.ShapeDtypeStruct((positions, outs), F32),
             jax.ShapeDtypeStruct(lifted_a.shape, BF16),
             jax.ShapeDtypeStruct(lifted_b.shape, BF16),
             jax.ShapeDtypeStruct((positions, width), F32),
-            *[jax.ShapeDtypeStruct(piece, BF16) for piece in pieces],
+            jax.ShapeDtypeStruct(parts, BF16),
             jax.ShapeDtypeStruct((width, outs), F32),
             jax.ShapeDtypeStruct(gains.shape, F32),
         ],
@@ -382,7 +422,7 @@
         ],
         compiler_params=pltpu.CompilerParams(vmem_limit_bytes=VMEM_LIMIT),
         name="tail",
-    )(lifted_a, lifted_b, seasonal, trend, cot, merge, ff_in, ff_out, head, gains)
+    )(lifted_a, lifted_b, seasonal, trend, cot, merge, ff_in, ff_out, head, gains, mine)
 
 
 def scale_backward_kernel(
@@ -478,100 +518,178 @@
     )(pre, up, iso, down, act, second, since, gains)
 
 
-def up_grad_kernel(joined_ref, pre_ref, out_ref, turned):
-    @pl.when(pl.program_id(0) == 0)
-    def _():
-        turned[...] = flip(joined_ref[...])
-
-    for k in range(pre_ref.shape[0]):
-        out_ref[k] = nn(turned[...], pre_ref[k]).astype(BF16)
-
-
-def up_grad(joined, pre):
-    stride, blocks, width = pre.shape
-    step_taps = 2
+def split_spec(grid, in_specs, out_specs, scratch):
+    return pltpu.PrefetchScalarGridSpec(
+        num_scalar_prefetch=1, grid=grid, in_specs=in_specs, out_specs=out_specs,
+        scratch_shapes=scratch,
+    )
+
+
+def up_grad_kernel(order, mine_ref, own_joined, other_joined, own_pre, other_pre, out_ref, turned):
+    blocks = own_joined.shape[0]
+
+    @pl.when(jnp.logical_and(pl.program_id(0) == 0, pl.program_id(1) == 0))
+    def _():
+        turned[:, :blocks] = flip(own_joined[...])
+        turned[:, blocks:] = flip(other_joined[...])
+
+    rows = jnp.concatenate([own_pre[0], other_pre[0]], axis=0)
+    product = nn(turned[...], rows).astype(BF16)
+    panels, height, _ = out_ref.shape[4:]
+    for r in range(ROW_PARTS):
+        for p in range(panels):
+            out_ref[(*part_at(order, r, 0), p)] = product[
+                r * height : (r + 1) * height, p * LANES : (p + 1) * LANES
+            ]
+
+
+def up_grad(mine, joined, pre, order):
+    stride, blocks, width = pre[0].shape
+    taps, panels = stride // COLUMN_PARTS, width // LANES
+    half = COLUMN_PARTS // 2
+    height = width // ROW_PARTS
+    sizes = tuple(1 if label == "x" else 2 for label in ORDERS[order])
+    joined_spec = pl.BlockSpec((blocks, width), lambda x, j, mine: (0, 0))
+    pre_spec = pl.BlockSpec(
+        (1, blocks, width), lambda x, j, mine: ((2 * x + mine[0]) * taps + j, 0, 0)
+    )
     return pl.pallas_call(
-        up_grad_kernel,
-        grid=(stride // step_taps,),
-        in_specs=[
-            pl.BlockSpec((blocks, width), lambda t: (0, 0)),
-            pl.BlockSpec((step_taps, blocks, width), lambda t: (t, 0, 0)),
-        ],
-        out_specs=pl.BlockSpec((step_taps, width, width), lambda t: (t, 0, 0)),
-        out_shape=jax.ShapeDtypeStruct((stride, width, width), BF16),
-        scratch_shapes=[pltpu.VMEM((width, blocks), BF16)],
+        functools.partial(up_grad_kernel, order),
+        grid_spec=split_spec(
+            (half, taps),
+            [joined_spec, joined_spec, pre_spec, pre_spec],
+            pl.BlockSpec(
+                (*sizes, panels, height, LANES),
+                lambda x, j, mine: (
+                    *[x if label == "x" else 0 for label in ORDERS[order]], j, 0, 0
+                ),
+            ),
+            [pltpu.VMEM((width, 2 * blocks), BF16)],
+        ),
+        out_shape=jax.ShapeDtypeStruct((2, 2, 2, 2, taps * panels, height, LANES), BF16),
         compiler_params=pltpu.CompilerParams(vmem_limit_bytes=VMEM_LIMIT),
         name="up_grad",
-    )(joined, pre)
-
-
-def store_halves(out_ref, k, product):
-    half = out_ref.shape[2]
-    out_ref[2 * k] = product[:, :half].astype(BF16)
-    out_ref[2 * k + 1] = product[:, half:].astype(BF16)
-
-
-def iso_grad_kernel(taps, step_taps, pre_ref, act_ref, since_ref, out_ref, turned):
+    )(mine, *joined, *pre)
+
+
+def turn_half(turned, own_pre, other_pre, mine):
+    blocks = own_pre.shape[0]
+    for side, pre_ref in enumerate((own_pre, other_pre)):
+        flipped = flip(pre_ref[...])
+        there = slice(side * blocks, (side + 1) * blocks)
+        for x in range(COLUMN_PARTS // 2):
+            even = flipped[2 * x * LANES : (2 * x + 1) * LANES, :]
+            odd = flipped[(2 * x + 1) * LANES : (2 * x + 2) * LANES, :]
+            lines = slice(x * LANES, (x + 1) * LANES)
+
+            @pl.when(mine == 0)
+            def _(even=even, lines=lines, there=there):
+                turned[lines, there] = even
+
+            @pl.when(mine == 1)
+            def _(odd=odd, lines=lines, there=there):
+                turned[lines, there] = odd
+
+
+def store_parts(orders, out_refs, k, product):
+    per_part = out_refs[0].shape[4]
+    panels = product.shape[1] // LANES
+    for p in range(panels):
+        r, at = divmod(panels * k + p, per_part * len(out_refs))
+        piece, at = divmod(at, per_part)
+        for x in range(COLUMN_PARTS // 2):
+            out_refs[piece][(*part_at(orders[piece], r, x), at)] = product[
+                x * LANES : (x + 1) * LANES, p * LANES : (p + 1) * LANES
+            ]
+
+
+GRAD_STEPS = 4
+
+
+def grad_output(taps, width, order, pieces):
+    per_part = taps * width // (ROW_PARTS * LANES * pieces)
+    sizes = tuple(1 if label in ("near", "far") else 2 for label in ORDERS[order])
+    spec = pl.BlockSpec(
+        (*sizes, per_part, LANES, LANES),
+        lambda t, mine: (
+            *[{"near": t % 2, "far": t // 2}.get(label, 0) for label in ORDERS[order]], 0, 0, 0
+        ),
+    )
+    return spec, jax.ShapeDtypeStruct((2, 2, 2, 2, per_part, LANES, LANES), BF16)
+
+
+def grad_call(kernel, name, taps, width, blocks, orders, arguments, mine):
+    whole = lambda shape: pl.BlockSpec(
+        shape, lambda t, mine: (0,) * len(shape), pipeline_mode=pl.Buffered(1)
+    )
+    specs, shapes = zip(*[grad_output(taps, width, order, len(orders)) for order in orders])
+    return pl.pallas_call(
+        kernel,
+        grid_spec=split_spec(
+            (GRAD_STEPS,), [whole(value.shape) for value in arguments], list(specs),
+            [pltpu.VMEM((width // 2, 2 * blocks), BF16)],
+        ),
+        out_shape=list(shapes),
+        compiler_params=pltpu.CompilerParams(vmem_limit_bytes=VMEM_LIMIT),
+        name=name,
+    )(mine, *arguments)
+
+
+def iso_grad_kernel(
+    taps, orders, mine_ref, own_pre, other_pre, own_act, other_act, own_since, other_since, *rest
+):
+    *out_refs, turned = rest
     step = pl.program_id(0)
-    blocks, width = act_ref.shape
+    step_taps = taps // GRAD_STEPS
 
     @pl.when(step == 0)
     def _():
-        turned[...] = flip(pre_ref[...])
+        turn_half(turned, own_pre, other_pre, mine_ref[0])
 
     for k in range(step_taps):
         back = taps - 1 - (step * step_taps + k)
-        rows = pltpu.roll(act_ref[...], back, 0)
-        rows = jnp.where(since_ref[...] >= back, rows, 0.0).astype(BF16)
-        store_halves(out_ref, k, nn(turned[...], rows))
-
-
-def iso_grad(pre, act, since, taps):
-    blocks, width = act.shape
-    step_taps = 2
-    whole = lambda shape: pl.BlockSpec(shape, lambda t: (0,) * len(shape))
-    return pl.pallas_call(
-        functools.partial(iso_grad_kernel, taps, step_taps),
-        grid=(taps // step_taps,),
-        in_specs=[whole(pre.shape), whole(act.shape), whole(since.shape)],
-        out_specs=pl.BlockSpec((2 * step_taps, width, width // 2), lambda t: (t, 0, 0)),
-        out_shape=jax.ShapeDtypeStruct((2 * taps, width, width // 2), BF16),
-        scratch_shapes=[pltpu.VMEM((width, blocks), BF16)],
-        compiler_params=pltpu.CompilerParams(vmem_limit_bytes=VMEM_LIMIT),
-        name="iso_grad",
-    )(pre, act, since)
-
-
-def down_grad_kernel(stride, step_taps, pre_ref, seasonal_ref, out_ref, turned):
+        rows = []
+        for act_ref, since_ref in ((own_act, own_since), (other_act, other_since)):
+            moved = pltpu.roll(act_ref[...], back, 0)
+            rows.append(jnp.where(since_ref[...] >= back, moved, 0.0).astype(BF16))
+        rows = jnp.concatenate(rows, axis=0)
+        store_parts(orders, out_refs, k, nn(turned[...], rows).astype(BF16))
+
+
+def iso_grad(mine, pre, act, since, taps, orders):
+    blocks, width = act[0].shape
+    kernel = functools.partial(iso_grad_kernel, taps, orders)
+    return grad_call(
+        kernel, "iso_grad", taps, width, blocks, orders, (*pre, *act, *since), mine
+    )
+
+
+def down_grad_kernel(
+    stride, orders, mine_ref, own_pre, other_pre, own_seasonal, other_seasonal, *rest
+):
+    *out_refs, turned = rest
     step = pl.program_id(0)
-    blocks = pre_ref.shape[0]
+    blocks = own_pre.shape[0]
+    step_taps = stride // GRAD_STEPS
 
     @pl.when(step == 0)
     def _():
-        turned[...] = flip(pre_ref[...])
+        turn_half(turned, own_pre, other_pre, mine_ref[0])
 
     for k in range(step_taps):
-        rows = picked(seasonal_ref, pl.ds(step * step_taps + k, blocks, stride=stride))
-        store_halves(out_ref, k, nn(turned[...], rows.astype(BF16)))
-
-
-def down_grad(pre, seasonal):
-    blocks, width = pre.shape
-    stride = seasonal.shape[1] // blocks
-    step_taps = 2
-    whole = lambda shape: pl.BlockSpec(
-        shape, lambda t: (0,) * len(shape), pipeline_mode=pl.Buffered(1)
-    )
-    return pl.pallas_call(
-        functools.partial(down_grad_kernel, stride, step_taps),
-        grid=(stride // step_taps,),
-        in_specs=[whole(pre.shape), whole(seasonal.shape)],
-        out_specs=pl.BlockSpec((2 * step_taps, width, width // 2), lambda t: (t, 0, 0)),
-        out_shape=jax.ShapeDtypeStruct((2 * stride, width, width // 2), BF16),
-        scratch_shapes=[pltpu.VMEM((width, blocks), BF16)],
-        compiler_params=pltpu.CompilerParams(vmem_limit_bytes=VMEM_LIMIT),
-        name="down_grad",
-    )(pre, seasonal)
+        there = pl.ds(step * step_taps + k, blocks, stride=stride)
+        rows = [picked(ref, there).astype(BF16) for ref in (own_seasonal, other_seasonal)]
+        rows = jnp.concatenate(rows, axis=0)
+        store_parts(orders, out_refs, k, nn(turned[...], rows).astype(BF16))
+
+
+def down_grad(mine, pre, seasonal, orders):
+    blocks, width = pre[0].shape
+    stride = seasonal[0].shape[1] // blocks
+    kernel = functools.partial(down_grad_kernel, stride, orders)
+    return grad_call(
+        kernel, "down_grad", stride, width, blocks, orders, (*pre, *seasonal), mine
+    )
 
 
 def back_kernel(
@@ -661,7 +779,8 @@
 def diagonal_blocks(matrix, count):
     height, width = matrix.shape[0] // count, matrix.shape[1] // count
     blocks = matrix.reshape(count, height, count, width)
-    return jnp.stack([blocks[at, :, at, :] for at in range(count)])
+    kept = jnp.eye(count, dtype=jnp.bool_)[:, None, :, None]
+    return jnp.sum(jnp.where(kept, blocks, 0.0), axis=2)
 
 
 def same_window(marks, offset):
@@ -697,62 +816,113 @@
     return since.astype(jnp.int32).reshape(-1, 1)
 
 
-def log2_of(size):
-    return size.bit_length() - 1
-
-
-def exchange(parts, axis, bit_axis, bit):
+BITS = {"core": ("var", 0), "x": ("var", 1), "y": ("rows", 0), "near": ("rows", 1), "far": ("rows", 2)}
+
+
+def own_bit(label):
+    axis, bit = BITS[label]
+    return (lax.axis_index(axis) >> bit) & 1
+
+
+def cross(values, label):
+    axis, bit = BITS[label]
+    flipped = (1 << bit, 0) if axis == "rows" else (0, 1 << bit)
+    pairs = [
+        (r * COLUMN_PARTS + c, (r ^ flipped[0]) * COLUMN_PARTS + (c ^ flipped[1]))
+        for r in range(ROW_PARTS)
+        for c in range(COLUMN_PARTS)
+    ]
+    return lax.ppermute(values, ("rows", "var"), pairs)
+
+
+class Turns:
+    def __init__(self):
+        self.last = ()
+
+    def seen(self, *values):
+        self.last = values
+
+    def after(self, small):
+        return lax.optimization_barrier((small, *self.last))[0]
+
+
+class Halving:
+    def __init__(self, turns, order):
+        self.turns, self.left, self.order = turns, list(ORDERS[order]), order
+
+    def start(self, *terms):
+        self.lines = terms[0].size // (16 * LANES)
+        self.terms = [term.reshape(-1, LANES) for term in terms]
+        self.places = [jnp.int32(0)] * len(terms)
+
+    def total(self, offset, lines):
+        pieces = [
+            lax.dynamic_slice(values, (place + offset, 0), (lines, LANES)).astype(F32)
+            for values, place in zip(self.terms, self.places)
+        ]
+        return functools.reduce(jnp.add, pieces)
+
+    def step(self):
+        label = self.left.pop(0)
+        lines = self.lines << len(self.left)
+        mine = self.turns.after(own_bit(label))
+        sent = self.total((1 - mine) * lines, lines).astype(BF16)
+        self.turns.seen(sent)
+        self.places = [place + mine * lines for place in self.places] + [jnp.int32(0)]
+        self.terms.append(cross(sent, label))
+
+    def finish(self):
+        while self.left:
+            self.step()
+        return self.total(0, self.lines)
+
+
+def by_columns(parts):
+    return parts.reshape(-1, LANES, LANES).transpose(0, 2, 1).reshape(-1, LANES)
+
+
+def by_features(parts, height):
+    panels = parts.reshape(-1, height, LANES)
+    return panels.transpose(1, 0, 2).reshape(height, -1)
+
+
+def other_core(values):
+    return lax.ppermute(
+        values, "var", [(c, c ^ 1) for c in range(lax.axis_size("var"))]
+    )
+
+
+def both_halves(home, away, order, mine):
+    home, away = from_part_order(home, order), from_part_order(away, order)
+    first = jnp.where(mine == 0, home, away)
+    second = jnp.where(mine == 0, away, home)
+    halves = jnp.stack([first, second], axis=2)
+    return halves.reshape(ROW_PARTS * COLUMN_PARTS, -1, LANES)
+
+
+def scattered(full):
     rows, columns = lax.axis_size("rows"), lax.axis_size("var")
-    mine = (lax.axis_index(bit_axis) >> bit) & 1
-    pairs = []
-    for r in range(rows):
-        for c in range(columns):
-            to = (r ^ (1 << bit), c) if bit_axis == "rows" else (r, c ^ (1 << bit))
-            pairs.append((r * columns + c, to[0] * columns + to[1]))
-    sent = lax.dynamic_index_in_dim(parts, 1 - mine, axis, keepdims=False)
-    kept = lax.dynamic_index_in_dim(parts, mine, axis, keepdims=False)
-    got = lax.ppermute(sent, ("rows", "var"), pairs)
-    return (kept.astype(F32) + got.astype(F32)).astype(BF16)
-
-
-def scatter_sum(grad, by_rows, order, shape):
-    rows, columns = lax.axis_size("rows"), lax.axis_size("var")
-    count, width, size = grad.shape
-    outer, inner = (rows, columns) if by_rows else (columns, rows)
-    names = ("rows", "var") if by_rows else ("var", "rows")
-    if count % outer or width % (16 * inner) or rows & (rows - 1) or columns & (columns - 1):
-        full = grad.transpose(1, 0, 2).reshape(width, count * size)
-        full = full.T if by_rows else full
-        height, depth = full.shape
-        full = full.reshape(rows, height // rows, columns, depth // columns)
-        full = full.transpose(0, 2, 1, 3).reshape(-1, depth // columns)
-        return lax.psum_scatter(full, ("rows", "var"), scatter_dimension=0, tiled=True).astype(F32)
-    labels = [(names[0], bit) for bit in reversed(range(log2_of(outer)))]
-    labels += [None]
-    labels += [(names[1], bit) for bit in reversed(range(log2_of(inner)))]
-    parts = grad.reshape(
-        (2,) * log2_of(outer) + (count // outer,) + (2,) * log2_of(inner) + (width // inner, size)
-    )
-    for label in order(log2_of(rows), log2_of(columns)):
-        axis = labels.index(label)
-        parts = exchange(parts, axis, *label)
-        labels.pop(axis)
-    parts = parts.astype(F32)
-    if by_rows:
-        return parts.transpose(0, 2, 1).reshape(shape)
-    return parts.transpose(1, 0, 2).reshape(shape)
-
-
-def across_first(row_bits, column_bits):
-    return [("var", bit) for bit in range(column_bits)] + [("rows", bit) for bit in range(row_bits)]
-
-
-def rows_first(row_bits, column_bits):
-    return (
-        [("var", 0), ("rows", 0)]
-        + [("var", bit) for bit in range(1, column_bits)]
-        + [("rows", bit) for bit in range(1, row_bits)]
-    )
+    height, depth = full.shape
+    full = full.reshape(rows, height // rows, columns, depth // columns)
+    full = full.transpose(0, 2, 1, 3).reshape(-1, depth // columns)
+    return lax.psum_scatter(full, ("rows", "var"), scatter_dimension=0, tiled=True).astype(F32)
+
+
+def scattered_columns(parts):
+    width = COLUMN_PARTS * LANES
+    panels = parts.reshape(ROW_PARTS, COLUMN_PARTS, -1, LANES, LANES)
+    return scattered(panels.transpose(0, 2, 4, 1, 3).reshape(-1, width))
+
+
+def scattered_features(parts, height):
+    panels = parts.reshape(ROW_PARTS, COLUMN_PARTS, -1, height, LANES)
+    return scattered(panels.transpose(0, 3, 1, 2, 4).reshape(ROW_PARTS * height, -1))
+
+
+def sum_everywhere(values):
+    for label in BITS:
+        values = values + cross(values, label)
+    return values
 
 
 def body(
@@ -794,27 +964,80 @@
     lifted_b, act_b, second_b, joined_b = scale_forward(
         seasonal, down_b, iso_b, up_b, since_b, norm_gains, SB
     )
-    (
-        predicted, pre_a, pre_b, sres, merge_parts, ff_in_parts, ff_out_parts, head_full, gains_late,
-    ) = tail(
+    mixing = rows == ROW_PARTS and columns == COLUMN_PARTS
+    mine = own_bit("core").reshape(1)
+    pair = lambda values: (values, other_core(values))
+    pair_marks = lax.dynamic_slice_in_dim(
+        frame_numbers, (var_index ^ 1) * time_rows, time_rows, 0
+    )
+    since_a = (since_a, blocks_since_start(pair_marks, SA, iso_a.shape[0] // width))
+    since_b = (since_b, blocks_since_start(pair_marks, SB, iso_b.shape[0] // width))
+    seasonal_pair, act_pair_a, act_pair_b = pair(seasonal), pair(act_a), pair(act_b)
+    joined_pair_a, joined_pair_b = pair(joined_a), pair(joined_b)
+    predicted, pre_a, pre_b, sres, late_parts, head_full, gains_late = tail(
         lifted_a, lifted_b, seasonal, trend, cotangent, merge_weight, ff_in, ff_out,
-        head_matrix, norm_gains, length,
-    )
-    up_a_parts = up_grad(joined_a, pre_a)
-    up_b_parts = up_grad(joined_b, pre_b)
+        head_matrix, norm_gains, mine, length,
+    )
+    turns = Turns()
+    orders = {
+        "late": ("z",), "up_b": ("x",), "up_a": ("y",), "iso_a": ("z", "x"), "down_a": ("y",),
+        "iso_b": ("x",), "down_b": ("y", "z"),
+    }
+    chains = {
+        name: [Halving(turns, order) for order in pieces] for name, pieces in orders.items()
+    }
+    done = {}
+
+    def go(*names):
+        for name in names if mixing else ():
+            for one in chains[name]:
+                one.step()
+
+    def produced(name, *pieces):
+        done[name] = pieces
+        turns.seen(*pieces)
+        for one, piece in zip(chains[name], pieces):
+            one.start(piece)
+
+    def turn():
+        return turns.after(mine)
+
+    taps_a, taps_b = iso_a.shape[0] // width, iso_b.shape[0] // width
+    turns.seen(late_parts)
+    done["late"] = (late_parts,)
+    if mixing:
+        chains["late"][0].start(late_parts[0], cross(late_parts[1].reshape(-1, LANES), "core"))
+    pre_pair_b, pre_pair_a = pair(pre_b), pair(pre_a)
     iso_pre_a, down_pre_a, block_a, gain_a = scale_backward(
-        pre_a, up_a, iso_a, down_a, act_a, second_a, since_a, norm_gains
-    )
+        pre_a, up_a, iso_a, down_a, act_a, second_a, since_a[0], turns.after(norm_gains)
+    )
+    turns.seen(iso_pre_a)
+    iso_pre_pair_a, down_pre_pair_a = pair(iso_pre_a), pair(down_pre_a)
+    go("late")
+    produced("up_b", up_grad(turn(), joined_pair_b, pre_pair_b, "x"))
+    go("up_b")
+    produced("up_a", up_grad(turn(), joined_pair_a, pre_pair_a, "y"))
+    go("up_a")
     iso_pre_b, down_pre_b, block_b, gain_b = scale_backward(
-        pre_b, up_b, iso_b, down_b, act_b, second_b, since_b, norm_gains
-    )
-    iso_a_parts = iso_grad(iso_pre_a, act_a, since_a, iso_a.shape[0] // width)
-    iso_b_parts = iso_grad(iso_pre_b, act_b, since_b, iso_b.shape[0] // width)
-    down_a_parts = down_grad(down_pre_a, seasonal)
-    down_b_parts = down_grad(down_pre_b, seasonal)
+        pre_b, up_b, iso_b, down_b, act_b, second_b, since_b[0], turns.after(norm_gains)
+    )
+    turns.seen(iso_pre_b)
+    iso_pre_pair_b, down_pre_pair_b = pair(iso_pre_b), pair(down_pre_b)
+    produced(
+        "iso_a", *iso_grad(turn(), iso_pre_pair_a, act_pair_a, since_a, taps_a, orders["iso_a"])
+    )
+    produced("down_a", *down_grad(turn(), down_pre_pair_a, seasonal_pair, orders["down_a"]))
+    go("late", "up_b", "up_a", "iso_a", "down_a")
+    produced(
+        "iso_b", *iso_grad(turn(), iso_pre_pair_b, act_pair_b, since_b, taps_b, orders["iso_b"])
+    )
+    produced("down_b", *down_grad(turn(), down_pre_pair_b, seasonal_pair, orders["down_b"]))
+    go("late", "up_b", "up_a", "iso_b", "down_b")
     series_grad, embed_full = back(
-        sres, block_a, block_b, cotangent, head_matrix, signal, flags, marks_row, by_group, length
-    )
+        sres, block_a, block_b, cotangent, head_matrix, signal, flags, marks_row,
+        turns.after(by_group), length
+    )
+    turns.seen(embed_full)
     gains_grad = jnp.concatenate([gains_late[0:1] + gain_a + gain_b, gains_late[1:]], axis=0)
     embed_full = jnp.einsum(
         "cv,tvd->tcd", pick.astype(F32), embed_full.reshape(3, variates, width),
@@ -824,23 +1047,51 @@
     head_grad = diagonal_blocks(head_full, groups)
     outward = jnp.stack([predicted, series_grad]).reshape(2, time_rows, length, variates)
     outward = lax.all_to_all(outward, "var", split_axis=3, concat_axis=1, tiled=True)
-    embed_sum, head_sum, gains_sum = lax.psum((embed_grad, head_grad, gains_grad), ("rows", "var"))
+    small = (embed_grad, head_grad, gains_grad)
+    if mixing:
+        flat = sum_everywhere(jnp.concatenate([part.reshape(-1, LANES) for part in small]))
+        pieces, at = [], 0
+        for part in small:
+            lines = part.size // LANES
+            pieces.append(flat[at : at + lines].reshape(part.shape))
+            at += lines
+        embed_sum, head_sum, gains_sum = pieces
+    else:
+        embed_sum, head_sum, gains_sum = lax.psum(small, ("rows", "var"))
     embed_sum = lax.dynamic_slice_in_dim(embed_sum, var_index * local_groups, local_groups, 0)
     head_sum = lax.dynamic_slice_in_dim(head_sum, var_index * local_groups, local_groups, 0)
 
-    def shard(weight):
-        return (weight.shape[0] // rows, weight.shape[1] // columns)
-
+    height = width // ROW_PARTS
+    merge_lines = merge_weight.size // (ROW_PARTS * COLUMN_PARTS * LANES)
+    in_lines = ff_in.size // (ROW_PARTS * COLUMN_PARTS * LANES)
+    if mixing:
+        go("iso_a", "down_a", "late", "up_b", "up_a", "iso_b", "down_b")
+        go("iso_a", "down_a", "iso_b", "down_b", "iso_a", "down_a", "iso_b", "down_b")
+        total = {
+            name: jnp.concatenate([one.finish() for one in pieces])
+            for name, pieces in chains.items()
+        }
+        late = total["late"]
+        turned, kept = by_columns, by_features
+    else:
+        total = {}
+        for name, pieces in done.items():
+            if name == "late":
+                halves = [(pieces[0][0], pieces[0][1])]
+            else:
+                halves = [(piece, jnp.zeros_like(piece)) for piece in pieces]
+            total[name] = jnp.concatenate(
+                [both_halves(*two, order, mine[0]) for two, order in zip(halves, orders[name])],
+                axis=1,
+            )
+        late = total["late"]
+        turned, kept = scattered_columns, scattered_features
+    split = (merge_lines, merge_lines + in_lines)
+    merge_part, in_part, out_part = jnp.split(late, split, axis=late.ndim - 2)
     summed = (
-        scatter_sum(down_a_parts, True, across_first, shard(down_a)),
-        scatter_sum(iso_a_parts, True, rows_first, shard(iso_a)),
-        scatter_sum(up_a_parts, False, across_first, shard(up_a)),
-        scatter_sum(down_b_parts, True, rows_first, shard(down_b)),
-        scatter_sum(iso_b_parts, True, across_first, shard(iso_b)),
-        scatter_sum(up_b_parts, False, rows_first, shard(up_b)),
-        scatter_sum(merge_parts, True, across_first, shard(merge_weight)),
-        scatter_sum(ff_in_parts, False, rows_first, shard(ff_in)),
-        scatter_sum(ff_out_parts, True, across_first, shard(ff_out)),
+        turned(total["down_a"]), turned(total["iso_a"]), kept(total["up_a"], height),
+        turned(total["down_b"]), turned(total["iso_b"]), kept(total["up_b"], height),
+        turned(merge_part), kept(in_part, height), turned(out_part),
     )
     return (outward[0], outward[1], embed_sum, head_sum, *summed, gains_sum)
 

time: 800 us -> 575 us (0.72)
  waiting for transfers between devices: 243 us -> 49.8 us
  blocking collectives: 59 us -> 16.2 us
  local copies, waits for them, and re-layouts: 85.6 us -> 64.4 us
  other arithmetic: 56.2 us -> 71.5 us
  Pallas kernels: 285 us -> 294 us
  starting transfers between devices: 55.8 us -> 64.2 us
    ppermute x45 -> x53, waiting for transfers between devices: 243 us -> 49.8 us  [the longest x42 49.8 us: cross(): return lax.ppermute(values, ('rows', 'var'), pairs)]
    psum x1 -> x0, blocking collectives: 48.1 us -> none  [body(): lax.psum((embed_grad, head_grad, gains_grad), ('rows', 'var'))]
    squeeze x42 -> x0, local copies, waits for them, and re-layouts: 38.7 us -> none  [exchange(): sent = lax.dynamic_index_in_dim(parts, 1 - mine, axis, keepdims=False)]
    dynamic_slice x6 -> x8, local copies, waits for them, and re-layouts: 7 us -> 20.3 us  [total(): lax.dynamic_slice(values, (place + offset, 0), (lines, LANES)).astype(F32)]
    add x0 -> x14, other arithmetic: none -> 11.6 us  [the longest x9 11.6 us: total(): return functools.reduce(jnp.add, pieces)]
    pallas_call x6, Pallas kernels: 49.7 us -> 58.8 us  [the longest x4 43.5 us: grad_call(): pl.pallas_call(kernel, grid_spec=split_spec((GRAD_STEPS,), [whole(value.s...]
    ppermute x45 -> x53, starting transfers between devices: 47.9 us -> 56.1 us  [the longest x42 53 us: cross(): return lax.ppermute(values, ('rows', 'var'), pairs)]
    convert_element_type x36 -> x28, other arithmetic: 48.6 us -> 54.9 us  [step(): sent = self.total((1 - mine) * lines, lines).astype(BF16)]
  transfers between devices with their start and end apart: 47 -> 55, of which waited for: 28 -> 11; matrix products, arithmetic and copies ran while one was open for 17% -> 24% of each run, Pallas kernels for 22% -> 52%
where the time goes in v3:
time: 575 us; the launch traced here: 565 us
  Pallas kernels  294 us (51%)
  other arithmetic  71.5 us (12%)
  local copies, waits for them, and re-layouts  64.4 us (11%)
  starting transfers between devices  64.2 us (11%)
  waiting for transfers between devices  49.8 us (9%)
  blocking collectives  16.2 us (3%)
    pallas_call x1, Pallas kernels, tail(): pl.pallas_call(tail_kernel, grid=(positions // length,), in_specs=[by_tap...  112 us
    convert_element_type x28, other arithmetic, step(): sent = self.total((1 - mine) * lines, lines).astype(BF16)  54.9 us
    ppermute x42, starting transfers between devices, cross(): return lax.ppermute(values, ('rows', 'var'), pairs)  53 us
    ppermute x42, waiting for transfers between devices, cross(): return lax.ppermute(values, ('rows', 'var'), pairs)  49.8 us
    pallas_call x2, Pallas kernels, scale_forward(): pl.pallas_call(functools.partial(scale_forward_kernel, stride, taps, step...  48.9 us
    pallas_call x2, Pallas kernels, scale_backward(): pl.pallas_call(functools.partial(scale_backward_kernel, stride, taps, ste...  47.8 us
    pallas_call x4, Pallas kernels, grad_call(): pl.pallas_call(kernel, grid_spec=split_spec((GRAD_STEPS,), [whole(value.s...  43.5 us
    dynamic_slice x8, local copies, waits for them, and re-layouts, total(): lax.dynamic_slice(values, (place + offset, 0), (lines, LANES)).astype(F32)  20.3 us
  transfers between devices with their start and end apart: 55, of which 11 were waited for; matrix products, arithmetic and copies ran while one was open for 24% of the time, Pallas kernels for 52%

profile of v3, /device:TPU:0, one launch (start us, length us, event | category | flops | bytes accessed | tf_op | source)
XLA Modules:
  0.0 564.9 jit_solution(12218008675710518263)
XLA Ops:
  0.7 4.4 all-to-all-start
  13.0 5.3 all_gather.6
  25.6 9.9 %front.1 = (f32[3072,512]{1,0:T(8,128)}, f32[4,3072,128]{2,1,0:T(8,128)}) custom-call(bf16[3072,32]{1,0:T(8,128)(2,1)} %bitcast.200, f32[3072,8]{1,0:T(8,128)} %copy.143.flags_ref, f32[4,1,768]{2,1,0:T(1,128)} %reshape.223.marks_ref, bf16[96,512]{1,0:T(8,128)(2,1)} %pad_maximum_fusion.3.weight_ref), custom_call_target="tpu_custom_call" | custom-call | tf_op jit(solution)/shard_map/front/pallas_call | solution.py:132
  36.1 10.9 %all_gather.7 = bf16[8,64,4]{1,2,0:T(4,128)(2,1)S(1)} all-gather(bf16[2,64,4]{1,2,0:T(4,128)(2,1)S(1)} %copy-done.14), channel_id=1, replica_groups=mesh['rows'=8,'var'=4] {'var'}, dimensions={0}, use_global_device_ids=true | all-gather | bytes 5120 | tf_op jit(solution)/shard_map/all_gather | solution.py:941
  49.7 25.0 %scale_forward.3 = (bf16[16,192,512]{2,1,0:T(8,128)(2,1)}, f32[192,512]{1,0:T(8,128)}, f32[192,512]{1,0:T(8,128)}, bf16[192,512]{1,0:T(8,128)(2,1)}) custom-call(f32[4,3072,128]{2,1,0:T(8,128)} %get-tuple-element.90.seasonal_ref.own_seasonal, bf16[8192,512]{1,0:T(8,128)(2,1)} %down_ref.7, bf16[6144,512]{1,0:T(8,128)(2,1)} %iso_ref.7, ...), custom_call_target="tpu_custom_call" | custom-call | tf_op jit(solution)/shard_map/scale_forward/pallas_call | solution.py:217
  74.7 23.9 %scale_forward.2 = (bf16[12,256,512]{2,1,0:T(8,128)(2,1)}, f32[256,512]{1,0:T(8,128)}, f32[256,512]{1,0:T(8,128)}, bf16[256,512]{1,0:T(8,128)(2,1)}) custom-call(f32[4,3072,128]{2,1,0:T(8,128)} %get-tuple-element.90.seasonal_ref.own_seasonal, bf16[6144,512]{1,0:T(8,128)(2,1)} %down_ref.6, bf16[8192,512]{1,0:T(8,128)(2,1)} %iso_ref.6, ...), custom_call_target="tpu_custom_call" | custom-call | tf_op jit(solution)/shard_map/scale_forward/pallas_call | solution.py:217
  99.9 112.4 %tail.1 = (f32[3072,32]{1,0:T(8,128)}, bf16[12,256,512]{2,1,0:T(8,128)(2,1)}, bf16[16,192,512]{2,1,0:T(8,128)(2,1)}, f32[3072,512]{1,0:T(8,128)}, bf16[2,2,2,2,2...) custom-call(bf16[12,256,512]{2,1,0:T(8,128)(2,1)} %get-tuple-element.91.lifted_a_ref, ...), custom_call_target="tpu_custom_call" | custom-call | tf_op jit(solution)/shard_map/tail/pallas_call | solution.py:391
  212.4 4.6 fusion.19
  217.9 23.2 %scale_backward.2 = (bf16[256,512]{1,0:T(8,128)(2,1)}, bf16[256,512]{1,0:T(8,128)(2,1)}, bf16[12,256,512]{2,1,0:T(8,128)(2,1)}, f32[1,512]{1,0:T(1,128)}) custom-call(bf16[12,256,512]{2,1,0:T(8,128)(2,1)} %get-tuple-element.96.pre_ref.own_pre, bf16[512,6144]{1,0:T(8,128)(2,1)} %up_ref.6, bf16[8192,512]{1,0:T(8,128)(2,1)} %iso_ref.6, ...), custom_call_target="tpu_custom_call" | custom-call | tf_op jit(solution)/shard_map/scale_backward/pallas_call | solution.py:489
  241.4 2.7 add_convert_fusion
  244.8 8.5 %up_grad.2 = bf16[2,2,2,2,16,64,128]{6,5,4,3,2,1,0:T(8,128)(2,1)} custom-call(s32[1]{0:T(128)} %bitcast.3.mine_ref, bf16[192,512]{1,0:T(8,128)(2,1)} %get-tuple-element.108.own_joined, bf16[192,512]{1,0:T(8,128)(2,1)} %copy-done.10, bf16[16,192,512]{2,1,0:T(8,128)(2,1)} %get-tuple-element.102.own_pre.pre_ref, ...), custom_call_target="tpu_custom_call" | custom-call | tf_op jit(solution)/shard_map/up_grad/pallas_call | solution.py:556
  253.3 3.1 constant_dynamic-slice_fusion.18
  261.7 6.7 %up_grad.3 = bf16[2,2,2,2,12,64,128]{6,5,4,3,2,1,0:T(8,128)(2,1)} custom-call(s32[1]{0:T(128)} %bitcast.3.mine_ref, bf16[256,512]{1,0:T(8,128)(2,1)} %get-tuple-element.111.own_joined, bf16[256,512]{1,0:T(8,128)(2,1)} %collective-permute-done.3.other_joined, bf16[12,256,512]{2,1,0:T(8,128)(2,1)} %get-tuple-element.96.pre_ref.own_pre, ...), custom_call_target="tpu_custom_call" | custom-call | tf_op jit(solution)/shard_map/up_grad/pallas_call | solution.py:556
  268.5 2.7 constant_dynamic-slice_fusion.17
  275.8 24.6 %scale_backward.3 = (bf16[192,512]{1,0:T(8,128)(2,1)}, bf16[192,512]{1,0:T(8,128)(2,1)}, bf16[16,192,512]{2,1,0:T(8,128)(2,1)}, f32[1,512]{1,0:T(1,128)}) custom-call(bf16[16,192,512]{2,1,0:T(8,128)(2,1)} %get-tuple-element.102.own_pre.pre_ref, bf16[512,8192]{1,0:T(8,128)(2,1)} %up_ref.7, bf16[6144,512]{1,0:T(8,128)(2,1)} %iso_ref.7, ...), custom_call_target="tpu_custom_call" | custom-call | tf_op jit(solution)/shard_map/scale_backward/pallas_call | solution.py:489
  301.2 11.7 %iso_grad.2 = (bf16[2,2,2,2,4,128,128]{6,5,4,3,2,1,0:T(8,128)(2,1)}, bf16[2,2,2,2,4,128,128]{6,5,4,3,2,1,0:T(8,128)(2,1)}) custom-call(s32[1]{0:T(128)} %bitcast.3.mine_ref, bf16[256,512]{1,0:T(8,128)(2,1)} %get-tuple-element.105.own_pre, bf16[256,512]{1,0:T(8,128)(2,1)} %collective-permute-done.5.other_pre, f32[256,512]{1,0:T(8,128)} %get-tuple-element.97.act_ref.own_act, ...), custom_call_target="tpu_custom_call" | custom-call | tf_op jit(solution)/shard_map/iso_grad/pallas_call | solution.py:626
  313.6 9.2 %down_grad.2 = bf16[2,2,2,2,6,128,128]{6,5,4,3,2,1,0:T(8,128)(2,1)} custom-call(s32[1]{0:T(128)} %bitcast.3.mine_ref, bf16[256,512]{1,0:T(8,128)(2,1)} %get-tuple-element.120.own_pre, bf16[256,512]{1,0:T(8,128)(2,1)} %copy-done.6, f32[4,3072,128]{2,1,0:T(8,128)} %get-tuple-element.90.seasonal_ref.own_seasonal, ...), custom_call_target="tpu_custom_call" | custom-call | tf_op jit(solution)/shard_map/down_grad/pallas_call | solution.py:626
  326.0 2.8 add_convert_fusion.1
  335.6 2.7 constant_dynamic-slice_fusion.11
  340.0 8.0 %iso_grad.3 = bf16[2,2,2,2,6,128,128]{6,5,4,3,2,1,0:T(8,128)(2,1)} custom-call(s32[1]{0:T(128)} %bitcast.3.mine_ref, bf16[192,512]{1,0:T(8,128)(2,1)} %get-tuple-element.115.own_pre, bf16[192,512]{1,0:T(8,128)(2,1)} %collective-permute-done.12.other_pre, f32[192,512]{1,0:T(8,128)} %get-tuple-element.103.act_ref.own_act, ...), custom_call_target="tpu_custom_call" | custom-call | tf_op jit(solution)/shard_map/iso_grad/pallas_call | solution.py:626
  350.0 14.6 %down_grad.3 = (bf16[2,2,2,2,4,128,128]{6,5,4,3,2,1,0:T(8,128)(2,1)}, bf16[2,2,2,2,4,128,128]{6,5,4,3,2,1,0:T(8,128)(2,1)}) custom-call(s32[1]{0:T(128)} %bitcast.3.mine_ref, bf16[192,512]{1,0:T(8,128)(2,1)} %get-tuple-element.129.own_pre, bf16[192,512]{1,0:T(8,128)(2,1)} %collective-permute-done.14.other_pre, ...), custom_call_target="tpu_custom_call" | custom-call | tf_op jit(solution)/shard_map/down_grad/pallas_call | solution.py:626
  380.0 16.6 %back.1 = (f32[3072,32]{1,0:T(8,128)}, f32[96,512]{1,0:T(8,128)}) custom-call(f32[3072,512]{1,0:T(8,128)} %get-tuple-element.95.sres_ref, bf16[12,256,512]{2,1,0:T(8,128)(2,1)} %get-tuple-element.101.block_a_ref, bf16[16,192,512]{2,1,0:T(8,128)(2,1)} %get-tuple-element.114.block_b_ref, bf16[3072,32]{1,0:T(8,128)(2,1)} %copy.148.cot_ref, ...), custom_call_target="tpu_custom_call" | custom-call | tf_op jit(solution)/shard_map/back/pallas_call | solution.py:748
  407.0 5.5 collective-permute-done.20
  423.6 3.7 all-to-all-start.1
  438.0 4.0 collective-permute-start.31
  451.4 14.5 %collective-permute-done.52 = bf16[640,128]{1,0:T(8,128)(2,1)} collective-permute-done((bf16[640,128]{1,0:T(8,128)(2,1)}, bf16[640,128]{1,0:T(8,128)(2,1)}, u32[]{:S(2)}, u32[]{:S(2)}) %collective-permute-start.52) | collective-permute-done | bytes 163872 | tf_op jit(solution)/shard_map/ppermute | solution.py:835
  465.9 3.4 collective-permute-start.44
  493.2 11.1 %collective-permute-done.34 = bf16[3072,128]{1,0:T(8,128)(2,1)} collective-permute-done((bf16[3072,128]{1,0:T(8,128)(2,1)}, bf16[3072,128]{1,0:T(8,128)(2,1)}, u32[]{:S(2)}, u32[]{:S(2)}) %collective-permute-start.34) | collective-permute-done | bytes 786464 | tf_op jit(solution)/shard_map/ppermute | solution.py:835
  537.7 3.8 collective-permute-done.45
  545.7 3.5 collective-permute-start.49
  551.6 2.9 collective-permute-start.50
  555.6 4.3 collective-permute-done.47
  (286 shorter events, 172.8 us)
Async XLA Ops:
  0.7 97.9 %all-to-all-start = ((bf16[16,768,8]{1,2,0:T(8,128)(2,1)}), bf16[16,768,8]{1,2,0:T(8,128)(2,1)S(1)}, u32[]{:S(2)}, u32[]{:S(2)}) async-start(bf16[16,768,8]{1,2,0:T(8,128)(2,1)} %param.31), calls=%async_computation | async-start | bytes 393216 | tf_op jit(solution)/shard_map/all_to_all | solution.py:942
  35.4 278.0 %collective-permute-start.8 = (f32[4,3072,128]{2,1,0:T(8,128)}, f32[4,3072,128]{2,1,0:T(8,128)}, u32[]{:S(2)}, u32[]{:S(2)}) collective-permute-start(f32[4,3072,128]{2,1,0:T(8,128)} %get-tuple-element.90.seasonal_ref.own_seasonal), channel_id=1, source_target_pairs={{0,1},{1,0},{2,3},{3,2},{4,5},{5,4},{6,7},{7,6},{8,9},{9,8},{10,11... | collective-permute-start | bytes 18874376 | tf_op jit(solution)/shard_map/ppermute | solution.py:890
  216.9 24.2 %collective-permute-start = (bf16[10240,128]{1,0:T(8,128)(2,1)}, bf16[10240,128]{1,0:T(8,128)(2,1)}, u32[]{:S(2)}, u32[]{:S(2)}) collective-permute-start(bf16[10240,128]{1,0:T(8,128)(2,1)} %bitcast.6), channel_id=1, source_target_pairs={{0,1},{1,0},{2,3},{3,2},{4,5},{5,4},{6,7},{7,6},{8,9},{9,8},{10,11... | collective-permute-start | bytes 7864328 | tf_op jit(solution)/shard_map/ppermute | solution.py:835
  217.1 27.4 %collective-permute-start.2 = (bf16[16,192,512]{2,1,0:T(8,128)(2,1)}, bf16[16,192,512]{2,1,0:T(8,128)(2,1)}, u32[]{:S(2)}, u32[]{:S(2)}) collective-permute-start(bf16[16,192,512]{2,1,0:T(8,128)(2,1)} %get-tuple-element.102.own_pre.pre_ref), channel_id=1, source_target_pairs={{0,1},{1,0},{2,3},{3,2},{4,5},{5,4},{6,7},{7,6},{8,9},{9,8},{10,11... | collective-permute-start | bytes 9437192 | tf_op jit(solution)/shard_map/ppermute | solution.py:890
  217.4 42.2 %collective-permute-start.4 = (bf16[12,256,512]{2,1,0:T(8,128)(2,1)}, bf16[12,256,512]{2,1,0:T(8,128)(2,1)}, u32[]{:S(2)}, u32[]{:S(2)}) collective-permute-start(bf16[12,256,512]{2,1,0:T(8,128)(2,1)} %get-tuple-element.96.pre_ref.own_pre), channel_id=1, source_target_pairs={{0,1},{1,0},{2,3},{3,2},{4,5},{5,4},{6,7},{7,6},{8,9},{9,8},{10,11... | collective-permute-start | bytes 9437192 | tf_op jit(solution)/shard_map/ppermute | solution.py:890
  217.6 82.8 %collective-permute-start.6 = (f32[256,512]{1,0:T(8,128)S(1)}, f32[256,512]{1,0:T(8,128)}, u32[]{:S(2)}, u32[]{:S(2)}) collective-permute-start(f32[256,512]{1,0:T(8,128)S(1)} %copy-done.3), channel_id=1, source_target_pairs={{0,1},{1,0},{2,3},{3,2},{4,5},{5,4},{6,7},{7,6},{8,9},{9,8},{10,11... | collective-permute-start | bytes 1572872 | tf_op jit(solution)/shard_map/ppermute | solution.py:890
  256.4 69.4 %collective-permute-start.10 = (bf16[8192,128]{1,0:T(8,128)(2,1)}, bf16[8192,128]{1,0:T(8,128)(2,1)}, u32[]{:S(2)}, u32[]{:S(2)}) collective-permute-start(bf16[8192,128]{1,0:T(8,128)(2,1)} %constant_dynamic-slice_fusion.18), channel_id=1, source_target_pairs={{0,2},{1,3},{2,0},{3,1},{4,6},{5,7},{6,4},{7,5},{8,10},{9,11},{10,... | collective-permute-start | bytes 6291464 | tf_op jit(solution)/shard_map/ppermute | solution.py:835
  259.6 63.2 %collective-permute-start.9 = (bf16[5120,128]{1,0:T(8,128)(2,1)}, bf16[5120,128]{1,0:T(8,128)(2,1)}, u32[]{:S(2)}, u32[]{:S(2)}) collective-permute-start(bf16[5120,128]{1,0:T(8,128)(2,1)} %add_convert_fusion), channel_id=1, source_target_pairs={{0,8},{1,9},{2,10},{3,11},{4,12},{5,13},{6,14},{7,15},{8,0},{9,1},... | collective-permute-start | bytes 3932168 | tf_op jit(solution)/shard_map/ppermute | solution.py:835
  271.1 57.7 %collective-permute-start.11 = (bf16[6144,128]{1,0:T(8,128)(2,1)}, bf16[6144,128]{1,0:T(8,128)(2,1)}, u32[]{:S(2)}, u32[]{:S(2)}) collective-permute-start(bf16[6144,128]{1,0:T(8,128)(2,1)} %constant_dynamic-slice_fusion.17), channel_id=1, source_target_pairs={{0,4},{1,5},{2,6},{3,7},{4,0},{5,1},{6,2},{7,3},{8,12},{9,13},{10,... | collective-permute-start | bytes 4718600 | tf_op jit(solution)/shard_map/ppermute | solution.py:835
  312.9 22.6 %collective-permute-start.13 = (f32[192,512]{1,0:T(8,128)}, f32[192,512]{1,0:T(8,128)}, u32[]{:S(2)}, u32[]{:S(2)}) collective-permute-start(f32[192,512]{1,0:T(8,128)} %get-tuple-element.103.act_ref.own_act), channel_id=1, source_target_pairs={{0,1},{1,0},{2,3},{3,2},{4,5},{5,4},{6,7},{7,6},{8,9},{9,8},{10,11... | collective-permute-start | bytes 1179656 | tf_op jit(solution)/shard_map/ppermute | solution.py:890
  313.5 24.8 %collective-permute-start.12 = (bf16[192,512]{1,0:T(8,128)(2,1)}, bf16[192,512]{1,0:T(8,128)(2,1)}, u32[]{:S(2)}, u32[]{:S(2)}) collective-permute-start(bf16[192,512]{1,0:T(8,128)(2,1)} %get-tuple-element.115.own_pre), channel_id=1, source_target_pairs={{0,1},{1,0},{2,3},{3,2},{4,5},{5,4},{6,7},{7,6},{8,9},{9,8},{10,11... | collective-permute-start | bytes 589832 | tf_op jit(solution)/shard_map/ppermute | solution.py:890
  322.8 25.2 %collective-permute-start.14 = (bf16[192,512]{1,0:T(8,128)(2,1)}, bf16[192,512]{1,0:T(8,128)(2,1)}, u32[]{:S(2)}, u32[]{:S(2)}) collective-permute-start(bf16[192,512]{1,0:T(8,128)(2,1)} %get-tuple-element.129.own_pre), channel_id=1, source_target_pairs={{0,1},{1,0},{2,3},{3,2},{4,5},{5,4},{6,7},{7,6},{8,9},{9,8},{10,11... | collective-permute-start | bytes 589832 | tf_op jit(solution)/shard_map/ppermute | solution.py:890
  325.8 38.9 %collective-permute-start.15 = (bf16[2560,128]{1,0:T(8,128)(2,1)}, bf16[2560,128]{1,0:T(8,128)(2,1)}, u32[]{:S(2)}, u32[]{:S(2)}) collective-permute-start(bf16[2560,128]{1,0:T(8,128)(2,1)} %add_convert_fusion.5), channel_id=1, source_target_pairs={{0,2},{1,3},{2,0},{3,1},{4,6},{5,7},{6,4},{7,5},{8,10},{9,11},{10,... | collective-permute-start | bytes 1966088 | tf_op jit(solution)/shard_map/ppermute | solution.py:835
  332.7 35.5 %collective-permute-start.16 = (bf16[4096,128]{1,0:T(8,128)(2,1)}, bf16[4096,128]{1,0:T(8,128)(2,1)}, u32[]{:S(2)}, u32[]{:S(2)}) collective-permute-start(bf16[4096,128]{1,0:T(8,128)(2,1)} %add_convert_fusion.1), channel_id=1, source_target_pairs={{0,4},{1,5},{2,6},{3,7},{4,0},{5,1},{6,2},{7,3},{8,12},{9,13},{10,... | collective-permute-start | bytes 3145736 | tf_op jit(solution)/shard_map/ppermute | solution.py:835
  335.5 35.1 %collective-permute-start.17 = (bf16[3072,128]{1,0:T(8,128)(2,1)S(1)}, bf16[3072,128]{1,0:T(8,128)(2,1)}, u32[]{:S(2)}, u32[]{:S(2)}) collective-permute-start(bf16[3072,128]{1,0:T(8,128)(2,1)S(1)} %add_convert_fusion.4), channel_id=1, source_target_pairs={{0,8},{1,9},{2,10},{3,11},{4,12},{5,13},{6,14},{7,15},{8,0},{9,1},... | collective-permute-start | bytes 2359304 | tf_op jit(solution)/shard_map/ppermute | solution.py:835
  338.2 80.6 %collective-permute-start.24 = (bf16[4096,128]{1,0:T(8,128)(2,1)}, bf16[4096,128]{1,0:T(8,128)(2,1)}, u32[]{:S(2)}, u32[]{:S(2)}) collective-permute-start(bf16[4096,128]{1,0:T(8,128)(2,1)} %constant_dynamic-slice_fusion.12), channel_id=1, source_target_pairs={{0,2},{1,3},{2,0},{3,1},{4,6},{5,7},{6,4},{7,5},{8,10},{9,11},{10,... | collective-permute-start | bytes 3145736 | tf_op jit(solution)/shard_map/ppermute | solution.py:835
  348.0 66.3 %collective-permute-start.23 = (bf16[4096,128]{1,0:T(8,128)(2,1)}, bf16[4096,128]{1,0:T(8,128)(2,1)}, u32[]{:S(2)}, u32[]{:S(2)}) collective-permute-start(bf16[4096,128]{1,0:T(8,128)(2,1)} %constant_dynamic-slice_fusion.13), channel_id=1, source_target_pairs={{0,8},{1,9},{2,10},{3,11},{4,12},{5,13},{6,14},{7,15},{8,0},{9,1},... | collective-permute-start | bytes 3145736 | tf_op jit(solution)/shard_map/ppermute | solution.py:835
  364.7 70.5 %collective-permute-start.25 = (bf16[6144,128]{1,0:T(8,128)(2,1)}, bf16[6144,128]{1,0:T(8,128)(2,1)}, u32[]{:S(2)}, u32[]{:S(2)}) collective-permute-start(bf16[6144,128]{1,0:T(8,128)(2,1)} %constant_dynamic-slice_fusion.11), channel_id=1, source_target_pairs={{0,4},{1,5},{2,6},{3,7},{4,0},{5,1},{6,2},{7,3},{8,12},{9,13},{10,... | collective-permute-start | bytes 4718600 | tf_op jit(solution)/shard_map/ppermute | solution.py:835
  401.9 36.1 %collective-permute-start.26 = (bf16[1280,128]{1,0:T(8,128)(2,1)}, bf16[1280,128]{1,0:T(8,128)(2,1)}, u32[]{:S(2)}, u32[]{:S(2)}) collective-permute-start(bf16[1280,128]{1,0:T(8,128)(2,1)} %add_convert_fusion.14), channel_id=1, source_target_pairs={{0,4},{1,5},{2,6},{3,7},{4,0},{5,1},{6,2},{7,3},{8,12},{9,13},{10,... | collective-permute-start | bytes 983048 | tf_op jit(solution)/shard_map/ppermute | solution.py:835
  412.5 35.0 %collective-permute-start.28 = (bf16[1536,128]{1,0:T(8,128)(2,1)}, bf16[1536,128]{1,0:T(8,128)(2,1)}, u32[]{:S(2)}, u32[]{:S(2)}) collective-permute-start(bf16[1536,128]{1,0:T(8,128)(2,1)} %add_convert_fusion.13), channel_id=1, source_target_pairs={{0,2},{1,3},{2,0},{3,1},{4,6},{5,7},{6,4},{7,5},{8,10},{9,11},{10,... | collective-permute-start | bytes 1179656 | tf_op jit(solution)/shard_map/ppermute | solution.py:835
  418.4 25.6 %collective-permute-start.27 = (bf16[2048,128]{1,0:T(8,128)(2,1)}, bf16[2048,128]{1,0:T(8,128)(2,1)}, u32[]{:S(2)}, u32[]{:S(2)}) collective-permute-start(bf16[2048,128]{1,0:T(8,128)(2,1)} %add_convert_fusion.10), channel_id=1, source_target_pairs={{0,8},{1,9},{2,10},{3,11},{4,12},{5,13},{6,14},{7,15},{8,0},{9,1},... | collective-permute-start | bytes 1572872 | tf_op jit(solution)/shard_map/ppermute | solution.py:835
  423.6 25.9 %all-to-all-start.1 = ((f32[2,4,768,32]{2,1,0,3:T(4,128)}), f32[2,4,768,32]{2,1,0,3:T(4,128)S(1)}, u32[]{:S(2)}, u32[]{:S(2)}) async-start(f32[2,4,768,32]{2,1,0,3:T(4,128)} %pad_maximum_fusion), calls=%async_computation.1 | async-start | bytes 1572864 | tf_op jit(solution)/shard_map/all_to_all | solution.py:1049
  429.5 61.7 %collective-permute-start.33 = (bf16[2048,128]{1,0:T(8,128)(2,1)}, bf16[2048,128]{1,0:T(8,128)(2,1)}, u32[]{:S(2)}, u32[]{:S(2)}) collective-permute-start(bf16[2048,128]{1,0:T(8,128)(2,1)} %add_convert_fusion.8), channel_id=1, source_target_pairs={{0,4},{1,5},{2,6},{3,7},{4,0},{5,1},{6,2},{7,3},{8,12},{9,13},{10,... | collective-permute-start | bytes 1572872 | tf_op jit(solution)/shard_map/ppermute | solution.py:835
  435.2 43.9 %collective-permute-start.29 = (bf16[6144,128]{1,0:T(8,128)(2,1)}, bf16[6144,128]{1,0:T(8,128)(2,1)}, u32[]{:S(2)}, u32[]{:S(2)}) collective-permute-start(bf16[6144,128]{1,0:T(8,128)(2,1)} %constant_dynamic-slice_fusion.9), channel_id=1, source_target_pairs={{0,2},{1,3},{2,0},{3,1},{4,6},{5,7},{6,4},{7,5},{8,10},{9,11},{10,... | collective-permute-start | bytes 4718600 | tf_op jit(solution)/shard_map/ppermute | solution.py:835
  438.0 46.3 %collective-permute-start.31 = (bf16[4096,128]{1,0:T(8,128)(2,1)}, bf16[4096,128]{1,0:T(8,128)(2,1)}, u32[]{:S(2)}, u32[]{:S(2)}) collective-permute-start(bf16[4096,128]{1,0:T(8,128)(2,1)} %constant_dynamic-slice_fusion.7), channel_id=1, source_target_pairs={{0,8},{1,9},{2,10},{3,11},{4,12},{5,13},{6,14},{7,15},{8,0},{9,1},... | collective-permute-start | bytes 3145736 | tf_op jit(solution)/shard_map/ppermute | solution.py:835
  443.9 36.7 %collective-permute-start.30 = (bf16[4096,128]{1,0:T(8,128)(2,1)}, bf16[4096,128]{1,0:T(8,128)(2,1)}, u32[]{:S(2)}, u32[]{:S(2)}) collective-permute-start(bf16[4096,128]{1,0:T(8,128)(2,1)} %constant_dynamic-slice_fusion.8), channel_id=1, source_target_pairs={{0,4},{1,5},{2,6},{3,7},{4,0},{5,1},{6,2},{7,3},{8,12},{9,13},{10,... | collective-permute-start | bytes 3145736 | tf_op jit(solution)/shard_map/ppermute | solution.py:835
  479.0 25.3 %collective-permute-start.34 = (bf16[3072,128]{1,0:T(8,128)(2,1)}, bf16[3072,128]{1,0:T(8,128)(2,1)}, u32[]{:S(2)}, u32[]{:S(2)}) collective-permute-start(bf16[3072,128]{1,0:T(8,128)(2,1)} %add_convert_fusion.3), channel_id=1, source_target_pairs={{0,8},{1,9},{2,10},{3,11},{4,12},{5,13},{6,14},{7,15},{8,0},{9,1},... | collective-permute-start | bytes 2359304 | tf_op jit(solution)/shard_map/ppermute | solution.py:835
  480.6 26.8 %collective-permute-start.35 = (bf16[3072,128]{1,0:T(8,128)(2,1)S(1)}, bf16[3072,128]{1,0:T(8,128)(2,1)}, u32[]{:S(2)}, u32[]{:S(2)}) collective-permute-start(bf16[3072,128]{1,0:T(8,128)(2,1)S(1)} %add_convert_fusion.2), channel_id=1, source_target_pairs={{0,4},{1,5},{2,6},{3,7},{4,0},{5,1},{6,2},{7,3},{8,12},{9,13},{10,... | collective-permute-start | bytes 2359304 | tf_op jit(solution)/shard_map/ppermute | solution.py:835
  484.2 37.2 %collective-permute-start.51 = (bf16[1024,128]{1,0:T(8,128)(2,1)}, bf16[1024,128]{1,0:T(8,128)(2,1)}, u32[]{:S(2)}, u32[]{:S(2)}) collective-permute-start(bf16[1024,128]{1,0:T(8,128)(2,1)} %add_convert_fusion.19), channel_id=1, source_target_pairs={{0,16},{1,17},{2,18},{3,19},{4,20},{5,21},{6,22},{7,23},{8,24},{9,... | collective-permute-start | bytes 786440 | tf_op jit(solution)/shard_map/ppermute | solution.py:835
  489.2 23.1 %collective-permute-start.36 = (bf16[2048,128]{1,0:T(8,128)(2,1)}, bf16[2048,128]{1,0:T(8,128)(2,1)S(1)}, u32[]{:S(2)}, u32[]{:S(2)}) collective-permute-start(bf16[2048,128]{1,0:T(8,128)(2,1)} %add_convert_fusion.7), channel_id=1, source_target_pairs={{0,8},{1,9},{2,10},{3,11},{4,12},{5,13},{6,14},{7,15},{8,0},{9,1},... | collective-permute-start | bytes 1572872 | tf_op jit(solution)/shard_map/ppermute | solution.py:835
  493.1 26.6 %collective-permute-start.39 = (bf16[1024,128]{1,0:T(8,128)(2,1)}, bf16[1024,128]{1,0:T(8,128)(2,1)}, u32[]{:S(2)}, u32[]{:S(2)}) collective-permute-start(bf16[1024,128]{1,0:T(8,128)(2,1)} %add_convert_fusion.17), channel_id=1, source_target_pairs={{0,8},{1,9},{2,10},{3,11},{4,12},{5,13},{6,14},{7,15},{8,0},{9,1},... | collective-permute-start | bytes 786440 | tf_op jit(solution)/shard_map/ppermute | solution.py:835
  528.6 20.6 %collective-permute-start.41 = (bf16[768,128]{1,0:T(8,128)(2,1)}, bf16[768,128]{1,0:T(8,128)(2,1)}, u32[]{:S(2)}, u32[]{:S(2)}) collective-permute-start(bf16[768,128]{1,0:T(8,128)(2,1)} %add_convert_fusion.21), channel_id=1, source_target_pairs={{0,16},{1,17},{2,18},{3,19},{4,20},{5,21},{6,22},{7,23},{8,24},{9,... | collective-permute-start | bytes 589832 | tf_op jit(solution)/shard_map/ppermute | solution.py:835
  (39 other events, 407.7 us)

commit v4 on v3

--- a/solution.py
+++ b/solution.py
@@ -31,12 +31,16 @@
 
 
 LANES = 128
+STEP_TAPS = 4
 ROW_PARTS = 8
 COLUMN_PARTS = 4
 ORDERS = {
-    "x": ("x", "y", "near", "far"),
-    "y": ("y", "near", "x", "far"),
-    "z": ("near", "x", "y", "far"),
+    "xyn": ("x", "y", "near", "far"),
+    "xny": ("x", "near", "y", "far"),
+    "yxn": ("y", "x", "near", "far"),
+    "ynx": ("y", "near", "x", "far"),
+    "nxy": ("near", "x", "y", "far"),
+    "nyx": ("near", "y", "x", "far"),
 }
 
 
@@ -104,7 +108,10 @@
     return [(at, min(max(at - 128, 0), length - span), tile, span) for at in range(0, length, tile)]
 
 
-def front_kernel(signal_ref, flags_ref, marks_ref, weight_ref, trend_ref, seasonal_ref, hidden_ref):
+def front_kernel(
+    signal_ref, flags_ref, marks_ref, weight_ref, trend_ref, seasonal_ref, taps_a_ref, taps_b_ref,
+    hidden_ref, lanes_ref,
+):
     length = signal_ref.shape[0]
     variates = signal_ref.shape[1]
     signal = signal_ref[...].astype(F32)
@@ -122,7 +129,13 @@
         trend = nn(near, source) * flags_ref[at : at + tile, 2:3]
         trend = trend + nn(wide, source) * flags_ref[at : at + tile, 3:4]
         trend_ref[at : at + tile, :] = trend
-        placed(seasonal_ref, slice(at, at + tile), hidden_ref[at : at + tile, :].astype(F32) - trend)
+        seasonal = hidden_ref[at : at + tile, :].astype(F32) - trend
+        seasonal_ref[at : at + tile, :] = seasonal
+        placed(lanes_ref, slice(at, at + tile), seasonal)
+    for taps_ref in (taps_a_ref, taps_b_ref):
+        stride, blocks, _ = taps_ref.shape
+        for j in range(stride):
+            taps_ref[j] = picked(lanes_ref, pl.ds(j, blocks, stride=stride)).astype(BF16)
 
 
 def front(signal, flags, marks_row, weight, length):
@@ -140,13 +153,17 @@
         ],
         out_specs=[
             pl.BlockSpec((length, width), lambda i: (i, 0)),
-            pl.BlockSpec((width // LANES, length, LANES), lambda i: (0, i, 0)),
+            pl.BlockSpec((length, width), lambda i: (i, 0)),
+            *[pl.BlockSpec((s, length // s, width), lambda i: (0, i, 0)) for s in (SA, SB)],
         ],
         out_shape=[
             jax.ShapeDtypeStruct((positions, width), F32),
-            jax.ShapeDtypeStruct((width // LANES, positions, LANES), F32),
-        ],
-        scratch_shapes=[pltpu.VMEM((length, width), BF16)],
+            jax.ShapeDtypeStruct((positions, width), F32),
+            *[jax.ShapeDtypeStruct((s, positions // s, width), BF16) for s in (SA, SB)],
+        ],
+        scratch_shapes=[
+            pltpu.VMEM((length, width), BF16), pltpu.VMEM((width // LANES, length, LANES), F32),
+        ],
         compiler_params=pltpu.CompilerParams(vmem_limit_bytes=VMEM_LIMIT),
         name="front",
     )(signal, flags, marks_row, weight)
@@ -168,47 +185,43 @@
 
     @pl.when(step < down_steps)
     def _():
-        sums = total[...]
-        for k in range(step_taps):
-            rows = picked(seasonal_ref, pl.ds(step * step_taps + k, blocks, stride=stride))
-            sums = sums + nn(rows.astype(BF16), down_ref[k * width : (k + 1) * width, :])
-        total[...] = sums
+        rows = jnp.concatenate([seasonal_ref[k] for k in range(step_taps)], axis=1)
+        total[...] += nn(rows, down_ref[...])
 
     @pl.when(step == down_steps - 1)
     def _():
         active = jnp.tanh(total[...])
         act_ref[...] = active
+        joined_ref[1] = active.astype(BF16)
         total[...] = jnp.zeros_like(total)
 
     @pl.when(jnp.logical_and(step >= down_steps, step < down_steps + iso_steps))
     def _():
-        sums = total[...]
+        pieces = []
         for k in range(step_taps):
             back = taps - 1 - ((step - down_steps) * step_taps + k)
             rows = pltpu.roll(act_ref[...], back, 0)
-            rows = jnp.where(since_ref[...] >= back, rows, 0.0).astype(BF16)
-            sums = sums + nn(rows, iso_ref[k * width : (k + 1) * width, :])
-        total[...] = sums
+            pieces.append(jnp.where(since_ref[...] >= back, rows, 0.0).astype(BF16))
+        total[...] += nn(jnp.concatenate(pieces, axis=1), iso_ref[...])
 
     @pl.when(step == down_steps + iso_steps - 1)
     def _():
         second = jnp.tanh(total[...])
         second_ref[...] = second
         unit, _ = norm_parts(second + act_ref[...])
-        joined_ref[...] = (unit * gain_ref[0:1, :]).astype(BF16)
+        joined_ref[0] = (unit * gain_ref[0:1, :]).astype(BF16)
 
     @pl.when(step >= down_steps + iso_steps)
     def _():
         for k in range(step_taps):
-            lifted = nn(joined_ref[...], up_ref[:, k * width : (k + 1) * width])
+            lifted = nn(joined_ref[0], up_ref[:, k * width : (k + 1) * width])
             lifted_ref[k] = jnp.tanh(lifted).astype(BF16)
 
 
 def scale_forward(seasonal, down, iso, up, since, gains, stride):
-    width, positions = down.shape[1], seasonal.shape[1]
-    blocks = positions // stride
+    _, blocks, width = seasonal.shape
     taps = iso.shape[0] // width
-    step_taps = 2
+    step_taps = STEP_TAPS
     ds, isteps = stride // step_taps, taps // step_taps
     whole = lambda shape: pl.BlockSpec(
         shape, lambda t: (0,) * len(shape), pipeline_mode=pl.Buffered(1)
@@ -218,7 +231,7 @@
         functools.partial(scale_forward_kernel, stride, taps, step_taps),
         grid=(2 * ds + isteps,),
         in_specs=[
-            whole(seasonal.shape),
+            pl.BlockSpec((step_taps, blocks, width), lambda t: (clip(t, ds - 1), 0, 0)),
             pl.BlockSpec((step_taps * width, width), lambda t: (clip(t, ds - 1), 0)),
             pl.BlockSpec((step_taps * width, width), lambda t: (clip(t - ds, isteps - 1), 0)),
             pl.BlockSpec((width, step_taps * width), lambda t: (0, clip(t - ds - isteps, ds - 1))),
@@ -231,13 +244,13 @@
             ),
             pl.BlockSpec((blocks, width), lambda t: (0, 0)),
             pl.BlockSpec((blocks, width), lambda t: (0, 0)),
-            pl.BlockSpec((blocks, width), lambda t: (0, 0)),
+            pl.BlockSpec((2, blocks, width), lambda t: (0, 0, 0)),
         ],
         out_shape=[
             jax.ShapeDtypeStruct((stride, blocks, width), BF16),
             jax.ShapeDtypeStruct((blocks, width), F32),
             jax.ShapeDtypeStruct((blocks, width), F32),
-            jax.ShapeDtypeStruct((blocks, width), BF16),
+            jax.ShapeDtypeStruct((2, blocks, width), BF16),
         ],
         scratch_shapes=[pltpu.VMEM((blocks, width), F32)],
         compiler_params=pltpu.CompilerParams(vmem_limit_bytes=VMEM_LIMIT),
@@ -276,7 +289,7 @@
 
     def part(at, carry):
         rows = pl.ds(pl.multiple_of(at * tile, tile), tile)
-        seasonal = picked(seasonal_ref, rows)
+        seasonal = seasonal_ref[rows, :]
         unit_a, scale_a = norm_parts(picked(wide_a, rows) + seasonal)
         unit_b, scale_b = norm_parts(picked(wide_b, rows) + seasonal)
         branch_a = (unit_a * gain_0).astype(BF16)
@@ -393,8 +406,7 @@
         grid=(positions // length,),
         in_specs=[
             by_tap(stride_a, per_a), by_tap(stride_b, per_b),
-            pl.BlockSpec((width // LANES, length, LANES), lambda i: (0, i, 0)), by_row(width),
-            by_row(outs), fixed(merge.shape), fixed(ff_in.shape), fixed(ff_out.shape),
+            by_row(width), by_row(width), by_row(outs), fixed(merge.shape), fixed(ff_in.shape), fixed(ff_out.shape),
             fixed(head.shape), fixed(gains.shape), pl.BlockSpec(memory_space=pltpu.SMEM),
         ],
         out_specs=[
@@ -428,7 +440,7 @@
 def scale_backward_kernel(
     stride, taps, step_taps,
     pre_ref, up_ref, iso_ref, down_ref, act_ref, second_ref, since_ref, gain_ref,
-    iso_pre_ref, down_pre_ref, block_ref, gain_out,
+    both_pre_ref, block_ref, gain_out,
     total, spread,
 ):
     step = pl.program_id(0)
@@ -442,10 +454,8 @@
 
     @pl.when(step < up_steps)
     def _():
-        sums = total[...]
-        for k in range(step_taps):
-            sums = sums + nt(pre_ref[k], up_ref[:, k * width : (k + 1) * width])
-        total[...] = sums
+        rows = jnp.concatenate([pre_ref[k] for k in range(step_taps)], axis=1)
+        total[...] += nt(rows, up_ref[...])
 
     @pl.when(step == up_steps - 1)
     def _():
@@ -453,34 +463,36 @@
         unit, scale = norm_parts(second + act_ref[...])
         sum_grad, gain_grad = norm_back(total[...], unit, scale, gain_ref[0:1, :])
         gain_out[...] = gain_grad
-        iso_pre_ref[...] = (sum_grad * (1.0 - second * second)).astype(BF16)
+        both_pre_ref[0] = (sum_grad * (1.0 - second * second)).astype(BF16)
         spread[...] = sum_grad
 
     @pl.when(jnp.logical_and(step >= up_steps, step < up_steps + iso_steps))
     def _():
+        sums = spread[...]
         for k in range(step_taps):
             back = taps - 1 - ((step - up_steps) * step_taps + k)
-            grad = nt(iso_pre_ref[...], iso_ref[k * width : (k + 1) * width, :])
+            grad = nt(both_pre_ref[0], iso_ref[k * width : (k + 1) * width, :])
             grad = jnp.where(since_ref[...] >= back, grad, 0.0)
-            spread[...] += pltpu.roll(grad, blocks - back, 0)
+            sums = sums + pltpu.roll(grad, blocks - back, 0)
+        spread[...] = sums
 
     @pl.when(step == up_steps + iso_steps - 1)
     def _():
         active = act_ref[...]
-        down_pre_ref[...] = (spread[...] * (1.0 - active * active)).astype(BF16)
+        both_pre_ref[1] = (spread[...] * (1.0 - active * active)).astype(BF16)
 
     @pl.when(step >= up_steps + iso_steps)
     def _():
         for k in range(step_taps):
             block_ref[k] = nt(
-                down_pre_ref[...], down_ref[k * width : (k + 1) * width, :]
+                both_pre_ref[1], down_ref[k * width : (k + 1) * width, :]
             ).astype(BF16)
 
 
 def scale_backward(pre, up, iso, down, act, second, since, gains):
     stride, blocks, width = pre.shape
     taps = iso.shape[0] // width
-    step_taps = 2
+    step_taps = STEP_TAPS
     us, isteps = stride // step_taps, taps // step_taps
     whole = lambda shape: pl.BlockSpec(
         shape, lambda t: (0,) * len(shape), pipeline_mode=pl.Buffered(1)
@@ -499,16 +511,14 @@
             whole(act.shape), whole(second.shape), whole(since.shape), whole(gains.shape),
         ],
         out_specs=[
-            pl.BlockSpec((blocks, width), lambda t: (0, 0)),
-            pl.BlockSpec((blocks, width), lambda t: (0, 0)),
+            pl.BlockSpec((2, blocks, width), lambda t: (0, 0, 0)),
             pl.BlockSpec(
                 (step_taps, blocks, width), lambda t: (clip(t - us - isteps, us - 1), 0, 0)
             ),
             pl.BlockSpec((1, width), lambda t: (0, 0)),
         ],
         out_shape=[
-            jax.ShapeDtypeStruct((blocks, width), BF16),
-            jax.ShapeDtypeStruct((blocks, width), BF16),
+            jax.ShapeDtypeStruct((2, blocks, width), BF16),
             jax.ShapeDtypeStruct((stride, blocks, width), BF16),
             jax.ShapeDtypeStruct((1, width), F32),
         ],
@@ -525,57 +535,69 @@
     )
 
 
-def up_grad_kernel(order, mine_ref, own_joined, other_joined, own_pre, other_pre, out_ref, turned):
-    blocks = own_joined.shape[0]
+def up_grad_kernel(
+    orders, mine_ref, own_joined, other_joined, own_pre, other_pre, *rest,
+):
+    *out_refs, turned = rest
+    blocks = own_joined.shape[1]
 
     @pl.when(jnp.logical_and(pl.program_id(0) == 0, pl.program_id(1) == 0))
     def _():
-        turned[:, :blocks] = flip(own_joined[...])
-        turned[:, blocks:] = flip(other_joined[...])
+        turned[:, :blocks] = flip(own_joined[0])
+        turned[:, blocks:] = flip(other_joined[0])
 
     rows = jnp.concatenate([own_pre[0], other_pre[0]], axis=0)
     product = nn(turned[...], rows).astype(BF16)
-    panels, height, _ = out_ref.shape[4:]
-    for r in range(ROW_PARTS):
-        for p in range(panels):
-            out_ref[(*part_at(order, r, 0), p)] = product[
-                r * height : (r + 1) * height, p * LANES : (p + 1) * LANES
-            ]
-
-
-def up_grad(mine, joined, pre, order):
+    panels, height, _ = out_refs[0].shape[4:]
+    for piece, (order, out_ref) in enumerate(zip(orders, out_refs)):
+        for r in range(ROW_PARTS):
+            for p in range(panels):
+                low = (piece * panels + p) * LANES
+                out_ref[(*part_at(order, r, 0), p)] = product[
+                    r * height : (r + 1) * height, low : low + LANES
+                ]
+
+
+def up_grad(mine, joined, pre, orders):
     stride, blocks, width = pre[0].shape
-    taps, panels = stride // COLUMN_PARTS, width // LANES
+    taps, panels = stride // COLUMN_PARTS, width // (LANES * len(orders))
     half = COLUMN_PARTS // 2
     height = width // ROW_PARTS
-    sizes = tuple(1 if label == "x" else 2 for label in ORDERS[order])
-    joined_spec = pl.BlockSpec((blocks, width), lambda x, j, mine: (0, 0))
+
+    def out_spec(order):
+        sizes = tuple(1 if label == "x" else 2 for label in ORDERS[order])
+        return pl.BlockSpec(
+            (*sizes, panels, height, LANES),
+            lambda x, j, mine: (
+                *[x if label == "x" else 0 for label in ORDERS[order]], j, 0, 0
+            ),
+        )
+
+    joined_spec = pl.BlockSpec((1, blocks, width), lambda x, j, mine: (0, 0, 0))
     pre_spec = pl.BlockSpec(
         (1, blocks, width), lambda x, j, mine: ((2 * x + mine[0]) * taps + j, 0, 0)
     )
     return pl.pallas_call(
-        functools.partial(up_grad_kernel, order),
+        functools.partial(up_grad_kernel, orders),
         grid_spec=split_spec(
             (half, taps),
             [joined_spec, joined_spec, pre_spec, pre_spec],
-            pl.BlockSpec(
-                (*sizes, panels, height, LANES),
-                lambda x, j, mine: (
-                    *[x if label == "x" else 0 for label in ORDERS[order]], j, 0, 0
-                ),
-            ),
+            [out_spec(order) for order in orders],
             [pltpu.VMEM((width, 2 * blocks), BF16)],
         ),
-        out_shape=jax.ShapeDtypeStruct((2, 2, 2, 2, taps * panels, height, LANES), BF16),
+        out_shape=[
+            jax.ShapeDtypeStruct((2, 2, 2, 2, taps * panels, height, LANES), BF16)
+            for _ in orders
+        ],
         compiler_params=pltpu.CompilerParams(vmem_limit_bytes=VMEM_LIMIT),
         name="up_grad",
     )(mine, *joined, *pre)
 
 
-def turn_half(turned, own_pre, other_pre, mine):
-    blocks = own_pre.shape[0]
+def turn_half(turned, own_pre, other_pre, which, mine):
+    blocks = own_pre.shape[1]
     for side, pre_ref in enumerate((own_pre, other_pre)):
-        flipped = flip(pre_ref[...])
+        flipped = flip(pre_ref[which])
         there = slice(side * blocks, (side + 1) * blocks)
         for x in range(COLUMN_PARTS // 2):
             even = flipped[2 * x * LANES : (2 * x + 1) * LANES, :]
@@ -622,11 +644,14 @@
     whole = lambda shape: pl.BlockSpec(
         shape, lambda t, mine: (0,) * len(shape), pipeline_mode=pl.Buffered(1)
     )
+    tapped = pl.BlockSpec((taps // GRAD_STEPS, blocks, width), lambda t, mine: (t, 0, 0))
     specs, shapes = zip(*[grad_output(taps, width, order, len(orders)) for order in orders])
     return pl.pallas_call(
         kernel,
         grid_spec=split_spec(
-            (GRAD_STEPS,), [whole(value.shape) for value in arguments], list(specs),
+            (GRAD_STEPS,),
+            [tapped if value.shape[0] == taps else whole(value.shape) for value in arguments],
+            list(specs),
             [pltpu.VMEM((width // 2, 2 * blocks), BF16)],
         ),
         out_shape=list(shapes),
@@ -644,13 +669,14 @@
 
     @pl.when(step == 0)
     def _():
-        turn_half(turned, own_pre, other_pre, mine_ref[0])
+        turn_half(turned, own_pre, other_pre, 0, mine_ref[0])
 
     for k in range(step_taps):
         back = taps - 1 - (step * step_taps + k)
         rows = []
         for act_ref, since_ref in ((own_act, own_since), (other_act, other_since)):
-            moved = pltpu.roll(act_ref[...], back, 0)
+            act = act_ref[1] if len(act_ref.shape) == 3 else act_ref[...]
+            moved = pltpu.roll(act.astype(F32), back, 0)
             rows.append(jnp.where(since_ref[...] >= back, moved, 0.0).astype(BF16))
         rows = jnp.concatenate(rows, axis=0)
         store_parts(orders, out_refs, k, nn(turned[...], rows).astype(BF16))
@@ -668,24 +694,20 @@
     stride, orders, mine_ref, own_pre, other_pre, own_seasonal, other_seasonal, *rest
 ):
     *out_refs, turned = rest
-    step = pl.program_id(0)
-    blocks = own_pre.shape[0]
     step_taps = stride // GRAD_STEPS
 
-    @pl.when(step == 0)
-    def _():
-        turn_half(turned, own_pre, other_pre, mine_ref[0])
+    @pl.when(pl.program_id(0) == 0)
+    def _():
+        turn_half(turned, own_pre, other_pre, 1, mine_ref[0])
 
     for k in range(step_taps):
-        there = pl.ds(step * step_taps + k, blocks, stride=stride)
-        rows = [picked(ref, there).astype(BF16) for ref in (own_seasonal, other_seasonal)]
-        rows = jnp.concatenate(rows, axis=0)
+        rows = jnp.concatenate([own_seasonal[k], other_seasonal[k]], axis=0)
         store_parts(orders, out_refs, k, nn(turned[...], rows).astype(BF16))
 
 
 def down_grad(mine, pre, seasonal, orders):
-    blocks, width = pre[0].shape
-    stride = seasonal[0].shape[1] // blocks
+    _, blocks, width = pre[0].shape
+    stride = seasonal[0].shape[0]
     kernel = functools.partial(down_grad_kernel, stride, orders)
     return grad_call(
         kernel, "down_grad", stride, width, blocks, orders, (*pre, *seasonal), mine
@@ -846,44 +868,170 @@
         return lax.optimization_barrier((small, *self.last))[0]
 
 
+LINKS = ("x", "y", "near", "far")
+
+
+class Place:
+    def __init__(self, base=0, times=()):
+        self.base, self.times = base, dict(times)
+
+    def plus(self, base, label=None, times=0):
+        moved = Place(self.base + base, self.times)
+        if label is not None:
+            moved.times[label] = moved.times.get(label, 0) + times
+        return moved
+
+    def value(self, bits_ref):
+        line = jnp.int32(self.base)
+        for label, times in self.times.items():
+            line = line + bits_ref[LINKS.index(label)] * times
+        return pl.multiple_of(line, LANES)
+
+
 class Halving:
-    def __init__(self, turns, order):
-        self.turns, self.left, self.order = turns, list(ORDERS[order]), order
-
-    def start(self, *terms):
-        self.lines = terms[0].size // (16 * LANES)
+    def __init__(self, order):
+        self.left = list(ORDERS[order])
+
+    def start(self, *terms, lines=None):
+        self.lines = lines or terms[0].size // (16 * LANES)
         self.terms = [term.reshape(-1, LANES) for term in terms]
-        self.places = [jnp.int32(0)] * len(terms)
-
-    def total(self, offset, lines):
-        pieces = [
-            lax.dynamic_slice(values, (place + offset, 0), (lines, LANES)).astype(F32)
-            for values, place in zip(self.terms, self.places)
-        ]
-        return functools.reduce(jnp.add, pieces)
-
-    def step(self):
-        label = self.left.pop(0)
-        lines = self.lines << len(self.left)
-        mine = self.turns.after(own_bit(label))
-        sent = self.total((1 - mine) * lines, lines).astype(BF16)
-        self.turns.seen(sent)
-        self.places = [place + mine * lines for place in self.places] + [jnp.int32(0)]
-        self.terms.append(cross(sent, label))
-
-    def finish(self):
-        while self.left:
-            self.step()
-        return self.total(0, self.lines)
-
-
-def by_columns(parts):
-    return parts.reshape(-1, LANES, LANES).transpose(0, 2, 1).reshape(-1, LANES)
-
-
-def by_features(parts, height):
-    panels = parts.reshape(-1, height, LANES)
-    return panels.transpose(1, 0, 2).reshape(height, -1)
+        self.places = [Place() for _ in terms]
+
+
+def fetch_terms(bits_ref, term_refs, terms, store, sems):
+    copies, at = [], 0
+    for n, (array, place, lines) in enumerate(terms):
+        copy = pltpu.make_async_copy(
+            term_refs[array].at[pl.ds(place.value(bits_ref), lines)],
+            store.at[pl.ds(at, lines)], sems.at[n],
+        )
+        copy.start()
+        copies.append((copy, at))
+        at += lines
+    return copies
+
+
+def sum_lines(store, starts, line, count):
+    total = store[pl.ds(starts[0] + line, count), :].astype(F32)
+    for start in starts[1:]:
+        total = total + store[pl.ds(start + line, count), :].astype(F32)
+    return total
+
+
+def send_kernel(plan, unique, bits_ref, *refs):
+    term_refs = refs[:unique]
+    out_refs, (store, sems) = refs[unique:-2], refs[-2:]
+    terms = [term for _, _, _, group in plan for term in group]
+    copies = fetch_terms(bits_ref, term_refs, terms, store, sems)
+    for out, at, lines, group in plan:
+        mine, copies = copies[: len(group)], copies[len(group) :]
+        for copy, _ in mine:
+            copy.wait()
+        starts = [start for _, start in mine]
+        out_ref = out_refs[out]
+
+        def part(n, carry, at=at, starts=starts, out_ref=out_ref):
+            line = pl.multiple_of(n * LANES, LANES)
+            there = pl.ds(pl.multiple_of(at + line, LANES), LANES)
+            out_ref[there, :] = sum_lines(store, starts, line, LANES).astype(BF16)
+            return carry
+
+        lax.fori_loop(0, lines // LANES, part, 0)
+
+
+def unique_arrays(lists):
+    arrays, where = [], []
+    for values in lists:
+        places = []
+        for value in values:
+            at = [n for n, one in enumerate(arrays) if one is value]
+            if not at:
+                at = [len(arrays)]
+                arrays.append(value)
+            places.append(at[0])
+        where.append(places)
+    return arrays, where
+
+
+def call_with_terms(kernel, bits, arrays, lines, copies, out_shape, name):
+    return pl.pallas_call(
+        kernel,
+        grid_spec=pltpu.PrefetchScalarGridSpec(
+            num_scalar_prefetch=1, grid=(1,),
+            in_specs=[pl.BlockSpec(memory_space=pl.ANY)] * len(arrays),
+            out_specs=[
+                pl.BlockSpec(one.shape, lambda t, bits: (0, 0), pipeline_mode=pl.Buffered(1))
+                for one in out_shape
+            ],
+            scratch_shapes=[
+                pltpu.VMEM((lines, LANES), BF16), pltpu.SemaphoreType.DMA((copies,)),
+            ],
+        ),
+        out_shape=out_shape,
+        compiler_params=pltpu.CompilerParams(vmem_limit_bytes=VMEM_LIMIT),
+        name=name,
+    )(bits, *arrays)
+
+
+def step_together(turns, bits, chains):
+    arrays, where = unique_arrays([one.terms for one in chains])
+    by_label, plan, moves = {}, [], []
+    for one, places in zip(chains, where):
+        label = one.left.pop(0)
+        lines = one.lines << len(one.left)
+        out = list(by_label).index(label) if label in by_label else len(by_label)
+        at = by_label.get(label, 0)
+        by_label[label] = at + lines
+        away = [place.plus(lines, label, -lines) for place in one.places]
+        plan.append((out, at, lines, [(n, p, lines) for n, p in zip(places, away)]))
+        moves.append((one, label, out, at, lines))
+    terms = [term for entry in plan for term in entry[3]]
+    sent = call_with_terms(
+        functools.partial(send_kernel, plan, len(arrays)), turns.after(bits), arrays,
+        sum(lines for _, _, lines in terms), len(terms),
+        [jax.ShapeDtypeStruct((lines, LANES), BF16) for lines in by_label.values()], "send",
+    )
+    turns.seen(*sent)
+    got = [cross(values, label) for values, label in zip(sent, by_label)]
+    for one, label, out, at, lines in moves:
+        one.places = [place.plus(0, label, lines) for place in one.places] + [Place(at)]
+        one.terms.append(got[out])
+    return got
+
+
+def finish_kernel(plan, unique, bits_ref, *refs):
+    term_refs = refs[:unique]
+    out_refs, (store, sems) = refs[unique:-2], refs[-2:]
+    terms = [term for group, _ in plan for term in group]
+    copies = fetch_terms(bits_ref, term_refs, terms, store, sems)
+    for group, pieces in plan:
+        mine, copies = copies[: len(group)], copies[len(group) :]
+        for copy, _ in mine:
+            copy.wait()
+        starts = [start for _, start in mine]
+        line = 0
+        for out, height, panels in pieces:
+            for p in panels:
+                block = sum_lines(store, starts, line, height)
+                there = slice(p * LANES, (p + 1) * LANES)
+                if height == LANES:
+                    out_refs[out][there, :] = block.T
+                else:
+                    out_refs[out][:, there] = block
+                line += height
+
+
+def finish_together(bits, chains, shapes, pieces):
+    arrays, where = unique_arrays([one.terms for one in chains])
+    plan = []
+    for one, places, mine in zip(chains, where, pieces):
+        plan.append(([(n, p, one.lines) for n, p in zip(places, one.places)], mine))
+    terms = [term for entry in plan for term in entry[0]]
+    return call_with_terms(
+        functools.partial(finish_kernel, plan, len(arrays)), bits, arrays,
+        sum(lines for _, _, lines in terms), len(terms),
+        [jax.ShapeDtypeStruct(shape, F32) for shape in shapes], "finish",
+    )
 
 
 def other_core(values):
@@ -919,8 +1067,8 @@
     return scattered(panels.transpose(0, 3, 1, 2, 4).reshape(ROW_PARTS * height, -1))
 
 
-def sum_everywhere(values):
-    for label in BITS:
+def sum_over(values, *labels):
+    for label in labels:
         values = values + cross(values, label)
     return values
 
@@ -938,7 +1086,10 @@
     groups = local_groups * columns
     time_rows = local_rows // columns
     width = norm_gains.shape[1]
-    embed_all, head_all = lax.all_gather((embed_weight, head_weight), "var", axis=0, tiled=True)
+    both_weights = jnp.concatenate([embed_weight, head_weight.transpose(0, 2, 1)], axis=1)
+    both_weights = lax.all_gather(both_weights, "var", axis=0, tiled=True)
+    taps = embed_weight.shape[1]
+    embed_all, head_all = both_weights[:, :taps], both_weights[:, taps:].transpose(0, 2, 1)
     cotangent = lax.all_to_all(
         estimate_cotangent, "var", split_axis=0, concat_axis=2, tiled=True
     ).reshape(-1, variates)
@@ -952,17 +1103,18 @@
     signal = lax.dynamic_slice_in_dim(signal_matrix, var_index * time_rows, time_rows, 0)
     signal = signal.reshape(-1, variates)
     marks = lax.dynamic_slice_in_dim(frame_numbers, var_index * time_rows, time_rows, 0)
+    marks = lax.optimization_barrier(marks)
     flags = window_flags(marks)
     marks_row = marks.astype(F32).reshape(time_rows, 1, length)
     since_a = blocks_since_start(marks, SA, iso_a.shape[0] // width)
     since_b = blocks_since_start(marks, SB, iso_b.shape[0] // width)
 
-    trend, seasonal = front(signal, flags, marks_row, by_signal, length)
+    trend, seasonal, taps_of_a, taps_of_b = front(signal, flags, marks_row, by_signal, length)
     lifted_a, act_a, second_a, joined_a = scale_forward(
-        seasonal, down_a, iso_a, up_a, since_a, norm_gains, SA
+        taps_of_a, down_a, iso_a, up_a, since_a, norm_gains, SA
     )
     lifted_b, act_b, second_b, joined_b = scale_forward(
-        seasonal, down_b, iso_b, up_b, since_b, norm_gains, SB
+        taps_of_b, down_b, iso_b, up_b, since_b, norm_gains, SB
     )
     mixing = rows == ROW_PARTS and columns == COLUMN_PARTS
     mine = own_bit("core").reshape(1)
@@ -972,26 +1124,30 @@
     )
     since_a = (since_a, blocks_since_start(pair_marks, SA, iso_a.shape[0] // width))
     since_b = (since_b, blocks_since_start(pair_marks, SB, iso_b.shape[0] // width))
-    seasonal_pair, act_pair_a, act_pair_b = pair(seasonal), pair(act_a), pair(act_b)
+    taps_pair_a, taps_pair_b = pair(taps_of_a), pair(taps_of_b)
     joined_pair_a, joined_pair_b = pair(joined_a), pair(joined_b)
+    act_pair_a, act_pair_b = (act_a, joined_pair_a[1]), (act_b, joined_pair_b[1])
     predicted, pre_a, pre_b, sres, late_parts, head_full, gains_late = tail(
         lifted_a, lifted_b, seasonal, trend, cotangent, merge_weight, ff_in, ff_out,
         head_matrix, norm_gains, mine, length,
     )
     turns = Turns()
+    bits = jnp.stack([own_bit(label) for label in LINKS]).astype(jnp.int32)
     orders = {
-        "late": ("z",), "up_b": ("x",), "up_a": ("y",), "iso_a": ("z", "x"), "down_a": ("y",),
-        "iso_b": ("x",), "down_b": ("y", "z"),
+        "late": ("nxy",), "up_b": ("xny", "yxn"), "up_a": ("xyn", "yxn"),
+        "iso_a": ("nyx", "ynx"), "down_a": ("yxn",), "iso_b": ("xyn",),
+        "down_b": ("nyx", "xny"),
     }
     chains = {
-        name: [Halving(turns, order) for order in pieces] for name, pieces in orders.items()
+        name: [Halving(order) for order in pieces] for name, pieces in orders.items()
     }
     done = {}
 
-    def go(*names):
-        for name in names if mixing else ():
-            for one in chains[name]:
-                one.step()
+    def go(*names, through=False):
+        if mixing:
+            got = step_together(turns, bits, [one for name in names for one in chains[name]])
+            if through:
+                turns.seen(*turns.last, *got)
 
     def produced(name, *pieces):
         done[name] = pieces
@@ -1003,36 +1159,41 @@
         return turns.after(mine)
 
     taps_a, taps_b = iso_a.shape[0] // width, iso_b.shape[0] // width
-    turns.seen(late_parts)
+    turns.seen(
+        late_parts, taps_pair_a[1], taps_pair_b[1], joined_pair_a[1], joined_pair_b[1]
+    )
     done["late"] = (late_parts,)
+    late_lines = late_parts.shape[-2]
     if mixing:
-        chains["late"][0].start(late_parts[0], cross(late_parts[1].reshape(-1, LANES), "core"))
+        chains["late"][0].start(
+            late_parts, cross(late_parts[1].reshape(-1, LANES), "core"), lines=late_lines
+        )
     pre_pair_b, pre_pair_a = pair(pre_b), pair(pre_a)
-    iso_pre_a, down_pre_a, block_a, gain_a = scale_backward(
+    both_pre_a, block_a, gain_a = scale_backward(
         pre_a, up_a, iso_a, down_a, act_a, second_a, since_a[0], turns.after(norm_gains)
     )
-    turns.seen(iso_pre_a)
-    iso_pre_pair_a, down_pre_pair_a = pair(iso_pre_a), pair(down_pre_a)
+    turns.seen(both_pre_a)
+    both_pre_pair_a = pair(both_pre_a)
     go("late")
-    produced("up_b", up_grad(turn(), joined_pair_b, pre_pair_b, "x"))
+    produced("up_b", *up_grad(turn(), joined_pair_b, pre_pair_b, orders["up_b"]))
     go("up_b")
-    produced("up_a", up_grad(turn(), joined_pair_a, pre_pair_a, "y"))
+    produced("up_a", *up_grad(turn(), joined_pair_a, pre_pair_a, orders["up_a"]))
     go("up_a")
-    iso_pre_b, down_pre_b, block_b, gain_b = scale_backward(
+    both_pre_b, block_b, gain_b = scale_backward(
         pre_b, up_b, iso_b, down_b, act_b, second_b, since_b[0], turns.after(norm_gains)
     )
-    turns.seen(iso_pre_b)
-    iso_pre_pair_b, down_pre_pair_b = pair(iso_pre_b), pair(down_pre_b)
+    turns.seen(both_pre_b)
+    both_pre_pair_b = pair(both_pre_b)
     produced(
-        "iso_a", *iso_grad(turn(), iso_pre_pair_a, act_pair_a, since_a, taps_a, orders["iso_a"])
-    )
-    produced("down_a", *down_grad(turn(), down_pre_pair_a, seasonal_pair, orders["down_a"]))
-    go("late", "up_b", "up_a", "iso_a", "down_a")
+        "iso_a", *iso_grad(turn(), both_pre_pair_a, act_pair_a, since_a, taps_a, orders["iso_a"])
+    )
+    go("late", "up_b", "up_a", "iso_a")
+    produced("down_a", *down_grad(turn(), both_pre_pair_a, taps_pair_a, orders["down_a"]))
     produced(
-        "iso_b", *iso_grad(turn(), iso_pre_pair_b, act_pair_b, since_b, taps_b, orders["iso_b"])
-    )
-    produced("down_b", *down_grad(turn(), down_pre_pair_b, seasonal_pair, orders["down_b"]))
-    go("late", "up_b", "up_a", "iso_b", "down_b")
+        "iso_b", *iso_grad(turn(), both_pre_pair_b, act_pair_b, since_b, taps_b, orders["iso_b"])
+    )
+    produced("down_b", *down_grad(turn(), both_pre_pair_b, taps_pair_b, orders["down_b"]))
+    go("late", "up_b", "up_a", "iso_a", "down_a", "iso_b", "down_b")
     series_grad, embed_full = back(
         sres, block_a, block_b, cotangent, head_matrix, signal, flags, marks_row,
         turns.after(by_group), length
@@ -1049,7 +1210,12 @@
     outward = lax.all_to_all(outward, "var", split_axis=3, concat_axis=1, tiled=True)
     small = (embed_grad, head_grad, gains_grad)
     if mixing:
-        flat = sum_everywhere(jnp.concatenate([part.reshape(-1, LANES) for part in small]))
+        flat = jnp.concatenate([part.reshape(-1, LANES) for part in small])
+        flat = sum_over(flat, "core", "x")
+        turns.seen(flat)
+        go("late", "up_b", "up_a", "iso_a", "down_a", "iso_b", "down_b", through=True)
+        flat = sum_over(flat, "y", "near", "far")
+        turns.seen(*turns.last, flat)
         pieces, at = [], 0
         for part in small:
             lines = part.size // LANES
@@ -1065,14 +1231,47 @@
     merge_lines = merge_weight.size // (ROW_PARTS * COLUMN_PARTS * LANES)
     in_lines = ff_in.size // (ROW_PARTS * COLUMN_PARTS * LANES)
     if mixing:
-        go("iso_a", "down_a", "late", "up_b", "up_a", "iso_b", "down_b")
-        go("iso_a", "down_a", "iso_b", "down_b", "iso_a", "down_a", "iso_b", "down_b")
-        total = {
-            name: jnp.concatenate([one.finish() for one in pieces])
-            for name, pieces in chains.items()
-        }
-        late = total["late"]
-        turned, kept = by_columns, by_features
+        go("iso_a", "down_a", "iso_b", "down_b", through=True)
+        go("down_a", "iso_b", "down_b")
+
+        def turned(out, one, first=0):
+            return out, LANES, range(first, first + one.lines // LANES)
+
+        def kept(out, one, piece):
+            half = width // LANES // 2
+            count = one.lines // height
+            return out, height, [2 * half * (p // half) + half * piece + p % half for p in range(count)]
+
+        late, down_a_one, iso_b_one = [
+            chains[name][0] for name in ("late", "down_a", "iso_b")
+        ]
+        first_a, second_a = chains["iso_a"]
+        first_b, second_b = chains["down_b"]
+        shard = lambda weight: (weight.shape[0] // rows, weight.shape[1] // columns)
+        ups = finish_together(
+            turns.after(bits), [*chains["up_a"], *chains["up_b"], late],
+            [shard(weight) for weight in (up_a, up_b, merge_weight, ff_in, ff_out)],
+            [
+                *[[kept(0, one, n)] for n, one in enumerate(chains["up_a"])],
+                *[[kept(1, one, n)] for n, one in enumerate(chains["up_b"])],
+                [
+                    (2, LANES, range(merge_lines // LANES)),
+                    (3, height, range(in_lines // height)),
+                    (4, LANES, range((late.lines - merge_lines - in_lines) // LANES)),
+                ],
+            ],
+        )
+        turns.seen(*ups)
+        downs = finish_together(
+            turns.after(bits), [down_a_one, first_a, second_a, iso_b_one, first_b, second_b],
+            [shard(weight) for weight in (down_a, iso_a, iso_b, down_b)],
+            [
+                [turned(0, down_a_one)], [turned(1, first_a)],
+                [turned(1, second_a, first_a.lines // LANES)], [turned(2, iso_b_one)],
+                [turned(3, first_b)], [turned(3, second_b, first_b.lines // LANES)],
+            ],
+        )
+        summed = (downs[0], downs[1], ups[0], downs[3], downs[2], ups[1], *ups[2:])
     else:
         total = {}
         for name, pieces in done.items():
@@ -1080,19 +1279,23 @@
                 halves = [(pieces[0][0], pieces[0][1])]
             else:
                 halves = [(piece, jnp.zeros_like(piece)) for piece in pieces]
-            total[name] = jnp.concatenate(
-                [both_halves(*two, order, mine[0]) for two, order in zip(halves, orders[name])],
-                axis=1,
-            )
-        late = total["late"]
+            parts = [
+                both_halves(*two, order, mine[0]) for two, order in zip(halves, orders[name])
+            ]
+            if name.startswith("up"):
+                half = width * height // (2 * LANES)
+                parts = [part.reshape(part.shape[0], -1, half, LANES) for part in parts]
+                total[name] = jnp.concatenate(parts, axis=2)
+            else:
+                total[name] = jnp.concatenate(parts, axis=1)
         turned, kept = scattered_columns, scattered_features
-    split = (merge_lines, merge_lines + in_lines)
-    merge_part, in_part, out_part = jnp.split(late, split, axis=late.ndim - 2)
-    summed = (
-        turned(total["down_a"]), turned(total["iso_a"]), kept(total["up_a"], height),
-        turned(total["down_b"]), turned(total["iso_b"]), kept(total["up_b"], height),
-        turned(merge_part), kept(in_part, height), turned(out_part),
-    )
+        split = (merge_lines, merge_lines + in_lines)
+        merge_part, in_part, out_part = jnp.split(total["late"], split, axis=1)
+        summed = (
+            turned(total["down_a"]), turned(total["iso_a"]), kept(total["up_a"], height),
+            turned(total["down_b"]), turned(total["iso_b"]), kept(total["up_b"], height),
+            turned(merge_part), kept(in_part, height), turned(out_part),
+        )
     return (outward[0], outward[1], embed_sum, head_sum, *summed, gains_sum)
 
 

time: 575 us -> 518 us (0.901)
  other arithmetic: 71.5 us -> 4.81 us
  waiting for transfers between devices: 49.8 us -> 100 us
  local copies, waits for them, and re-layouts: 64.4 us -> 34.8 us
  Pallas kernels: 294 us -> 318 us
  starting transfers between devices: 64.2 us -> 40.6 us
  blocking collectives: 16.2 us -> 5.35 us
    convert_element_type x28 -> x0, other arithmetic: 54.9 us -> none  [step(): sent = self.total((1 - mine) * lines, lines).astype(BF16)]
    ppermute x42 -> x26, waiting for transfers between devices: 49.8 us -> 100 us  [cross(): return lax.ppermute(values, ('rows', 'var'), pairs)]
    pallas_call x6 -> x16, Pallas kernels: 58.8 us -> 100 us  [the longest x10 50.7 us: call_with_terms(): pl.pallas_call(kernel, grid_spec=pltpu.PrefetchScalarGridSpec(num_scalar_...]
    ppermute x42 -> x26, starting transfers between devices: 53 us -> 30.5 us  [cross(): return lax.ppermute(values, ('rows', 'var'), pairs)]
    dynamic_slice x8 -> x1, local copies, waits for them, and re-layouts: 20.3 us -> 0.82 us  [body(): lax.dynamic_slice_in_dim(frame_numbers, (var_index ^ 1) * time_rows, time...]
    pallas_call x2, Pallas kernels: 48.9 us -> 36.5 us  [scale_forward(): pl.pallas_call(functools.partial(scale_forward_kernel, stride, taps, step...]
    add x14 -> x5, other arithmetic: 11.6 us -> 0.03 us  [sum_over(): values = values + cross(values, label)]
    all_gather x2 -> x1, blocking collectives: 16.2 us -> 5.35 us  [body(): both_weights = lax.all_gather(both_weights, 'var', axis=0, tiled=True)]
  transfers between devices with their start and end apart: 55 -> 36, of which waited for: 11 -> 11; matrix products, arithmetic and copies ran while one was open for 24% -> 6% of each run, Pallas kernels for 52% -> 53%
where the time goes in v4:
time: 518 us; the launch traced here: 509 us
  Pallas kernels  318 us (61%)
  waiting for transfers between devices  100 us (19%)
  starting transfers between devices  40.6 us (8%)
  local copies, waits for them, and re-layouts  34.8 us (7%)
  blocking collectives  5.35 us (1%)
    pallas_call x1, Pallas kernels, tail(): pl.pallas_call(tail_kernel, grid=(positions // length,), in_specs=[by_tap...  112 us
    ppermute x26, waiting for transfers between devices, cross(): return lax.ppermute(values, ('rows', 'var'), pairs)  100 us
    pallas_call x10, Pallas kernels, call_with_terms(): pl.pallas_call(kernel, grid_spec=pltpu.PrefetchScalarGridSpec(num_scalar_...  50.7 us
    pallas_call x2, Pallas kernels, scale_backward(): pl.pallas_call(functools.partial(scale_backward_kernel, stride, taps, ste...  38.3 us
    pallas_call x2, Pallas kernels, scale_forward(): pl.pallas_call(functools.partial(scale_forward_kernel, stride, taps, step...  36.5 us
    pallas_call x4, Pallas kernels, grad_call(): pl.pallas_call(kernel, grid_spec=split_spec((GRAD_STEPS,), [tapped if val...  34.4 us
    ppermute x26, starting transfers between devices, cross(): return lax.ppermute(values, ('rows', 'var'), pairs)  30.5 us
    pallas_call x1, Pallas kernels, back(): pl.pallas_call(back_kernel, grid=(positions // length,), in_specs=[by_row...  16.6 us
  transfers between devices with their start and end apart: 36, of which 11 were waited for; matrix products, arithmetic and copies ran while one was open for 6% of the time, Pallas kernels for 53%

profile of v4, /device:TPU:0, one launch (start us, length us, event | category | flops | bytes accessed | tf_op | source)
XLA Modules:
  0.0 509.0 jit_solution(2638081421692241184)
XLA Ops:
  0.7 4.4 all-to-all-start
  8.0 5.3 %all_gather.3 = bf16[8,16,64]{2,1,0:T(8,128)(2,1)S(1)} all-gather(bf16[2,16,64]{2,1,0:T(8,128)(2,1)S(1)} %pad_maximum_fusion.4), channel_id=1, replica_groups=mesh['rows'=8,'var'=4] {'var'}, dimensions={0}, use_global_device_ids=true | all-gather | bytes 20480 | tf_op jit(solution)/shard_map/all_gather | solution.py:1090
  21.2 13.8 %front.1 = (f32[3072,512]{1,0:T(8,128)}, f32[3072,512]{1,0:T(8,128)}, bf16[12,256,512]{2,1,0:T(8,128)(2,1)}, bf16[16,192,512]{2,1,0:T(8,128)(2,1)}) custom-call(bf16[3072,32]{1,0:T(8,128)(2,1)} %bitcast.193, f32[3072,8]{1,0:T(8,128)} %copy.114.flags_ref, f32[4,1,768]{2,1,0:T(1,128)} %reshape.178.marks_ref, bf16[96,512]{1,0:T(8,128)(2,1)} %pad_maximum_fusion.1.weight_ref), custom_call_target="tpu_custom_call" | custom-call | tf_op jit(solution)/shard_map/front/pallas_call | solution.py:145
  36.5 18.7 %scale_forward.2 = (bf16[12,256,512]{2,1,0:T(8,128)(2,1)}, f32[256,512]{1,0:T(8,128)}, f32[256,512]{1,0:T(8,128)}, bf16[2,256,512]{2,1,0:T(8,128)(2,1)}) custom-call(bf16[12,256,512]{2,1,0:T(8,128)(2,1)} %get-tuple-element.95.seasonal_ref.own_seasonal, bf16[6144,512]{1,0:T(8,128)(2,1)} %down_ref.6, bf16[8192,512]{1,0:T(8,128)(2,1)} %iso_ref.6, ...), custom_call_target="tpu_custom_call" | custom-call | tf_op jit(solution)/shard_map/scale_forward/pallas_call | solution.py:230
  56.6 17.8 %scale_forward.3 = (bf16[16,192,512]{2,1,0:T(8,128)(2,1)}, f32[192,512]{1,0:T(8,128)}, f32[192,512]{1,0:T(8,128)}, bf16[2,192,512]{2,1,0:T(8,128)(2,1)}) custom-call(bf16[16,192,512]{2,1,0:T(8,128)(2,1)} %get-tuple-element.97.seasonal_ref.own_seasonal, bf16[8192,512]{1,0:T(8,128)(2,1)} %down_ref.7, bf16[6144,512]{1,0:T(8,128)(2,1)} %iso_ref.7, ...), custom_call_target="tpu_custom_call" | custom-call | tf_op jit(solution)/shard_map/scale_forward/pallas_call | solution.py:230
  76.9 112.0 %tail.1 = (f32[3072,32]{1,0:T(8,128)}, bf16[12,256,512]{2,1,0:T(8,128)(2,1)}, bf16[16,192,512]{2,1,0:T(8,128)(2,1)}, f32[3072,512]{1,0:T(8,128)}, bf16[2,2,2,2,2...) custom-call(bf16[12,256,512]{2,1,0:T(8,128)(2,1)} %get-tuple-element.96.lifted_a_ref, ...), custom_call_target="tpu_custom_call" | custom-call | tf_op jit(solution)/shard_map/tail/pallas_call | solution.py:404
  189.5 3.5 slice.317
  194.1 18.9 %scale_backward.2 = (bf16[2,256,512]{2,1,0:T(8,128)(2,1)}, bf16[12,256,512]{2,1,0:T(8,128)(2,1)}, f32[1,512]{1,0:T(1,128)}) custom-call(bf16[12,256,512]{2,1,0:T(8,128)(2,1)} %get-tuple-element.103.pre_ref.own_pre, bf16[512,6144]{1,0:T(8,128)(2,1)} %up_ref.6, bf16[8192,512]{1,0:T(8,128)(2,1)} %iso_ref.6, bf16[6144,512]{1,0:T(8,128)(2,1)} %down_ref.6, ...), custom_call_target="tpu_custom_call" | custom-call | tf_op jit(solution)/shard_map/scale_backward/pallas_call | solution.py:501
  214.8 4.0 send.8
  220.9 8.6 %up_grad.2 = (bf16[2,2,2,2,8,64,128]{6,5,4,3,2,1,0:T(8,128)(2,1)}, bf16[2,2,2,2,8,64,128]{6,5,4,3,2,1,0:T(8,128)(2,1)}) custom-call(s32[1]{0:T(128)} %bitcast.5.mine_ref, bf16[2,192,512]{2,1,0:T(8,128)(2,1)} %get-tuple-element.108.own_joined, bf16[2,192,512]{2,1,0:T(8,128)(2,1)} %copy-done.13, bf16[16,192,512]{2,1,0:T(8,128)(2,1)} %get-tuple-element.111.own_pre.pre_ref, ...), custom_call_target="tpu_custom_call" | custom-call | tf_op jit(solution)/shard_map/up_grad/pallas_call | solution.py:580
  229.4 3.9 send.9
  236.9 6.7 %up_grad.3 = (bf16[2,2,2,2,6,64,128]{6,5,4,3,2,1,0:T(8,128)(2,1)}, bf16[2,2,2,2,6,64,128]{6,5,4,3,2,1,0:T(8,128)(2,1)}) custom-call(s32[1]{0:T(128)} %bitcast.5.mine_ref, bf16[2,256,512]{2,1,0:T(8,128)(2,1)} %get-tuple-element.107.own_joined, bf16[2,256,512]{2,1,0:T(8,128)(2,1)} %copy-done.12, bf16[12,256,512]{2,1,0:T(8,128)(2,1)} %get-tuple-element.103.pre_ref.own_pre, ...), custom_call_target="tpu_custom_call" | custom-call | tf_op jit(solution)/shard_map/up_grad/pallas_call | solution.py:580
  248.9 19.4 %scale_backward.3 = (bf16[2,192,512]{2,1,0:T(8,128)(2,1)}, bf16[16,192,512]{2,1,0:T(8,128)(2,1)}, f32[1,512]{1,0:T(1,128)}) custom-call(bf16[16,192,512]{2,1,0:T(8,128)(2,1)} %get-tuple-element.111.own_pre.pre_ref, bf16[512,8192]{1,0:T(8,128)(2,1)} %up_ref.7, bf16[6144,512]{1,0:T(8,128)(2,1)} %iso_ref.7, bf16[8192,512]{1,0:T(8,128)(2,1)} %down_ref.7, ...), custom_call_target="tpu_custom_call" | custom-call | tf_op jit(solution)/shard_map/scale_backward/pallas_call | solution.py:501
  268.3 12.2 %iso_grad.2 = (bf16[2,2,2,2,4,128,128]{6,5,4,3,2,1,0:T(8,128)(2,1)}, bf16[2,2,2,2,4,128,128]{6,5,4,3,2,1,0:T(8,128)(2,1)}) custom-call(s32[1]{0:T(128)} %bitcast.5.mine_ref, bf16[2,256,512]{2,1,0:T(8,128)(2,1)} %get-tuple-element.114.own_pre, bf16[2,256,512]{2,1,0:T(8,128)(2,1)} %collective-permute-done.7.other_pre, ...), custom_call_target="tpu_custom_call" | custom-call | tf_op jit(solution)/shard_map/iso_grad/pallas_call | solution.py:649
  282.3 6.6 %send.11 = (bf16[6144,128]{1,0:T(8,128)(2,1)}, bf16[6144,128]{1,0:T(8,128)(2,1)}, bf16[5632,128]{1,0:T(8,128)(2,1)}) custom-call(s32[4]{0:T(128)} %pad_add_fusion.bits_ref, bf16[20480,128]{1,0:T(8,128)(2,1)} %bitcast.139, bf16[10240,128]{1,0:T(8,128)(2,1)} %copy-done.3, bf16[5120,128]{1,0:T(8,128)(2,1)} %copy-done.5, bf16[8192,128]{1,0:T(8,128)(2,1)} %bitcast.154, ...), custom_call_target="tpu_custom_call" | custom-call | tf_op jit(solution)/shard_map/send/pallas_call | solution.py:957
  293.8 6.6 %down_grad.2 = bf16[2,2,2,2,6,128,128]{6,5,4,3,2,1,0:T(8,128)(2,1)} custom-call(s32[1]{0:T(128)} %bitcast.5.mine_ref, bf16[2,256,512]{2,1,0:T(8,128)(2,1)} %get-tuple-element.114.own_pre, bf16[2,256,512]{2,1,0:T(8,128)(2,1)} %collective-permute-done.7.other_pre, bf16[12,256,512]{2,1,0:T(8,128)(2,1)} %get-tuple-element.95.seasonal_ref.own_seasonal, ...), custom_call_target="tpu_custom_call" | custom-call | tf_op jit(solution)/shard_map/down_grad/pallas_call | solution.py:649
  301.2 8.4 %iso_grad.3 = bf16[2,2,2,2,6,128,128]{6,5,4,3,2,1,0:T(8,128)(2,1)} custom-call(s32[1]{0:T(128)} %bitcast.5.mine_ref, bf16[2,192,512]{2,1,0:T(8,128)(2,1)} %get-tuple-element.130.own_pre, bf16[2,192,512]{2,1,0:T(8,128)(2,1)} %copy-done.14, f32[192,512]{1,0:T(8,128)} %get-tuple-element.112.act_ref.own_act, bf16[2,192,512]{2,1,0:T(8,128)(2,1)} %copy-done.13, ...), custom_call_target="tpu_custom_call" | custom-call | tf_op jit(solution)/shard_map/iso_grad/pallas_call | solution.py:649
  309.6 7.2 %down_grad.3 = (bf16[2,2,2,2,4,128,128]{6,5,4,3,2,1,0:T(8,128)(2,1)}, bf16[2,2,2,2,4,128,128]{6,5,4,3,2,1,0:T(8,128)(2,1)}) custom-call(s32[1]{0:T(128)} %bitcast.5.mine_ref, bf16[2,192,512]{2,1,0:T(8,128)(2,1)} %get-tuple-element.130.own_pre, bf16[2,192,512]{2,1,0:T(8,128)(2,1)} %copy-done.14, ...), custom_call_target="tpu_custom_call" | custom-call | tf_op jit(solution)/shard_map/down_grad/pallas_call | solution.py:649
  316.8 6.6 %collective-permute-done.16.refs_11_.refs_13_.refs_5_.refs_2_.refs_9_ = bf16[5632,128]{1,0:T(8,128)(2,1)} collective-permute-done((bf16[5632,128]{1,0:T(8,128)(2,1)}, bf16[5632,128]{1,0:T(8,128)(2,1)}, u32[]{:S(2)}, u32[]{:S(2)}) %collective-permute-start.16) | collective-permute-done | bytes 1441824 | tf_op jit(solution)/shard_map/ppermute | solution.py:857
  327.2 9.1 %send.12 = (bf16[10496,128]{1,0:T(8,128)(2,1)}, bf16[8704,128]{1,0:T(8,128)(2,1)}, bf16[10240,128]{1,0:T(8,128)(2,1)}) custom-call(s32[4]{0:T(128)} %pad_add_fusion.bits_ref, bf16[20480,128]{1,0:T(8,128)(2,1)} %bitcast.140, bf16[10240,128]{1,0:T(8,128)(2,1)} %copy-done.3, bf16[5120,128]{1,0:T(8,128)(2,1)} %copy-done.5, ...), custom_call_target="tpu_custom_call" | custom-call | tf_op jit(solution)/shard_map/send/pallas_call | solution.py:957
  340.2 16.6 %back.1 = (f32[3072,32]{1,0:T(8,128)}, f32[96,512]{1,0:T(8,128)}) custom-call(f32[3072,512]{1,0:T(8,128)} %get-tuple-element.102.sres_ref, bf16[12,256,512]{2,1,0:T(8,128)(2,1)} %get-tuple-element.110.block_a_ref, bf16[16,192,512]{2,1,0:T(8,128)(2,1)} %get-tuple-element.129.block_b_ref, bf16[3072,32]{1,0:T(8,128)(2,1)} %copy.119.cot_ref, ...), custom_call_target="tpu_custom_call" | custom-call | tf_op jit(solution)/shard_map/back/pallas_call | solution.py:770
  361.5 33.8 %collective-permute-done.18 = f32[76,128]{1,0:T(8,128)S(1)} collective-permute-done((f32[76,128]{1,0:T(8,128)S(1)}, f32[76,128]{1,0:T(8,128)S(1)}, u32[]{:S(2)}, u32[]{:S(2)}) %collective-permute-start.18) | collective-permute-done | bytes 38944 | tf_op jit(solution)/shard_map/ppermute | solution.py:857
  397.0 6.9 %send.13 = (bf16[2432,128]{1,0:T(8,128)(2,1)}, bf16[5120,128]{1,0:T(8,128)(2,1)}, bf16[5120,128]{1,0:T(8,128)(2,1)}, bf16[2048,128]{1,0:T(8,128)(2,1)}) custom-call(s32[4]{0:T(128)} %pad_add_fusion.bits_ref, bf16[20480,128]{1,0:T(8,128)(2,1)} %bitcast.141, bf16[10240,128]{1,0:T(8,128)(2,1)} %copy-done.3, bf16[5120,128]{1,0:T(8,128)(2,1)} %copy-done.5, ...), custom_call_target="tpu_custom_call" | custom-call | tf_op jit(solution)/shard_map/send/pallas_call | solution.py:957
  409.6 23.5 %collective-permute-done.19 = f32[76,128]{1,0:T(8,128)S(1)} collective-permute-done((f32[76,128]{1,0:T(8,128)S(1)}, f32[76,128]{1,0:T(8,128)S(1)}, u32[]{:S(2)}, u32[]{:S(2)}) %collective-permute-start.19) | collective-permute-done | bytes 38944 | tf_op jit(solution)/shard_map/ppermute | solution.py:857
  433.6 3.9 collective-permute-done.20
  445.7 4.6 send.14
  458.9 3.8 all-to-all-start.1
  462.7 5.6 %collective-permute-done.29.refs_7_ = bf16[1024,128]{1,0:T(8,128)(2,1)S(1)} collective-permute-done((bf16[1024,128]{1,0:T(8,128)(2,1)}, bf16[1024,128]{1,0:T(8,128)(2,1)S(1)}, u32[]{:S(2)}, u32[]{:S(2)}) %collective-permute-start.29) | collective-permute-done | bytes 262176 | tf_op jit(solution)/shard_map/ppermute | solution.py:857
  471.2 3.5 send.15
  481.0 3.9 finish.2
  484.9 18.0 %collective-permute-done.33.refs_4_ = bf16[2560,128]{1,0:T(8,128)(2,1)S(1)} collective-permute-done((bf16[2560,128]{1,0:T(8,128)(2,1)}, bf16[2560,128]{1,0:T(8,128)(2,1)S(1)}, u32[]{:S(2)}, u32[]{:S(2)}) %collective-permute-start.33) | collective-permute-done | bytes 655392 | tf_op jit(solution)/shard_map/ppermute | solution.py:857
  503.8 4.7 finish.3
  (226 shorter events, 84.8 us)
Async XLA Ops:
  0.7 75.0 %all-to-all-start = ((bf16[16,768,8]{1,2,0:T(8,128)(2,1)}), bf16[16,768,8]{1,2,0:T(8,128)(2,1)S(1)}, u32[]{:S(2)}, u32[]{:S(2)}) async-start(bf16[16,768,8]{1,2,0:T(8,128)(2,1)} %param.31), calls=%async_computation | async-start | bytes 393216 | tf_op jit(solution)/shard_map/all_to_all | solution.py:1093
  35.0 159.1 %collective-permute-start = (bf16[12,256,512]{2,1,0:T(8,128)(2,1)}, bf16[12,256,512]{2,1,0:T(8,128)(2,1)}, u32[]{:S(2)}, u32[]{:S(2)}) collective-permute-start(bf16[12,256,512]{2,1,0:T(8,128)(2,1)} %get-tuple-element.95.seasonal_ref.own_seasonal), channel_id=1, source_target_pairs={{0,1},{1,0},{2,3},{3,2},{4,5},{5,4},{6,7},{7,6},{8,9},{9,8},{10,11... | collective-permute-start | bytes 9437192 | tf_op jit(solution)/shard_map/ppermute | solution.py:1038
  35.3 158.7 %collective-permute-start.1 = (bf16[16,192,512]{2,1,0:T(8,128)(2,1)}, bf16[16,192,512]{2,1,0:T(8,128)(2,1)}, u32[]{:S(2)}, u32[]{:S(2)}) collective-permute-start(bf16[16,192,512]{2,1,0:T(8,128)(2,1)} %get-tuple-element.97.seasonal_ref.own_seasonal), channel_id=1, source_target_pairs={{0,1},{1,0},{2,3},{3,2},{4,5},{5,4},{6,7},{7,6},{8,9},{9,8},{10,11... | collective-permute-start | bytes 9437192 | tf_op jit(solution)/shard_map/ppermute | solution.py:1038
  55.2 137.8 %collective-permute-start.2 = (bf16[2,256,512]{2,1,0:T(8,128)(2,1)}, bf16[2,256,512]{2,1,0:T(8,128)(2,1)S(1)}, u32[]{:S(2)}, u32[]{:S(2)}) collective-permute-start(bf16[2,256,512]{2,1,0:T(8,128)(2,1)} %get-tuple-element.107.own_joined), channel_id=1, source_target_pairs={{0,1},{1,0},{2,3},{3,2},{4,5},{5,4},{6,7},{7,6},{8,9},{9,8},{10,11... | collective-permute-start | bytes 1572872 | tf_op jit(solution)/shard_map/ppermute | solution.py:1038
  74.4 114.9 %collective-permute-start.3 = (bf16[2,192,512]{2,1,0:T(8,128)(2,1)}, bf16[2,192,512]{2,1,0:T(8,128)(2,1)S(1)}, u32[]{:S(2)}, u32[]{:S(2)}) collective-permute-start(bf16[2,192,512]{2,1,0:T(8,128)(2,1)} %get-tuple-element.108.own_joined), channel_id=1, source_target_pairs={{0,1},{1,0},{2,3},{3,2},{4,5},{5,4},{6,7},{7,6},{8,9},{9,8},{10,11... | collective-permute-start | bytes 1179656 | tf_op jit(solution)/shard_map/ppermute | solution.py:1038
  188.9 32.0 %collective-permute-start.5 = (bf16[16,192,512]{2,1,0:T(8,128)(2,1)}, bf16[16,192,512]{2,1,0:T(8,128)(2,1)}, u32[]{:S(2)}, u32[]{:S(2)}) collective-permute-start(bf16[16,192,512]{2,1,0:T(8,128)(2,1)} %get-tuple-element.111.own_pre.pre_ref), channel_id=1, source_target_pairs={{0,1},{1,0},{2,3},{3,2},{4,5},{5,4},{6,7},{7,6},{8,9},{9,8},{10,11... | collective-permute-start | bytes 9437192 | tf_op jit(solution)/shard_map/ppermute | solution.py:1038
  189.3 47.6 %collective-permute-start.6 = (bf16[12,256,512]{2,1,0:T(8,128)(2,1)}, bf16[12,256,512]{2,1,0:T(8,128)(2,1)}, u32[]{:S(2)}, u32[]{:S(2)}) collective-permute-start(bf16[12,256,512]{2,1,0:T(8,128)(2,1)} %get-tuple-element.103.pre_ref.own_pre), channel_id=1, source_target_pairs={{0,1},{1,0},{2,3},{3,2},{4,5},{5,4},{6,7},{7,6},{8,9},{9,8},{10,11... | collective-permute-start | bytes 9437192 | tf_op jit(solution)/shard_map/ppermute | solution.py:1038
  193.0 20.2 %collective-permute-start.4 = (bf16[10240,128]{1,0:T(8,128)(2,1)}, bf16[10240,128]{1,0:T(8,128)(2,1)S(1)}, u32[]{:S(2)}, u32[]{:S(2)}) collective-permute-start(bf16[10240,128]{1,0:T(8,128)(2,1)} %bitcast.12), channel_id=1, source_target_pairs={{0,1},{1,0},{2,3},{3,2},{4,5},{5,4},{6,7},{7,6},{8,9},{9,8},{10,11... | collective-permute-start | bytes 7864328 | tf_op jit(solution)/shard_map/ppermute | solution.py:857
  213.0 34.4 %collective-permute-start.7 = (bf16[2,256,512]{2,1,0:T(8,128)(2,1)}, bf16[2,256,512]{2,1,0:T(8,128)(2,1)}, u32[]{:S(2)}, u32[]{:S(2)}) collective-permute-start(bf16[2,256,512]{2,1,0:T(8,128)(2,1)} %get-tuple-element.114.own_pre), channel_id=1, source_target_pairs={{0,1},{1,0},{2,3},{3,2},{4,5},{5,4},{6,7},{7,6},{8,9},{9,8},{10,11... | collective-permute-start | bytes 1572872 | tf_op jit(solution)/shard_map/ppermute | solution.py:1038
  218.7 61.8 %collective-permute-start.8 = (bf16[5120,128]{1,0:T(8,128)(2,1)}, bf16[5120,128]{1,0:T(8,128)(2,1)S(1)}, u32[]{:S(2)}, u32[]{:S(2)}) collective-permute-start(bf16[5120,128]{1,0:T(8,128)(2,1)} %send.8), channel_id=1, source_target_pairs={{0,8},{1,9},{2,10},{3,11},{4,12},{5,13},{6,14},{7,15},{8,0},{9,1},... | collective-permute-start | bytes 3932168 | tf_op jit(solution)/shard_map/ppermute | solution.py:857
  233.4 47.2 %collective-permute-start.9 = (bf16[4096,128]{1,0:T(8,128)(2,1)}, bf16[4096,128]{1,0:T(8,128)(2,1)S(1)}, u32[]{:S(2)}, u32[]{:S(2)}) collective-permute-start(bf16[4096,128]{1,0:T(8,128)(2,1)} %get-tuple-element.120), channel_id=1, source_target_pairs={{0,2},{1,3},{2,0},{3,1},{4,6},{5,7},{6,4},{7,5},{8,10},{9,11},{10,... | collective-permute-start | bytes 3145736 | tf_op jit(solution)/shard_map/ppermute | solution.py:857
  235.4 45.2 %collective-permute-start.10 = (bf16[4096,128]{1,0:T(8,128)(2,1)}, bf16[4096,128]{1,0:T(8,128)(2,1)}, u32[]{:S(2)}, u32[]{:S(2)}) collective-permute-start(bf16[4096,128]{1,0:T(8,128)(2,1)} %get-tuple-element.121), channel_id=1, source_target_pairs={{0,4},{1,5},{2,6},{3,7},{4,0},{5,1},{6,2},{7,3},{8,12},{9,13},{10,... | collective-permute-start | bytes 3145736 | tf_op jit(solution)/shard_map/ppermute | solution.py:857
  247.2 33.4 %collective-permute-start.11 = (bf16[3072,128]{1,0:T(8,128)(2,1)}, bf16[3072,128]{1,0:T(8,128)(2,1)S(1)}, u32[]{:S(2)}, u32[]{:S(2)}) collective-permute-start(bf16[3072,128]{1,0:T(8,128)(2,1)} %get-tuple-element.126), channel_id=1, source_target_pairs={{0,2},{1,3},{2,0},{3,1},{4,6},{5,7},{6,4},{7,5},{8,10},{9,11},{10,... | collective-permute-start | bytes 2359304 | tf_op jit(solution)/shard_map/ppermute | solution.py:857
  247.3 33.2 %collective-permute-start.12 = (bf16[3072,128]{1,0:T(8,128)(2,1)}, bf16[3072,128]{1,0:T(8,128)(2,1)}, u32[]{:S(2)}, u32[]{:S(2)}) collective-permute-start(bf16[3072,128]{1,0:T(8,128)(2,1)} %get-tuple-element.127), channel_id=1, source_target_pairs={{0,4},{1,5},{2,6},{3,7},{4,0},{5,1},{6,2},{7,3},{8,12},{9,13},{10,... | collective-permute-start | bytes 2359304 | tf_op jit(solution)/shard_map/ppermute | solution.py:857
  288.9 35.9 %collective-permute-start.14 = (bf16[6144,128]{1,0:T(8,128)(2,1)}, bf16[6144,128]{1,0:T(8,128)(2,1)}, u32[]{:S(2)}, u32[]{:S(2)}) collective-permute-start(bf16[6144,128]{1,0:T(8,128)(2,1)} %get-tuple-element.135), channel_id=1, source_target_pairs={{0,2},{1,3},{2,0},{3,1},{4,6},{5,7},{6,4},{7,5},{8,10},{9,11},{10,... | collective-permute-start | bytes 4718600 | tf_op jit(solution)/shard_map/ppermute | solution.py:857
  290.9 35.2 %collective-permute-start.15 = (bf16[6144,128]{1,0:T(8,128)(2,1)}, bf16[6144,128]{1,0:T(8,128)(2,1)S(1)}, u32[]{:S(2)}, u32[]{:S(2)}) collective-permute-start(bf16[6144,128]{1,0:T(8,128)(2,1)} %get-tuple-element.136), channel_id=1, source_target_pairs={{0,8},{1,9},{2,10},{3,11},{4,12},{5,13},{6,14},{7,15},{8,0},{9,1},... | collective-permute-start | bytes 4718600 | tf_op jit(solution)/shard_map/ppermute | solution.py:857
  290.9 32.5 %collective-permute-start.16 = (bf16[5632,128]{1,0:T(8,128)(2,1)}, bf16[5632,128]{1,0:T(8,128)(2,1)}, u32[]{:S(2)}, u32[]{:S(2)}) collective-permute-start(bf16[5632,128]{1,0:T(8,128)(2,1)} %get-tuple-element.137), channel_id=1, source_target_pairs={{0,4},{1,5},{2,6},{3,7},{4,0},{5,1},{6,2},{7,3},{8,12},{9,13},{10,... | collective-permute-start | bytes 4325384 | tf_op jit(solution)/shard_map/ppermute | solution.py:857
  336.3 59.1 %collective-permute-start.22 = (bf16[10496,128]{1,0:T(8,128)(2,1)}, bf16[10496,128]{1,0:T(8,128)(2,1)S(1)}, u32[]{:S(2)}, u32[]{:S(2)}) collective-permute-start(bf16[10496,128]{1,0:T(8,128)(2,1)} %get-tuple-element.144), channel_id=1, source_target_pairs={{0,4},{1,5},{2,6},{3,7},{4,0},{5,1},{6,2},{7,3},{8,12},{9,13},{10,... | collective-permute-start | bytes 8060936 | tf_op jit(solution)/shard_map/ppermute | solution.py:857
  337.9 57.5 %collective-permute-start.24 = (bf16[10240,128]{1,0:T(8,128)(2,1)}, bf16[10240,128]{1,0:T(8,128)(2,1)}, u32[]{:S(2)}, u32[]{:S(2)}) collective-permute-start(bf16[10240,128]{1,0:T(8,128)(2,1)} %get-tuple-element.146), channel_id=1, source_target_pairs={{0,2},{1,3},{2,0},{3,1},{4,6},{5,7},{6,4},{7,5},{8,10},{9,11},{10,... | collective-permute-start | bytes 7864328 | tf_op jit(solution)/shard_map/ppermute | solution.py:857
  338.3 57.1 %collective-permute-start.23 = (bf16[8704,128]{1,0:T(8,128)(2,1)}, bf16[8704,128]{1,0:T(8,128)(2,1)}, u32[]{:S(2)}, u32[]{:S(2)}) collective-permute-start(bf16[8704,128]{1,0:T(8,128)(2,1)} %get-tuple-element.145), channel_id=1, source_target_pairs={{0,8},{1,9},{2,10},{3,11},{4,12},{5,13},{6,14},{7,15},{8,0},{9,1},... | collective-permute-start | bytes 6684680 | tf_op jit(solution)/shard_map/ppermute | solution.py:857
  359.9 35.5 %collective-permute-start.18 = (f32[76,128]{1,0:T(8,128)S(1)}, f32[76,128]{1,0:T(8,128)S(1)}, u32[]{:S(2)}, u32[]{:S(2)}) collective-permute-start(f32[76,128]{1,0:T(8,128)S(1)} %add.424), channel_id=1, source_target_pairs={{0,2},{1,3},{2,0},{3,1},{4,6},{5,7},{6,4},{7,5},{8,10},{9,11},{10,... | collective-permute-start | bytes 116744 | tf_op jit(solution)/shard_map/ppermute | solution.py:857
  403.9 38.7 %collective-permute-start.26 = (bf16[5120,128]{1,0:T(8,128)(2,1)}, bf16[5120,128]{1,0:T(8,128)(2,1)S(1)}, u32[]{:S(2)}, u32[]{:S(2)}) collective-permute-start(bf16[5120,128]{1,0:T(8,128)(2,1)} %get-tuple-element.156), channel_id=1, source_target_pairs={{0,2},{1,3},{2,0},{3,1},{4,6},{5,7},{6,4},{7,5},{8,10},{9,11},{10,... | collective-permute-start | bytes 3932168 | tf_op jit(solution)/shard_map/ppermute | solution.py:857
  404.5 38.9 %collective-permute-start.27 = (bf16[5120,128]{1,0:T(8,128)(2,1)}, bf16[5120,128]{1,0:T(8,128)(2,1)S(1)}, u32[]{:S(2)}, u32[]{:S(2)}) collective-permute-start(bf16[5120,128]{1,0:T(8,128)(2,1)} %get-tuple-element.157), channel_id=1, source_target_pairs={{0,4},{1,5},{2,6},{3,7},{4,0},{5,1},{6,2},{7,3},{8,12},{9,13},{10,... | collective-permute-start | bytes 3932168 | tf_op jit(solution)/shard_map/ppermute | solution.py:857
  405.3 37.2 %collective-permute-start.25 = (bf16[2432,128]{1,0:T(8,128)(2,1)}, bf16[2432,128]{1,0:T(8,128)(2,1)S(1)}, u32[]{:S(2)}, u32[]{:S(2)}) collective-permute-start(bf16[2432,128]{1,0:T(8,128)(2,1)} %get-tuple-element.155), channel_id=1, source_target_pairs={{0,16},{1,17},{2,18},{3,19},{4,20},{5,21},{6,22},{7,23},{8,24},{9,... | collective-permute-start | bytes 1867784 | tf_op jit(solution)/shard_map/ppermute | solution.py:857
  407.9 34.6 %collective-permute-start.28 = (bf16[2048,128]{1,0:T(8,128)(2,1)}, bf16[2048,128]{1,0:T(8,128)(2,1)S(1)}, u32[]{:S(2)}, u32[]{:S(2)}) collective-permute-start(bf16[2048,128]{1,0:T(8,128)(2,1)} %get-tuple-element.158), channel_id=1, source_target_pairs={{0,8},{1,9},{2,10},{3,11},{4,12},{5,13},{6,14},{7,15},{8,0},{9,1},... | collective-permute-start | bytes 1572872 | tf_op jit(solution)/shard_map/ppermute | solution.py:857
  408.4 24.8 %collective-permute-start.19 = (f32[76,128]{1,0:T(8,128)S(1)}, f32[76,128]{1,0:T(8,128)S(1)}, u32[]{:S(2)}, u32[]{:S(2)}) collective-permute-start(f32[76,128]{1,0:T(8,128)S(1)} %add.425), channel_id=1, source_target_pairs={{0,4},{1,5},{2,6},{3,7},{4,0},{5,1},{6,2},{7,3},{8,12},{9,13},{10,... | collective-permute-start | bytes 116744 | tf_op jit(solution)/shard_map/ppermute | solution.py:857
  450.3 20.1 %collective-permute-start.30 = (bf16[3072,128]{1,0:T(8,128)(2,1)}, bf16[3072,128]{1,0:T(8,128)(2,1)S(1)}, u32[]{:S(2)}, u32[]{:S(2)}) collective-permute-start(bf16[3072,128]{1,0:T(8,128)(2,1)} %get-tuple-element.161), channel_id=1, source_target_pairs={{0,8},{1,9},{2,10},{3,11},{4,12},{5,13},{6,14},{7,15},{8,0},{9,1},... | collective-permute-start | bytes 2359304 | tf_op jit(solution)/shard_map/ppermute | solution.py:857
  452.9 15.3 %collective-permute-start.29 = (bf16[1024,128]{1,0:T(8,128)(2,1)}, bf16[1024,128]{1,0:T(8,128)(2,1)S(1)}, u32[]{:S(2)}, u32[]{:S(2)}) collective-permute-start(bf16[1024,128]{1,0:T(8,128)(2,1)} %get-tuple-element.160), channel_id=1, source_target_pairs={{0,16},{1,17},{2,18},{3,19},{4,20},{5,21},{6,22},{7,23},{8,24},{9,... | collective-permute-start | bytes 786440 | tf_op jit(solution)/shard_map/ppermute | solution.py:857
  455.6 12.6 %collective-permute-start.31 = (bf16[1024,128]{1,0:T(8,128)(2,1)}, bf16[1024,128]{1,0:T(8,128)(2,1)S(1)}, u32[]{:S(2)}, u32[]{:S(2)}) collective-permute-start(bf16[1024,128]{1,0:T(8,128)(2,1)} %get-tuple-element.162), channel_id=1, source_target_pairs={{0,2},{1,3},{2,0},{3,1},{4,6},{5,7},{6,4},{7,5},{8,10},{9,11},{10,... | collective-permute-start | bytes 786440 | tf_op jit(solution)/shard_map/ppermute | solution.py:857
  456.9 11.4 %collective-permute-start.32 = (bf16[1024,128]{1,0:T(8,128)(2,1)S(1)}, bf16[1024,128]{1,0:T(8,128)(2,1)S(1)}, u32[]{:S(2)}, u32[]{:S(2)}) collective-permute-start(bf16[1024,128]{1,0:T(8,128)(2,1)S(1)} %copy-done.28), channel_id=1, source_target_pairs={{0,4},{1,5},{2,6},{3,7},{4,0},{5,1},{6,2},{7,3},{8,12},{9,13},{10,... | collective-permute-start | bytes 786440 | tf_op jit(solution)/shard_map/ppermute | solution.py:857
  458.9 20.2 %all-to-all-start.1 = ((f32[2,4,768,32]{2,1,0,3:T(4,128)}), f32[2,4,768,32]{2,1,0,3:T(4,128)S(1)}, u32[]{:S(2)}, u32[]{:S(2)}) async-start(f32[2,4,768,32]{2,1,0,3:T(4,128)} %pad_maximum_fusion), calls=%async_computation.1 | async-start | bytes 1572864 | tf_op jit(solution)/shard_map/all_to_all | solution.py:1210
  474.8 28.1 %collective-permute-start.33 = (bf16[2560,128]{1,0:T(8,128)(2,1)}, bf16[2560,128]{1,0:T(8,128)(2,1)S(1)}, u32[]{:S(2)}, u32[]{:S(2)}) collective-permute-start(bf16[2560,128]{1,0:T(8,128)(2,1)} %send.15), channel_id=1, source_target_pairs={{0,16},{1,17},{2,18},{3,19},{4,20},{5,21},{6,22},{7,23},{8,24},{9,... | collective-permute-start | bytes 1966088 | tf_op jit(solution)/shard_map/ppermute | solution.py:857
  (33 other events, 178.2 us)
